TPU v7x, 32 devices: a whole 2x2x4 slice. The times are simulated.
32 devices in a mesh: seq: 16 (over z, x, core), head: 2 (over y).
Axes of the slice: x: 2, y: 2, z: 4, core: 2. Of those that a mesh axis runs over, the one named last changes fastest.
Arguments:
- queries: bfloat16 [4096, 4096], P(('seq', 'head')), may hold values from -130 to 130
- keys: bfloat16 [4096, 1024], P(('seq', 'head')), may hold values from -5 to 5
- values: bfloat16 [4096, 1024], P(('seq', 'head')), may hold values from -6 to 6
- vertical: int32 [8, 128], P('head'), may hold values from 0 to 4095, as said below
- slash: int32 [8, 64, 40], P('head'), may hold values from -1 to 59, as said below
Outputs:
- attended: bfloat16 [4096, 4096], P(('seq', 'head'))
Inputs may be any that keep to these rules, and one draw needn't show every extreme that they name: `vertical`: for each KV head the 128 entries are distinct token positions; the 256 tokens of one seq shard hold at most 15 of them, and for every head some seq shard holds exactly that many. Each KV head h has 40 distinct block offsets d[h, n], each at least 4, and some offset of every head equals 4; slash[h, b, n] = b - d[h, n] where that is not negative, else -1.
All inputs are finite; a program needn't handle non-finite values.
Results may differ from a plain program's by a relative error of at most 0.0052.
Values may be sent and summed in bfloat16 or wider, within the bound.
No kernel may reach another device: no remote copies, remote signals or barrier semaphores. Data moves between devices by JAX's collectives and lax.ppermute only.
A program may use at most 128 MiB of HBM per device.

v0:
```python
import math

import jax
import jax.numpy as jnp
from jax import lax
from jax.sharding import PartitionSpec as P

BLK = 64
NS = 40


def live_entries(lists):
    count = lists.shape[-1]
    earlier = jnp.arange(count)[:, None] > jnp.arange(count)[None, :]
    repeated = jnp.any(earlier & (lists[..., :, None] == lists[..., None, :]), axis=-1)
    return (lists >= 0) & jnp.logical_not(repeated)


def block_attention(
    query_part,
    diag_part,
    slash_part,
    slash_live,
    slash_list,
    vert_part,
    vert_where,
    block_ids,
    head_dim,
):
    scaling = 1.0 / math.sqrt(head_dim)
    width = query_part.shape[1]
    steps = query_part.shape[0]
    rows = query_part.shape[2]
    listed = slash_part.shape[1]
    positions = block_ids[:, None] * width + jnp.arange(width, dtype=jnp.int32)[None, :]
    first = (
        jnp.einsum(
            "gqrd,gkd->gqrk",
            query_part,
            diag_part[..., :head_dim],
            preferred_element_type=jnp.float32,
        )
        * scaling
    )
    causal = jnp.arange(width)[None, :] <= jnp.arange(width)[:, None]
    first = jnp.where(causal[None, :, None, :], first, -jnp.inf)
    second = (
        jnp.einsum(
            "gqrd,gnkd->gqrnk",
            query_part,
            slash_part[..., :head_dim],
            preferred_element_type=jnp.float32,
        )
        * scaling
    )
    second = jnp.where(slash_live[:, None, None, :, None], second, -jnp.inf)
    second = second.reshape(steps, width, rows, listed * width)
    third = (
        jnp.einsum(
            "gqrd,vd->gqrv", query_part, vert_part[:, :head_dim], preferred_element_type=jnp.float32
        )
        * scaling
    )
    vert_block = vert_where // width
    covered = (vert_block[None, :] == block_ids[:, None]) | jnp.any(
        slash_live[:, :, None] & (slash_list[:, :, None] == vert_block[None, None, :]), axis=1
    )
    visible = (vert_where[None, None, :] <= positions[:, :, None]) & jnp.logical_not(covered)[
        :, None, :
    ]
    third = jnp.where(visible[:, :, None, :], third, -jnp.inf)
    scores = jnp.concatenate([first, second, third], axis=-1)
    top = jnp.max(scores, axis=-1, keepdims=True)
    expo = jnp.exp(scores - top)
    total = jnp.sum(expo, axis=-1, keepdims=True)
    weights = (expo / total).astype(jnp.bfloat16)
    w_diag = weights[..., :width]
    w_slash = weights[..., width : width + listed * width].reshape(
        steps, width, rows, listed, width
    )
    w_vert = weights[..., width + listed * width :]
    out_diag = jnp.einsum(
        "gqrk,gkd->gqrd", w_diag, diag_part[..., head_dim:], preferred_element_type=jnp.float32
    )
    out_slash = jnp.einsum(
        "gqrnk,gnkd->gqrd", w_slash, slash_part[..., head_dim:], preferred_element_type=jnp.float32
    )
    out_vert = jnp.einsum(
        "gqrv,vd->gqrd", w_vert, vert_part[:, head_dim:], preferred_element_type=jnp.float32
    )
    return (out_diag + out_slash + out_vert).astype(jnp.bfloat16)


def make_step(own_rows, head_index, vert_head, vert_where, head_dim):

    def per_step(items):
        query_part, diag_part, slash_list, slash_live, sources, ident = items
        slash_part = own_rows[sources, :, head_index]
        return block_attention(
            query_part,
            diag_part,
            slash_part,
            slash_live,
            slash_list,
            vert_head,
            vert_where,
            ident,
            head_dim,
        )

    return per_step


def body(queries, keys, values, vertical, slash):
    query_rows, key_rows, value_rows = (
        lax.all_to_all(queries, "head", split_axis=1, concat_axis=0, tiled=True),
        lax.all_to_all(keys, "head", split_axis=1, concat_axis=0, tiled=True),
        lax.all_to_all(values, "head", split_axis=1, concat_axis=0, tiled=True),
    )
    shards = lax.axis_size("seq")
    seq_rank = lax.axis_index("seq")
    tok_count = key_rows.shape[0]
    local_heads = vertical.shape[0]
    head_dim = key_rows.shape[1] // local_heads
    group = query_rows.shape[1] // key_rows.shape[1]
    blocks_here = tok_count // BLK
    first_block = seq_rank * blocks_here
    paired = jnp.concatenate(
        [
            key_rows.reshape(tok_count, local_heads, head_dim),
            value_rows.reshape(tok_count, local_heads, head_dim),
        ],
        axis=2,
    )
    by_dest = slash.reshape(local_heads, shards, blocks_here * NS)
    own_ids = first_block + jnp.arange(blocks_here, dtype=jnp.int32)
    needed = jnp.any(by_dest[:, :, :, None] == own_ids[None, None, None, :], axis=2)
    needed = jnp.transpose(needed, (1, 2, 0))
    own_blocks = paired.reshape(blocks_here, BLK, local_heads, 2 * head_dim)
    outgoing = jnp.where(needed[:, :, None, :, None], own_blocks[None], jnp.zeros((), jnp.bfloat16))
    outgoing = outgoing.reshape(shards, tok_count, local_heads, 2 * head_dim)
    vert_shard = vertical // tok_count
    owned = vert_shard == seq_rank
    local_where = vertical - seq_rank * tok_count
    incoming = lax.all_to_all(outgoing, "seq", split_axis=0, concat_axis=0, tiled=True)
    token_iota = jnp.arange(tok_count)
    select = ((local_where[:, :, None] == token_iota[None, None, :]) & owned[:, :, None]).astype(
        jnp.bfloat16
    )
    partial_rows = jnp.einsum("hvt,thx->hvx", select, paired, preferred_element_type=jnp.float32)
    vert_part = lax.psum(partial_rows, "seq").astype(jnp.bfloat16)
    mine = lax.dynamic_slice_in_dim(slash, first_block, blocks_here, axis=1)
    live = live_entries(mine)
    source_block = jnp.where(live, mine, 0)
    step_blocks = math.gcd(blocks_here, 2)
    steps_count = blocks_here // step_blocks
    block_ids = (first_block + jnp.arange(blocks_here, dtype=jnp.int32)).reshape(
        steps_count, step_blocks
    )
    query_all = query_rows.reshape(steps_count, step_blocks, BLK, local_heads, group, head_dim)
    all_blocks = incoming.reshape(shards * blocks_here, BLK, local_heads, 2 * head_dim)
    results = []
    for head_index in range(local_heads):
        per_step = make_step(
            all_blocks, head_index, vert_part[head_index], vertical[head_index], head_dim
        )
        diag_all = paired[:, head_index].reshape(steps_count, step_blocks, BLK, 2 * head_dim)
        lists = mine[head_index].reshape(steps_count, step_blocks, NS)
        lives = live[head_index].reshape(steps_count, step_blocks, NS)
        sources = source_block[head_index].reshape(steps_count, step_blocks, NS)
        outputs = lax.map(
            per_step, (query_all[:, :, :, head_index], diag_all, lists, lives, sources, block_ids)
        )
        results.append(outputs)
    stacked = jnp.stack(results, axis=3).reshape(tok_count, local_heads * group * head_dim)
    return lax.all_to_all(stacked, "head", split_axis=0, concat_axis=1, tiled=True)


def solution(mesh):
    in_specs = (
        P(("seq", "head"), None),
        P(("seq", "head"), None),
        P(("seq", "head"), None),
        P("head", None),
        P("head", None, None),
    )
    out_specs = P(("seq", "head"), None)
    return jax.shard_map(body, mesh=mesh, in_specs=in_specs, out_specs=out_specs, check_vma=False)
```

profile of v0, /device:TPU:0, one launch (start us, length us, event | category | flops | bytes accessed | tf_op | source)
XLA Modules:
  0.0 732.4 jit_solution(8951616375855945567)
XLA Ops:
  15.4 5.8 all-to-all-done.2
  24.9 5.8 broadcast_select_fusion
  30.6 7.4 %all-to-all-done = bf16[128,2,2048]{2,0,1:T(8,128)(2,1)S(1)} async-done(((bf16[128,2,2048]{2,0,1:T(8,128)(2,1)}), bf16[128,2,2048]{2,0,1:T(8,128)(2,1)S(1)}, u32[]{:S(2)}, u32[]{:S(2)}) %all-to-all-start) | async-done | bytes 1048608 | tf_op jit(solution)/shard_map/all_to_all | solution.py:116
  38.0 5.9 all-to-all-start.3
  49.6 219.6 %all-reduce.5 = bf16[4,128,256]{2,1,0:T(8,128)(2,1)S(1)} all-reduce(f32[4,128,256]{2,1,0:T(8,128)S(1)} %fusion.118), channel_id=1, replica_groups=mesh['seq'=16,'head'=2] {'seq'}, use_global_device_ids=true, to_apply=%region_2.3 | all-reduce | flops 131072 | bytes 786432 | tf_op jit(solution)/shard_map/psum | solution.py:151
  272.7 7.7 %copy.163 = bf16[16,256,4,256]{3,1,0,2:T(8,128)(2,1)} copy(bf16[16,256,4,256]{3,1,2,0:T(8,128)(2,1)} %all-to-all-done.3) | data formatting | bytes 16777216 | tf_op jit(solution)/shard_map/all_to_all | solution.py:145
  280.4 8.3 %copy.165 = bf16[64,64,4,256]{3,1,2,0:T(8,128)(2,1)} copy(bf16[64,64,4,256]{3,1,0,2:T(8,128)(2,1)} %bitcast.710) | data formatting | bytes 16777216 | tf_op jit(solution)/shard_map/while | solution.py:171
  289.5 107.5 %while.52 = (s32[]{:T(128)}, bf16[2,2,64,4,128]{4,2,3,1,0:T(8,128)(2,1)}, bf16[2,2,64,4,128]{4,3,2,1,0:T(4,128)(2,1)}, bf16[2,2,64,256]{3,2,1,0:T(8,128)(2,1)}, ...) while((s32[]{:T(128)}, ...), condition=%wide.region_9.10_spmd, body=%wide.region_3.9_spmd.sunk | while | flops 732959872 | bytes 101075352 | solution.py:171
  294.6 4.3 gather_fusion
  299.0 4.9 fusion.201
  303.9 9.2 %copy.334 = f32[2,64,4,2560]{3,1,2,0:T(8,128)} copy(f32[2,64,4,2560]{1,3,2,0:T(8,128)} %bitcast.698) | data formatting | bytes 10485760 | tf_op jit(solution)/shard_map/while/body/eval_jaxpr/reshape | solution.py:57
  313.4 7.2 concatenate.63
  329.7 7.6 %reshape.1116 = bf16[2,64,4,40,64]{4,3,1,2,0:T(8,128)(2,1)} reshape(bf16[2,64,4,2560]{3,1,2,0:T(8,128)(2,1)} %slice.620) | data formatting | bytes 5242880 | tf_op jit(solution)/shard_map/while/body/eval_jaxpr/reshape | solution.py:78
  348.3 4.3 gather_fusion
  352.7 4.9 fusion.201
  357.6 9.2 %copy.334 = f32[2,64,4,2560]{3,1,2,0:T(8,128)} copy(f32[2,64,4,2560]{1,3,2,0:T(8,128)} %bitcast.698) | data formatting | bytes 10485760 | tf_op jit(solution)/shard_map/while/body/eval_jaxpr/reshape | solution.py:57
  367.1 7.2 concatenate.63
  383.4 7.6 %reshape.1116 = bf16[2,64,4,40,64]{4,3,1,2,0:T(8,128)(2,1)} reshape(bf16[2,64,4,2560]{3,1,2,0:T(8,128)(2,1)} %slice.620) | data formatting | bytes 5242880 | tf_op jit(solution)/shard_map/while/body/eval_jaxpr/reshape | solution.py:78
  397.7 102.7 %while.53 = (s32[]{:T(128)}, bf16[2,2,64,4,128]{4,2,3,1,0:T(8,128)(2,1)}, bf16[2,2,64,4,128]{4,3,2,1,0:T(4,128)(2,1)S(1)}, bf16[2,2,64,256]{3,2,1,0:T(8,128)(2,1...) while((s32[]{:T(128)}, ...), condition=%wide.region_16.17_spmd, body=%wide.region_10.16_spmd.sunk | while | flops 732960000 | bytes 100545856 | solution.py:171
  401.4 4.3 gather_fusion.1
  405.7 4.9 fusion.213
  410.6 9.1 %copy.339 = f32[2,64,4,2560]{3,1,2,0:T(8,128)} copy(f32[2,64,4,2560]{1,3,2,0:T(8,128)} %bitcast.699) | data formatting | bytes 10485760 | tf_op jit(solution)/shard_map/while/body/eval_jaxpr/reshape | solution.py:57
  420.1 7.2 concatenate.65
  436.4 7.6 %reshape.1120 = bf16[2,64,4,40,64]{4,3,1,2,0:T(8,128)(2,1)} reshape(bf16[2,64,4,2560]{3,1,2,0:T(8,128)(2,1)} %slice.629) | data formatting | bytes 5242880 | tf_op jit(solution)/shard_map/while/body/eval_jaxpr/reshape | solution.py:78
  452.6 4.3 gather_fusion.1
  457.0 4.9 fusion.213
  461.9 9.1 %copy.339 = f32[2,64,4,2560]{3,1,2,0:T(8,128)} copy(f32[2,64,4,2560]{1,3,2,0:T(8,128)} %bitcast.699) | data formatting | bytes 10485760 | tf_op jit(solution)/shard_map/while/body/eval_jaxpr/reshape | solution.py:57
  471.4 7.2 concatenate.65
  487.7 7.6 %reshape.1120 = bf16[2,64,4,40,64]{4,3,1,2,0:T(8,128)(2,1)} reshape(bf16[2,64,4,2560]{3,1,2,0:T(8,128)(2,1)} %slice.629) | data formatting | bytes 5242880 | tf_op jit(solution)/shard_map/while/body/eval_jaxpr/reshape | solution.py:78
  501.2 107.5 %while.54 = (s32[]{:T(128)}, bf16[2,2,64,4,128]{4,2,3,1,0:T(8,128)(2,1)}, bf16[2,2,64,4,128]{4,3,2,1,0:T(4,128)(2,1)}, bf16[2,2,64,256]{3,2,1,0:T(8,128)(2,1)}, ...) while((s32[]{:T(128)}, ...), condition=%wide.region_23.24_spmd, body=%wide.region_17.23_spmd.sunk | while | flops 732960000 | bytes 101332344 | solution.py:171
  511.5 4.9 fusion.225
  516.4 9.2 %copy.344 = f32[2,64,4,2560]{3,1,2,0:T(8,128)} copy(f32[2,64,4,2560]{1,3,2,0:T(8,128)} %bitcast.700) | data formatting | bytes 10485760 | tf_op jit(solution)/shard_map/while/body/eval_jaxpr/reshape | solution.py:57
  526.0 7.2 concatenate.67
  542.3 7.6 %reshape.1124 = bf16[2,64,4,40,64]{4,3,1,2,0:T(8,128)(2,1)} reshape(bf16[2,64,4,2560]{3,1,2,0:T(8,128)(2,1)} %slice.638) | data formatting | bytes 5242880 | tf_op jit(solution)/shard_map/while/body/eval_jaxpr/reshape | solution.py:78
  565.1 4.9 fusion.225
  570.0 9.2 %copy.344 = f32[2,64,4,2560]{3,1,2,0:T(8,128)} copy(f32[2,64,4,2560]{1,3,2,0:T(8,128)} %bitcast.700) | data formatting | bytes 10485760 | tf_op jit(solution)/shard_map/while/body/eval_jaxpr/reshape | solution.py:57
  579.5 7.2 concatenate.67
  595.8 7.6 %reshape.1124 = bf16[2,64,4,40,64]{4,3,1,2,0:T(8,128)(2,1)} reshape(bf16[2,64,4,2560]{3,1,2,0:T(8,128)(2,1)} %slice.638) | data formatting | bytes 5242880 | tf_op jit(solution)/shard_map/while/body/eval_jaxpr/reshape | solution.py:78
  609.4 102.8 %while.55 = (s32[]{:T(128)}, bf16[2,2,64,4,128]{4,2,3,1,0:T(8,128)(2,1)}, bf16[2,2,64,4,128]{4,3,2,1,0:T(4,128)(2,1)S(1)}, bf16[2,2,64,256]{3,2,1,0:T(8,128)(2,1...) while((s32[]{:T(128)}, ...), condition=%wide.region_30.31_spmd, body=%wide.region_24.30_spmd.sunk | while | flops 732960000 | bytes 100545856 | solution.py:171
  617.5 4.9 fusion.237
  622.4 9.2 %copy.349 = f32[2,64,4,2560]{3,1,2,0:T(8,128)} copy(f32[2,64,4,2560]{1,3,2,0:T(8,128)} %bitcast.701) | data formatting | bytes 10485760 | tf_op jit(solution)/shard_map/while/body/eval_jaxpr/reshape | solution.py:57
  631.9 7.2 concatenate.69
  648.1 7.6 %reshape.1128 = bf16[2,64,4,40,64]{4,3,1,2,0:T(8,128)(2,1)} reshape(bf16[2,64,4,2560]{3,1,2,0:T(8,128)(2,1)} %slice.647) | data formatting | bytes 5242880 | tf_op jit(solution)/shard_map/while/body/eval_jaxpr/reshape | solution.py:78
  668.8 4.9 fusion.237
  673.7 9.2 %copy.349 = f32[2,64,4,2560]{3,1,2,0:T(8,128)} copy(f32[2,64,4,2560]{1,3,2,0:T(8,128)} %bitcast.701) | data formatting | bytes 10485760 | tf_op jit(solution)/shard_map/while/body/eval_jaxpr/reshape | solution.py:57
  683.2 7.2 concatenate.69
  699.5 7.6 %reshape.1128 = bf16[2,64,4,40,64]{4,3,1,2,0:T(8,128)(2,1)} reshape(bf16[2,64,4,2560]{3,1,2,0:T(8,128)(2,1)} %slice.647) | data formatting | bytes 5242880 | tf_op jit(solution)/shard_map/while/body/eval_jaxpr/reshape | solution.py:78
  715.2 15.0 %all_to_all.72 = bf16[2,128,2048]{2,1,0:T(8,128)(2,1)S(1)} all-to-all(bf16[2,128,2048]{2,1,0:T(8,128)(2,1)S(1)} %all_to_all.63), channel_id=1, replica_groups=mesh['seq'=16,'head'=2] {'head'}, dimensions={0} | all-to-all | bytes 2097152 | tf_op jit(solution)/shard_map/all_to_all | solution.py:176
  (292 shorter events, 206.9 us)
Async XLA Ops:
  1.7 10.1 %all-to-all-start.1 = ((bf16[128,2,512]{2,0,1:T(8,128)(2,1)}), bf16[128,2,512]{2,0,1:T(8,128)(2,1)S(1)}, u32[]{:S(2)}, u32[]{:S(2)}) async-start(bf16[128,2,512]{2,0,1:T(8,128)(2,1)} %bitcast.489), calls=%async_computation.1 | async-start | bytes 524288 | tf_op jit(solution)/shard_map/all_to_all | solution.py:117
  11.8 9.3 %all-to-all-start.2 = ((bf16[128,2,512]{2,0,1:T(8,128)(2,1)}), bf16[128,2,512]{2,0,1:T(8,128)(2,1)S(1)}, u32[]{:S(2)}, u32[]{:S(2)}) async-start(bf16[128,2,512]{2,0,1:T(8,128)(2,1)} %bitcast.488), calls=%async_computation.2 | async-start | bytes 524288 | tf_op jit(solution)/shard_map/all_to_all | solution.py:118
  21.1 16.9 %all-to-all-start = ((bf16[128,2,2048]{2,0,1:T(8,128)(2,1)}), bf16[128,2,2048]{2,0,1:T(8,128)(2,1)S(1)}, u32[]{:S(2)}, u32[]{:S(2)}) async-start(bf16[128,2,2048]{2,0,1:T(8,128)(2,1)} %bitcast.487), calls=%async_computation | async-start | bytes 2097152 | tf_op jit(solution)/shard_map/all_to_all | solution.py:116
  30.6 16.8 %copy-start.14 = (s32[4,128]{1,0:T(4,128)S(1)}, s32[4,128]{1,0:T(4,128)}, u32[]{:S(2)}) copy-start(s32[4,128]{1,0:T(4,128)} %param.16) | copy-start | bytes 6148
  38.0 234.7 %all-to-all-start.3 = ((bf16[16,256,4,256]{3,1,2,0:T(8,128)(2,1)}), bf16[16,256,4,256]{3,1,2,0:T(8,128)(2,1)}, u32[]{:S(2)}, u32[]{:S(2)}) async-start(bf16[16,256,4,256]{3,1,2,0:T(8,128)(2,1)} %broadcast_select_fusion), calls=%async_computation.3 | async-start | bytes 16777216 | tf_op jit(solution)/shard_map/all_to_all | solution.py:145
  289.5 0.7 copy-start.16
  299.0 4.9 copy-start.4
  303.9 9.2 %copy-start.11 = (bf16[2,2,64,256]{3,2,1,0:T(8,128)(2,1)S(1)}, bf16[2,2,64,256]{3,2,1,0:T(8,128)(2,1)}, u32[]{:S(2)}) copy-start(bf16[2,2,64,256]{3,2,1,0:T(8,128)(2,1)} %get-tuple-element.1995) | copy-start | bytes 393220 | tf_op jit(solution)/shard_map/while
  320.7 4.3 copy-start
  337.3 6.0 copy-start.17
  343.2 0.6 copy-start.16
  352.7 4.9 copy-start.4
  357.6 9.2 %copy-start.11 = (bf16[2,2,64,256]{3,2,1,0:T(8,128)(2,1)S(1)}, bf16[2,2,64,256]{3,2,1,0:T(8,128)(2,1)}, u32[]{:S(2)}) copy-start(bf16[2,2,64,256]{3,2,1,0:T(8,128)(2,1)} %get-tuple-element.1995) | copy-start | bytes 393220 | tf_op jit(solution)/shard_map/while
  374.4 4.3 copy-start
  391.0 6.0 copy-start.17
  405.7 4.9 copy-start.5
  427.3 4.3 copy-start.1
  457.0 4.9 copy-start.5
  478.6 4.3 copy-start.1
  501.2 108.2 %copy-start.8 = (bf16[2,2,64,4,128]{4,3,2,1,0:T(4,128)(2,1)S(1)}, bf16[2,2,64,4,128]{4,3,2,1,0:T(4,128)(2,1)}, u32[]{:S(2)}) copy-start(bf16[2,2,64,4,128]{4,3,2,1,0:T(4,128)(2,1)} %get-tuple-element.1807) | copy-start | bytes 786436
  501.2 108.2 %copy-start.9 = (bf16[256,1,256]{2,0,1:T(8,128)(2,1)S(1)}, bf16[256,1,256]{2,0,1:T(8,128)(2,1)}, u32[]{:S(2)}) copy-start(bf16[256,1,256]{2,0,1:T(8,128)(2,1)} %get-tuple-element.1294) | copy-start | bytes 393220
  501.2 108.2 %copy-start.12 = (bf16[128,256]{1,0:T(8,128)(2,1)S(1)}, bf16[128,256]{1,0:T(8,128)(2,1)}, u32[]{:S(2)}) copy-start(bf16[128,256]{1,0:T(8,128)(2,1)} %get-tuple-element.1820) | copy-start | bytes 196612
  501.2 108.2 %copy-start.15 = (s32[1,4,40]{2,1,0:T(4,128)S(1)}, s32[1,4,40]{2,1,0:T(4,128)}, u32[]{:S(2)}) copy-start(s32[1,4,40]{2,1,0:T(4,128)} %get-tuple-element.1302) | copy-start | bytes 1924
  511.5 4.9 copy-start.6
  516.4 9.2 %copy-start.10 = (bf16[2,2,64,256]{3,2,1,0:T(8,128)(2,1)S(1)}, bf16[2,2,64,256]{3,2,1,0:T(8,128)(2,1)}, u32[]{:S(2)}) copy-start(bf16[2,2,64,256]{3,2,1,0:T(8,128)(2,1)} %get-tuple-element.1893) | copy-start | bytes 393220 | tf_op jit(solution)/shard_map/while
  533.2 4.3 copy-start.2
  549.8 4.3 copy-start.13
  565.1 4.9 copy-start.6
  570.0 9.2 %copy-start.10 = (bf16[2,2,64,256]{3,2,1,0:T(8,128)(2,1)S(1)}, bf16[2,2,64,256]{3,2,1,0:T(8,128)(2,1)}, u32[]{:S(2)}) copy-start(bf16[2,2,64,256]{3,2,1,0:T(8,128)(2,1)} %get-tuple-element.1893) | copy-start | bytes 393220 | tf_op jit(solution)/shard_map/while
  586.8 4.3 copy-start.2
  603.4 4.3 copy-start.13
  617.5 4.9 copy-start.7
  639.1 4.3 copy-start.3
  668.8 4.9 copy-start.7
  690.4 4.3 copy-start.3
where the time goes:
time: 740 us; the launch traced here: 732 us
  local copies, waits for them, and re-layouts  306 us (41%)
  blocking collectives  235 us (32%)
  matrix products  90.4 us (12%)
  other arithmetic  69.6 us (9%)
  starting transfers between devices  17.1 us (2%)
  waiting for transfers between devices  13.1 us (2%)
    psum x1, blocking collectives, body(): vert_part = lax.psum(partial_rows, 'seq').astype(jnp.bfloat16)  220 us
    reshape x8, local copies, waits for them, and re-layouts, block_attention(): second = second.reshape(steps, width, rows, listed * width)  73.5 us
    reshape x8, local copies, waits for them, and re-layouts, block_attention(): weights[..., width:width + listed * width]  60.4 us
    concatenate x8, local copies, waits for them, and re-layouts, block_attention(): scores = jnp.concatenate([first, second, third], axis=-1)  57.8 us
    dot_general x8, matrix products, block_attention(): jnp.einsum('gqrd,gnkd->gqrnk', query_part, slash_part[..., :head_dim], pr...  39.2 us
    gather x8, local copies, waits for them, and re-layouts, per_step(): slash_part = own_rows[sources, :, head_index]  34.6 us
    dot_general x8, matrix products, block_attention(): jnp.einsum('gqrnk,gnkd->gqrd', w_slash, slash_part[..., head_dim:], prefe...  33.1 us
    reduce_sum x8, other arithmetic, block_attention(): total = jnp.sum(expo, axis=-1, keepdims=True)  29.5 us
  transfers between devices with their start and end apart: 4, of which 2 were waited for; matrix products, arithmetic and copies ran while one was open for 3% of the time, Pallas kernels for 0%

commit v1 on v0

v1 whole, which is shorter than its diff:
```python
import functools
import math

import jax
import jax.numpy as jnp
from jax import lax
from jax.experimental import pallas as pl
from jax.experimental.pallas import tpu as pltpu
from jax.sharding import Mesh, PartitionSpec as P

BLK = 64
BIG = 1.0e30
CHUNK = 4


def attention_kernel(
    idx_ref, dead_ref, own_ref, q_ref, vrow_ref, ev_ref, *rest, parts, listed, head_dim, group
):
    kv_parts = rest[:parts]
    out_ref, kv, vt, kvert, vtvert, qext, etile, scores, sems = rest[parts:]
    rows = BLK * group
    part_rows = kv_parts[0].shape[0]
    total = parts * part_rows
    blocks_here = q_ref.shape[0] // BLK
    verts = vrow_ref.shape[0]
    scale = math.log2(math.e) / math.sqrt(head_dim)
    copies = [
        pltpu.make_async_copy(part, kv.at[pl.ds(i * part_rows, part_rows), :], sems.at[i])
        for i, part in enumerate(kv_parts)
    ]
    for copy in copies:
        copy.start()

    token = lax.rem(lax.broadcasted_iota(jnp.int32, (rows, head_dim), 0), BLK)
    column = lax.broadcasted_iota(jnp.int32, (rows, head_dim), 1)
    masked = ((column < BLK) & (column > token)) | (column == BLK)
    qext[...] = jnp.where(masked, -BIG, 0.0).astype(jnp.bfloat16)
    key_iota = lax.broadcasted_iota(jnp.int32, (BLK, head_dim), 0)
    lane = lax.broadcasted_iota(jnp.int32, (BLK, head_dim), 1)
    etile[0] = jnp.zeros((BLK, head_dim), jnp.bfloat16)
    etile[1] = jnp.where(lane == BLK, 1.0, 0.0).astype(jnp.bfloat16)
    etile[2] = jnp.where(lane == key_iota, 1.0, 0.0).astype(jnp.bfloat16)

    for copy in copies:
        copy.wait()

    @pl.loop(0, total // BLK)
    def _(block):
        start = pl.multiple_of(block * BLK, BLK)
        value = kv[pl.ds(start, BLK), pl.ds(head_dim, head_dim)]
        vt[block] = jnp.concatenate([value, value], axis=0).T

    span = math.gcd(total, 512)
    where = vrow_ref[...]
    position = lax.broadcasted_iota(jnp.int32, (verts, span), 1)

    def select(step, found):
        start = pl.multiple_of(step * span, span)
        chosen = jnp.where(where == position + start, 1.0, 0.0).astype(jnp.bfloat16)
        return found + jnp.dot(
            chosen, kv[pl.ds(start, span), :], preferred_element_type=jnp.float32
        )

    found = lax.fori_loop(
        0, total // span, select, jnp.zeros((verts, 2 * head_dim), jnp.float32)
    ).astype(jnp.bfloat16)
    kvert[...] = found[:, :head_dim]
    vtvert[...] = found[:, head_dim:].T

    low = lax.broadcasted_iota(jnp.int32, (head_dim, 2 * BLK), 1) < BLK

    @pl.loop(0, blocks_here)
    def _(here):
        start = pl.multiple_of(here * BLK, BLK)
        query = jnp.concatenate(
            [q_ref[pl.ds(start, BLK), pl.ds(g * head_dim, head_dim)] for g in range(group)], axis=0
        )
        query = jnp.concatenate([query, qext[...]], axis=1)
        own = own_ref[0] + here

        def key_block(block):
            return kv[pl.ds(pl.multiple_of(block * BLK, BLK), BLK), pl.ds(0, head_dim)]

        def keys_of(t):
            if t == 0:
                key = key_block(own)
                left = jnp.concatenate([key, key], axis=0)
                right = jnp.concatenate([etile[2], etile[1]], axis=0)
            elif t <= listed // CHUNK:
                at = here * listed + (t - 1) * CHUNK
                left = jnp.concatenate([key_block(idx_ref[at + i]) for i in range(CHUNK)], axis=0)
                right = jnp.concatenate([etile[dead_ref[at + i]] for i in range(CHUNK)], axis=0)
            else:
                left = kvert[...]
                right = ev_ref[here]
            return jnp.concatenate([left, right], axis=1)

        def values_of(t):
            if t == 0:
                return vt[own]
            if t <= listed // CHUNK:
                at = here * listed + (t - 1) * CHUNK
                return jnp.concatenate(
                    [
                        jnp.where(low, vt[idx_ref[at + i]], vt[idx_ref[at + i + 1]])
                        for i in range(0, CHUNK, 2)
                    ],
                    axis=1,
                )
            return vtvert[...]

        tiles = listed // CHUNK + 2
        sizes = [2 * BLK] + [CHUNK * BLK] * (listed // CHUNK) + [verts]
        starts = [sum(sizes[:t]) for t in range(tiles)]
        top = jnp.full((8, rows), -jnp.inf, jnp.float32)
        for t in range(tiles):
            tile = lax.dot_general(
                keys_of(t), query, (((1,), (1,)), ((), ())), preferred_element_type=jnp.float32
            )
            scores[pl.ds(starts[t], sizes[t]), :] = tile
            top = jnp.maximum(top, jnp.max(tile.reshape(sizes[t] // 8, 8, rows), axis=0))
        top = jnp.max(top, axis=0, keepdims=True)
        weight = jnp.zeros((8, rows), jnp.float32)
        mixed = jnp.zeros((head_dim, rows), jnp.float32)
        for t in range(tiles):
            expo = jnp.exp2((scores[pl.ds(starts[t], sizes[t]), :] - top) * scale)
            weight = weight + jnp.sum(expo.reshape(sizes[t] // 8, 8, rows), axis=0)
            mixed = mixed + jnp.dot(
                values_of(t), expo.astype(jnp.bfloat16), preferred_element_type=jnp.float32
            )
        mixed = mixed / jnp.sum(weight, axis=0, keepdims=True)
        result = mixed.T.astype(jnp.bfloat16)
        for g in range(group):
            out_ref[pl.ds(start, BLK), pl.ds(g * head_dim, head_dim)] = result[
                g * BLK : (g + 1) * BLK
            ]


def attend(idx, dead, own, query, vrow, ev, kv_parts, head_dim, group, listed):
    parts = len(kv_parts)
    total = sum(part.shape[0] for part in kv_parts)
    tokens = query.shape[0]
    verts = vrow.shape[0]
    rows = BLK * group
    keys = (listed + 2) * BLK + verts
    smem = pl.BlockSpec(memory_space=pltpu.SMEM)
    vmem = pl.BlockSpec(memory_space=pltpu.VMEM)
    hbm = pl.BlockSpec(memory_space=pl.ANY)
    work = tokens * group * keys
    return pl.pallas_call(
        functools.partial(
            attention_kernel, parts=parts, listed=listed, head_dim=head_dim, group=group
        ),
        out_shape=jax.ShapeDtypeStruct((tokens, group * head_dim), jnp.bfloat16),
        in_specs=[smem, smem, smem, vmem, vmem, vmem] + [hbm] * parts,
        out_specs=vmem,
        scratch_shapes=[
            pltpu.VMEM((total, 2 * head_dim), jnp.bfloat16),
            pltpu.VMEM((total // BLK, head_dim, 2 * BLK), jnp.bfloat16),
            pltpu.VMEM((verts, head_dim), jnp.bfloat16),
            pltpu.VMEM((head_dim, verts), jnp.bfloat16),
            pltpu.VMEM((rows, head_dim), jnp.bfloat16),
            pltpu.VMEM((3, BLK, head_dim), jnp.bfloat16),
            pltpu.VMEM((keys, rows), jnp.float32),
            pltpu.SemaphoreType.DMA((parts,)),
        ],
        compiler_params=pltpu.CompilerParams(vmem_limit_bytes=48 << 20),
        cost_estimate=pl.CostEstimate(
            flops=4 * work * head_dim,
            transcendentals=work,
            bytes_accessed=total * 2 * head_dim * 2 + tokens * group * head_dim * 4,
        ),
    )(idx, dead, own, query, vrow, ev, *kv_parts)


def body(queries, keys, values, vertical, slash, *, cores, chips, heads):
    tok, q_width = queries.shape
    all_heads = vertical.shape[0] * heads
    head_dim = keys.shape[1] // all_heads
    group = q_width // keys.shape[1]
    ways = cores * heads
    mine = all_heads // ways
    listed = slash.shape[2]
    axes = ("head", "core") if cores > 1 else ("head",)
    groups = chips if cores > 1 else lax.axis_size("chip") * lax.axis_size("core")
    per_group = tok * ways // BLK
    chip = lax.axis_index("chip")
    if cores == 1:
        chip = chip * lax.axis_size("core") + lax.axis_index("core")

    swap = functools.partial(lax.all_to_all, axis_name=axes, tiled=True)
    pair = jnp.concatenate(
        [
            keys.reshape(tok, ways, mine, 1, head_dim),
            values.reshape(tok, ways, mine, 1, head_dim),
        ],
        axis=3,
    ).reshape(tok, ways * mine * 2 * head_dim)
    pair = swap(pair, split_axis=1, concat_axis=0)
    query = swap(queries, split_axis=1, concat_axis=0)

    relative = cores > 1 and chips == 8
    along = tok // BLK if cores > 1 else per_group

    def stored(local):
        if cores == 1:
            return local
        chunk, rest = local // along, local % along
        return ((chunk % heads) * cores + chunk // heads) * along + rest

    def place(block):
        source, local = block // per_group, block % per_group
        if relative:
            source = 2 * (chip // 2 - source // 2) + (chip % 2 + source % 2) % 2
        return source * per_group + stored(local)

    first = lax.axis_index("core") * mine if cores > 1 else 0
    slash = lax.dynamic_slice_in_dim(slash, first, mine, axis=0)
    vertical = lax.dynamic_slice_in_dim(vertical, first, mine, axis=0)
    lists = lax.dynamic_slice_in_dim(slash, chip * per_group, per_group, axis=1)
    ids = chip * per_group + jnp.arange(per_group, dtype=jnp.int32)
    vert_block = vertical // BLK
    covered = jnp.any(lists[:, :, :, None] == vert_block[:, None, None, :], axis=2)
    hidden = covered | (vert_block[:, None, :] >= ids[None, :, None])
    if cores > 1:
        order = lambda x: jnp.swapaxes(
            x.reshape(mine, cores, heads, along, x.shape[2]), 1, 2
        ).reshape(x.shape)
        lists, hidden = order(lists), order(hidden)
    lane = jnp.arange(head_dim, dtype=jnp.int32) == BLK
    ev = (hidden[..., None] & lane).astype(jnp.bfloat16)
    dead = (lists < 0).astype(jnp.int32)
    own = jnp.full((1,), 0 if relative else 1, jnp.int32) * chip * per_group
    idx = jnp.where(lists < 0, own, place(jnp.maximum(lists, 0)))
    vrow = place(vert_block) * BLK + vertical % BLK
    vrow = jnp.where(vert_block < chip * per_group + per_group, vrow, -1)

    results = []
    for h in range(mine):
        part = pair[:, h * 2 * head_dim : (h + 1) * 2 * head_dim]
        if relative:
            across = [(i, i ^ 1) for i in range(chips)]
            up = [(i, i + 2) for i in range(chips - 2)]
            parts = []
            for step in range(chips // 2):
                parts += [part, lax.ppermute(part, "chip", across)]
                if step + 1 < chips // 2:
                    part = lax.ppermute(part, "chip", up)
        else:
            axis = "chip" if cores > 1 else ("chip", "core")
            parts = [lax.all_gather(part, axis, axis=0, tiled=True)]
        results.append(
            attend(
                idx[h].reshape(-1),
                dead[h].reshape(-1),
                own,
                query[:, h * group * head_dim : (h + 1) * group * head_dim],
                vrow[h][:, None],
                ev[h],
                parts,
                head_dim,
                group,
                listed,
            )
        )
    out = [swap(result, split_axis=0, concat_axis=1) for result in results]
    out = jnp.stack([x.reshape(tok, ways, group * head_dim) for x in out], axis=2)
    return out.reshape(tok, q_width)


def solution(mesh):
    seq, heads = mesh.shape["seq"], mesh.shape["head"]
    split = Mesh(mesh.devices.reshape(seq // 2, 2, heads), ("chip", "core", "head"))
    spec = P(("chip", "core", "head"), None)

    def run(queries, keys, values, vertical, slash):
        local_heads = vertical.shape[0] // heads
        tok = queries.shape[0] // (seq * heads)
        cores = 2 if local_heads % 2 == 0 and tok % BLK == 0 else 1
        return jax.shard_map(
            functools.partial(body, cores=cores, chips=seq // 2, heads=heads),
            mesh=split,
            in_specs=(spec, spec, spec, P("head", None), P("head", None, None)),
            out_specs=spec,
            check_vma=False,
        )(queries, keys, values, vertical, slash)

    return run
```

time: 740 us -> 135 us (0.18)
  local copies, waits for them, and re-layouts: 306 us -> 9.78 us
  blocking collectives: 235 us -> 11.9 us
  matrix products: 90.4 us -> 0 us
  other arithmetic: 69.6 us -> 1.55 us
  Pallas kernels: 0 us -> 41.8 us
  starting transfers between devices: 17.1 us -> 45.7 us
  waiting for transfers between devices: 13.1 us -> 23.5 us
    psum x1 -> x0, blocking collectives: 220 us -> none  [body(): vert_part = lax.psum(partial_rows, 'seq').astype(jnp.bfloat16)]
    reshape x19 -> x3, local copies, waits for them, and re-layouts: 135 us -> 2.95 us  [the longest x1 1.61 us: body(): return out.reshape(tok, q_width)]
    dot_general x49 -> x0, matrix products: 90.4 us -> none  [the longest x8 39.2 us: block_attention(): jnp.einsum('gqrd,gnkd->gqrnk', query_part, slash_part[..., :head_dim], pr...]
    concatenate x17 -> x1, local copies, waits for them, and re-layouts: 58.6 us -> 0.81 us  [body(): jnp.concatenate([keys.reshape(tok, ways, mine, 1, head_dim), values.resha...]
    pallas_call x0 -> x2, Pallas kernels: none -> 41.8 us  [attend(): pl.pallas_call(functools.partial(attention_kernel, parts=parts, listed=li...]
    gather x8 -> x0, local copies, waits for them, and re-layouts: 34.6 us -> none  [per_step(): slash_part = own_rows[sources, :, head_index]]
    ppermute x0 -> x14, starting transfers between devices: none -> 33.8 us  [the longest x6 24.3 us: body(): part = lax.ppermute(part, 'chip', up)]
    reduce_sum x8 -> x0, other arithmetic: 29.5 us -> none  [block_attention(): total = jnp.sum(expo, axis=-1, keepdims=True)]
  transfers between devices with their start and end apart: 4 -> 17, of which waited for: 2 -> 8; matrix products, arithmetic and copies ran while one was open for 3% -> 3% of each run, Pallas kernels for 0% -> 31%
where the time goes in v1:
time: 135 us
  starting transfers between devices  45.7 us (34%)
  Pallas kernels  41.8 us (31%)
  waiting for transfers between devices  23.5 us (17%)
  blocking collectives  11.9 us (9%)
  local copies, waits for them, and re-layouts  9.78 us (7%)
  other arithmetic  1.55 us (1%)
    pallas_call x2, Pallas kernels, attend(): pl.pallas_call(functools.partial(attention_kernel, parts=parts, listed=li...  41.8 us
    ppermute x6, starting transfers between devices, body(): part = lax.ppermute(part, 'chip', up)  24.3 us
    ppermute x8, waiting for transfers between devices, body(): parts += [part, lax.ppermute(part, 'chip', across)]  12 us
    all_to_all x1, blocking collectives, body(): out = [swap(result, split_axis=0, concat_axis=1) for result in results]  11.9 us
    ppermute x8, starting transfers between devices, body(): parts += [part, lax.ppermute(part, 'chip', across)]  9.5 us
    all_to_all x1, waiting for transfers between devices, body(): pair = swap(pair, split_axis=1, concat_axis=0)  6.47 us
    ppermute x6, waiting for transfers between devices, body(): part = lax.ppermute(part, 'chip', up)  5.06 us
    all_to_all x1, starting transfers between devices, body(): query = swap(queries, split_axis=1, concat_axis=0)  4.25 us
  transfers between devices with their start and end apart: 17, of which 8 were waited for; matrix products, arithmetic and copies ran while one was open for 3% of the time, Pallas kernels for 31%

profile of v1, /device:TPU:0, one launch (start us, length us, event | category | flops | bytes accessed | tf_op | source)
XLA Modules:
  0.0 134.7 jit_solution(6780340082709763764)
XLA Ops:
  0.0 1.2 reshape.65
  1.2 0.2 reshape.64
  1.4 0.7 pad_maximum_fusion.1
  2.1 0.8 copy.44
  2.9 1.0 all_to_all.56
  4.0 4.2 %all-to-all-start.1 = ((bf16[128,4,512]{2,0,1:T(8,128)(2,1)}), bf16[128,4,512]{2,0,1:T(8,128)(2,1)S(1)}, u32[]{:S(2)}, u32[]{:S(2)}) async-start(bf16[128,4,512]{2,0,1:T(8,128)(2,1)} %all_to_all.56), calls=%async_computation.1 | async-start | bytes 1048576 | tf_op jit(solution)/shard_map/all_to_all | solution.py:199
  8.5 1.1 copy.51
  9.6 0.7 copy-done.3
  10.3 0.2 compare_reduce_fusion
  10.6 6.5 %all-to-all-done.1 = bf16[128,4,512]{2,0,1:T(8,128)(2,1)S(1)} async-done(((bf16[128,4,512]{2,0,1:T(8,128)(2,1)}), bf16[128,4,512]{2,0,1:T(8,128)(2,1)S(1)}, u32[]{:S(2)}, u32[]{:S(2)}) %all-to-all-start.1) | async-done | bytes 524320 | tf_op jit(solution)/shard_map/all_to_all | solution.py:199
  17.0 4.3 %all-to-all-start = ((bf16[128,4,1024]{2,0,1:T(8,128)(2,1)}), bf16[128,4,1024]{2,0,1:T(8,128)(2,1)}, u32[]{:S(2)}, u32[]{:S(2)}) async-start(bf16[128,4,1024]{2,0,1:T(8,128)(2,1)} %bitcast.39), calls=%async_computation | async-start | bytes 2097152 | tf_op jit(solution)/shard_map/all_to_all | solution.py:200
  21.3 4.1 %collective-permute-start.8 = (bf16[512,256]{1,0:T(8,128)(2,1)S(1)}, bf16[512,256]{1,0:T(8,128)(2,1)S(1)}, u32[]{:S(2)}, u32[]{:S(2)}) collective-permute-start(bf16[512,256]{1,0:T(8,128)(2,1)S(1)} %get-tuple-element.10.rest_0_), channel_id=1, source_target_pairs={{0,8},{4,12},{8,16},{12,20},{16,24},{20,28},{1,9},{5,13},{9,17},{1... | collective-permute-start | bytes 786440 | tf_op jit(solution)/shard_map/ppermute | solution.py:248
  25.5 0.1 or_bitcast_fusion
  25.6 3.5 %collective-permute-start.1 = (bf16[512,256]{1,0:T(8,128)(2,1)S(1)}, bf16[512,256]{1,0:T(8,128)(2,1)S(1)}, u32[]{:S(2)}, u32[]{:S(2)}) collective-permute-start(bf16[512,256]{1,0:T(8,128)(2,1)S(1)} %get-tuple-element.9.rest_0_), channel_id=1, source_target_pairs={{0,8},{4,12},{8,16},{12,20},{16,24},{20,28},{1,9},{5,13},{9,17},{1... | collective-permute-start | bytes 786440 | tf_op jit(solution)/shard_map/ppermute | solution.py:248
  29.1 3.0 %collective-permute-done.8.rest_2_ = bf16[512,256]{1,0:T(8,128)(2,1)S(1)} collective-permute-done((bf16[512,256]{1,0:T(8,128)(2,1)S(1)}, bf16[512,256]{1,0:T(8,128)(2,1)S(1)}, u32[]{:S(2)}, u32[]{:S(2)}) %collective-permute-start.8) | collective-permute-done | bytes 262176 | tf_op jit(solution)/shard_map/ppermute | solution.py:248
  32.1 4.4 %collective-permute-start.10 = (bf16[512,256]{1,0:T(8,128)(2,1)S(1)}, bf16[512,256]{1,0:T(8,128)(2,1)S(1)}, u32[]{:S(2)}, u32[]{:S(2)}) collective-permute-start(bf16[512,256]{1,0:T(8,128)(2,1)S(1)} %collective-permute-done.8.rest_2_), channel_id=1, source_target_pairs={{0,8},{4,12},{8,16},{12,20},{16,24},{20,28},{1,9},{5,13},{9,17},{1... | collective-permute-start | bytes 786440 | tf_op jit(solution)/shard_map/ppermute | solution.py:248
  36.5 0.3 and_convert_fusion
  36.9 0.8 collective-permute-done.1.rest_2_
  37.7 4.4 %collective-permute-start.3 = (bf16[512,256]{1,0:T(8,128)(2,1)S(1)}, bf16[512,256]{1,0:T(8,128)(2,1)S(1)}, u32[]{:S(2)}, u32[]{:S(2)}) collective-permute-start(bf16[512,256]{1,0:T(8,128)(2,1)S(1)} %collective-permute-done.1.rest_2_), channel_id=1, source_target_pairs={{0,8},{4,12},{8,16},{12,20},{16,24},{20,28},{1,9},{5,13},{9,17},{1... | collective-permute-start | bytes 786440 | tf_op jit(solution)/shard_map/ppermute | solution.py:248
  42.1 1.2 collective-permute-done.10.rest_4_
  43.3 4.4 %collective-permute-start.12 = (bf16[512,256]{1,0:T(8,128)(2,1)S(1)}, bf16[512,256]{1,0:T(8,128)(2,1)S(1)}, u32[]{:S(2)}, u32[]{:S(2)}) collective-permute-start(bf16[512,256]{1,0:T(8,128)(2,1)S(1)} %collective-permute-done.10.rest_4_), channel_id=1, source_target_pairs={{0,8},{4,12},{8,16},{12,20},{16,24},{20,28},{1,9},{5,13},{9,17},{1... | collective-permute-start | bytes 786440 | tf_op jit(solution)/shard_map/ppermute | solution.py:248
  47.7 0.1 reshape_squeeze.14.idx_ref
  47.8 0.1 reshape_squeeze.15.dead_ref
  47.9 0.1 copy.46.vrow_ref
  48.1 1.6 %collective-permute-start.7 = (bf16[512,256]{1,0:T(8,128)(2,1)S(1)}, bf16[512,256]{1,0:T(8,128)(2,1)}, u32[]{:S(2)}, u32[]{:S(2)}) collective-permute-start(bf16[512,256]{1,0:T(8,128)(2,1)S(1)} %get-tuple-element.10.rest_0_), channel_id=1, source_target_pairs={{0,4},{4,0},{8,12},{12,8},{16,20},{20,16},{24,28},{28,24},{1,5},{5... | collective-permute-start | bytes 786440 | tf_op jit(solution)/shard_map/ppermute | solution.py:246
  49.6 0.5 collective-permute-start.9
  50.2 1.5 %collective-permute-start.11 = (bf16[512,256]{1,0:T(8,128)(2,1)S(1)}, bf16[512,256]{1,0:T(8,128)(2,1)}, u32[]{:S(2)}, u32[]{:S(2)}) collective-permute-start(bf16[512,256]{1,0:T(8,128)(2,1)S(1)} %collective-permute-done.10.rest_4_), channel_id=1, source_target_pairs={{0,4},{4,0},{8,12},{12,8},{16,20},{20,16},{24,28},{28,24},{1,5},{5... | collective-permute-start | bytes 786440 | tf_op jit(solution)/shard_map/ppermute | solution.py:246
  51.7 3.5 %collective-permute-start.5 = (bf16[512,256]{1,0:T(8,128)(2,1)S(1)}, bf16[512,256]{1,0:T(8,128)(2,1)S(1)}, u32[]{:S(2)}, u32[]{:S(2)}) collective-permute-start(bf16[512,256]{1,0:T(8,128)(2,1)S(1)} %collective-permute-done.3.rest_4_), channel_id=1, source_target_pairs={{0,8},{4,12},{8,16},{12,20},{16,24},{20,28},{1,9},{5,13},{9,17},{1... | collective-permute-start | bytes 786440 | tf_op jit(solution)/shard_map/ppermute | solution.py:248
  55.1 0.9 collective-permute-start.13
  56.1 1.3 fusion.28
  57.3 0.1 collective-permute-done.7.rest_1_
  57.5 1.5 %collective-permute-start = (bf16[512,256]{1,0:T(8,128)(2,1)S(1)}, bf16[512,256]{1,0:T(8,128)(2,1)}, u32[]{:S(2)}, u32[]{:S(2)}) collective-permute-start(bf16[512,256]{1,0:T(8,128)(2,1)S(1)} %get-tuple-element.9.rest_0_), channel_id=1, source_target_pairs={{0,4},{4,0},{8,12},{12,8},{16,20},{20,16},{24,28},{28,24},{1,5},{5... | collective-permute-start | bytes 786440 | tf_op jit(solution)/shard_map/ppermute | solution.py:246
  59.0 4.1 %collective-permute-done.9.rest_3_ = bf16[512,256]{1,0:T(8,128)(2,1)} collective-permute-done((bf16[512,256]{1,0:T(8,128)(2,1)S(1)}, bf16[512,256]{1,0:T(8,128)(2,1)}, u32[]{:S(2)}, u32[]{:S(2)}) %collective-permute-start.9) | collective-permute-done | bytes 262176 | tf_op jit(solution)/shard_map/ppermute | solution.py:246
  63.1 1.5 %collective-permute-start.2 = (bf16[512,256]{1,0:T(8,128)(2,1)S(1)}, bf16[512,256]{1,0:T(8,128)(2,1)}, u32[]{:S(2)}, u32[]{:S(2)}) collective-permute-start(bf16[512,256]{1,0:T(8,128)(2,1)S(1)} %collective-permute-done.1.rest_2_), channel_id=1, source_target_pairs={{0,4},{4,0},{8,12},{12,8},{16,20},{20,16},{24,28},{28,24},{1,5},{5... | collective-permute-start | bytes 786440 | tf_op jit(solution)/shard_map/ppermute | solution.py:246
  64.6 4.1 %collective-permute-done.11.rest_5_ = bf16[512,256]{1,0:T(8,128)(2,1)} collective-permute-done((bf16[512,256]{1,0:T(8,128)(2,1)S(1)}, bf16[512,256]{1,0:T(8,128)(2,1)}, u32[]{:S(2)}, u32[]{:S(2)}) %collective-permute-start.11) | collective-permute-done | bytes 262176 | tf_op jit(solution)/shard_map/ppermute | solution.py:246
  68.7 1.5 %collective-permute-start.4 = (bf16[512,256]{1,0:T(8,128)(2,1)S(1)}, bf16[512,256]{1,0:T(8,128)(2,1)}, u32[]{:S(2)}, u32[]{:S(2)}) collective-permute-start(bf16[512,256]{1,0:T(8,128)(2,1)S(1)} %collective-permute-done.3.rest_4_), channel_id=1, source_target_pairs={{0,4},{4,0},{8,12},{12,8},{16,20},{20,16},{24,28},{28,24},{1,5},{5... | collective-permute-start | bytes 786440 | tf_op jit(solution)/shard_map/ppermute | solution.py:246
  70.2 0.5 collective-permute-start.6
  70.7 3.6 %collective-permute-done.13.rest_7_ = bf16[512,256]{1,0:T(8,128)(2,1)} collective-permute-done((bf16[512,256]{1,0:T(8,128)(2,1)S(1)}, bf16[512,256]{1,0:T(8,128)(2,1)}, u32[]{:S(2)}, u32[]{:S(2)}) %collective-permute-start.13) | collective-permute-done | bytes 262176 | tf_op jit(solution)/shard_map/ppermute | solution.py:246
  74.3 21.3 %shard_map.56 = bf16[512,512]{1,0:T(8,128)(2,1)} custom-call(s32[320]{0:T(512)S(1)} %reshape_squeeze.14.idx_ref, s32[320]{0:T(512)S(1)} %reshape_squeeze.15.dead_ref, s32[1]{0:T(128)} %constant.215.clone.1.own_ref, bf16[512,512]{1,0:T(8,128)(2,1)S(1)} %get-tuple-element.8.q_ref, s32[128,1]{1,0:T(8,128)S(1)} %copy.46.vrow_ref, ...), custom_call_target="tpu_custom_call" | custom-call | flops 2952790016 | bytes 3145728 | tf_op jit(solution)/shard_map/pallas_call | solution.py:150
  95.7 3.5 %all-to-all-start.3 = ((bf16[4,128,512]{2,1,0:T(8,128)(2,1)}), bf16[4,128,512]{2,1,0:T(8,128)(2,1)S(1)}, u32[]{:S(2)}, u32[]{:S(2)}) async-start(bf16[4,128,512]{2,1,0:T(8,128)(2,1)} %bitcast.22), calls=%async_computation.3 | async-start | bytes 1048576 | tf_op jit(solution)/shard_map/all_to_all | solution.py:266
  99.2 0.1 reshape_squeeze.12.idx_ref
  99.2 0.1 reshape_squeeze.13.dead_ref
  99.3 0.1 copy.45.vrow_ref
  99.5 20.5 %shard_map.55 = bf16[512,512]{1,0:T(8,128)(2,1)S(1)} custom-call(s32[320]{0:T(512)S(1)} %reshape_squeeze.12.idx_ref, s32[320]{0:T(512)S(1)} %reshape_squeeze.13.dead_ref, s32[1]{0:T(128)} %constant.215.clone.1.own_ref, bf16[512,512]{1,0:T(8,128)(2,1)S(1)} %get-tuple-element.7.q_ref, s32[128,1]{1,0:T(8,128)S(1)} %copy.45.vrow_ref, ...), custom_call_target="tpu_custom_call" | custom-call | flops 2952790016 | bytes 3145728 | tf_op jit(solution)/shard_map/pallas_call | solution.py:150
  120.0 11.9 %all_to_all.70 = bf16[4,128,512]{2,1,0:T(8,128)(2,1)S(1)} all-to-all(bf16[4,128,512]{2,1,0:T(8,128)(2,1)S(1)} %bitcast.40), channel_id=1, replica_groups=mesh['chip'=8,'core'=2,'head'=2] {'head','core'}, dimensions={0} | all-to-all | bytes 1048576 | tf_op jit(solution)/shard_map/all_to_all | solution.py:266
  131.9 0.1 pad_maximum_fusion
  132.0 1.1 copy.47
  133.1 1.6 %reshape.66 = bf16[128,4096]{1,0:T(8,128)(2,1)} reshape(bf16[128,4,2,512]{3,2,1,0:T(2,128)(2,1)S(1)} %copy.47) | data formatting | bytes 2097152 | tf_op jit(solution)/shard_map/reshape | solution.py:268
  (41 shorter events, 0.5 us)
Async XLA Ops:
  0.0 8.2 %copy-start = (s32[4,64,40]{1,2,0:T(8,128)S(1)}, s32[4,64,40]{1,2,0:T(8,128)}, u32[]{:S(2)}) copy-start(s32[4,64,40]{1,2,0:T(8,128)} %param.9) | copy-start | bytes 122884
  0.0 1.2 copy-start.2
  2.9 5.6 %copy-start.1 = (bf16[128,4096]{1,0:T(8,128)(2,1)S(1)}, bf16[128,4096]{1,0:T(8,128)(2,1)}, u32[]{:S(2)}) copy-start(bf16[128,4096]{1,0:T(8,128)(2,1)} %param.5) | copy-start | bytes 3145732
  4.0 13.1 %all-to-all-start.1 = ((bf16[128,4,512]{2,0,1:T(8,128)(2,1)}), bf16[128,4,512]{2,0,1:T(8,128)(2,1)S(1)}, u32[]{:S(2)}, u32[]{:S(2)}) async-start(bf16[128,4,512]{2,0,1:T(8,128)(2,1)} %all_to_all.56), calls=%async_computation.1 | async-start | bytes 1048576 | tf_op jit(solution)/shard_map/all_to_all | solution.py:199
  9.6 0.7 copy-start.3
  17.0 39.0 %all-to-all-start = ((bf16[128,4,1024]{2,0,1:T(8,128)(2,1)}), bf16[128,4,1024]{2,0,1:T(8,128)(2,1)}, u32[]{:S(2)}, u32[]{:S(2)}) async-start(bf16[128,4,1024]{2,0,1:T(8,128)(2,1)} %bitcast.39), calls=%async_computation | async-start | bytes 2097152 | tf_op jit(solution)/shard_map/all_to_all | solution.py:200
  21.3 10.7 %collective-permute-start.8 = (bf16[512,256]{1,0:T(8,128)(2,1)S(1)}, bf16[512,256]{1,0:T(8,128)(2,1)S(1)}, u32[]{:S(2)}, u32[]{:S(2)}) collective-permute-start(bf16[512,256]{1,0:T(8,128)(2,1)S(1)} %get-tuple-element.10.rest_0_), channel_id=1, source_target_pairs={{0,8},{4,12},{8,16},{12,20},{16,24},{20,28},{1,9},{5,13},{9,17},{1... | collective-permute-start | bytes 786440 | tf_op jit(solution)/shard_map/ppermute | solution.py:248
  25.6 12.1 %collective-permute-start.1 = (bf16[512,256]{1,0:T(8,128)(2,1)S(1)}, bf16[512,256]{1,0:T(8,128)(2,1)S(1)}, u32[]{:S(2)}, u32[]{:S(2)}) collective-permute-start(bf16[512,256]{1,0:T(8,128)(2,1)S(1)} %get-tuple-element.9.rest_0_), channel_id=1, source_target_pairs={{0,8},{4,12},{8,16},{12,20},{16,24},{20,28},{1,9},{5,13},{9,17},{1... | collective-permute-start | bytes 786440 | tf_op jit(solution)/shard_map/ppermute | solution.py:248
  32.1 11.2 %collective-permute-start.10 = (bf16[512,256]{1,0:T(8,128)(2,1)S(1)}, bf16[512,256]{1,0:T(8,128)(2,1)S(1)}, u32[]{:S(2)}, u32[]{:S(2)}) collective-permute-start(bf16[512,256]{1,0:T(8,128)(2,1)S(1)} %collective-permute-done.8.rest_2_), channel_id=1, source_target_pairs={{0,8},{4,12},{8,16},{12,20},{16,24},{20,28},{1,9},{5,13},{9,17},{1... | collective-permute-start | bytes 786440 | tf_op jit(solution)/shard_map/ppermute | solution.py:248
  37.7 13.9 %collective-permute-start.3 = (bf16[512,256]{1,0:T(8,128)(2,1)S(1)}, bf16[512,256]{1,0:T(8,128)(2,1)S(1)}, u32[]{:S(2)}, u32[]{:S(2)}) collective-permute-start(bf16[512,256]{1,0:T(8,128)(2,1)S(1)} %collective-permute-done.1.rest_2_), channel_id=1, source_target_pairs={{0,8},{4,12},{8,16},{12,20},{16,24},{20,28},{1,9},{5,13},{9,17},{1... | collective-permute-start | bytes 786440 | tf_op jit(solution)/shard_map/ppermute | solution.py:248
  43.3 11.8 %collective-permute-start.12 = (bf16[512,256]{1,0:T(8,128)(2,1)S(1)}, bf16[512,256]{1,0:T(8,128)(2,1)S(1)}, u32[]{:S(2)}, u32[]{:S(2)}) collective-permute-start(bf16[512,256]{1,0:T(8,128)(2,1)S(1)} %collective-permute-done.10.rest_4_), channel_id=1, source_target_pairs={{0,8},{4,12},{8,16},{12,20},{16,24},{20,28},{1,9},{5,13},{9,17},{1... | collective-permute-start | bytes 786440 | tf_op jit(solution)/shard_map/ppermute | solution.py:248
  48.1 9.4 %collective-permute-start.7 = (bf16[512,256]{1,0:T(8,128)(2,1)S(1)}, bf16[512,256]{1,0:T(8,128)(2,1)}, u32[]{:S(2)}, u32[]{:S(2)}) collective-permute-start(bf16[512,256]{1,0:T(8,128)(2,1)S(1)} %get-tuple-element.10.rest_0_), channel_id=1, source_target_pairs={{0,4},{4,0},{8,12},{12,8},{16,20},{20,16},{24,28},{28,24},{1,5},{5... | collective-permute-start | bytes 786440 | tf_op jit(solution)/shard_map/ppermute | solution.py:246
  49.6 13.5 %collective-permute-start.9 = (bf16[512,256]{1,0:T(8,128)(2,1)S(1)}, bf16[512,256]{1,0:T(8,128)(2,1)}, u32[]{:S(2)}, u32[]{:S(2)}) collective-permute-start(bf16[512,256]{1,0:T(8,128)(2,1)S(1)} %collective-permute-done.8.rest_2_), channel_id=1, source_target_pairs={{0,4},{4,0},{8,12},{12,8},{16,20},{20,16},{24,28},{28,24},{1,5},{5... | collective-permute-start | bytes 786440 | tf_op jit(solution)/shard_map/ppermute | solution.py:246
  50.2 18.6 %collective-permute-start.11 = (bf16[512,256]{1,0:T(8,128)(2,1)S(1)}, bf16[512,256]{1,0:T(8,128)(2,1)}, u32[]{:S(2)}, u32[]{:S(2)}) collective-permute-start(bf16[512,256]{1,0:T(8,128)(2,1)S(1)} %collective-permute-done.10.rest_4_), channel_id=1, source_target_pairs={{0,4},{4,0},{8,12},{12,8},{16,20},{20,16},{24,28},{28,24},{1,5},{5... | collective-permute-start | bytes 786440 | tf_op jit(solution)/shard_map/ppermute | solution.py:246
  51.7 18.6 %collective-permute-start.5 = (bf16[512,256]{1,0:T(8,128)(2,1)S(1)}, bf16[512,256]{1,0:T(8,128)(2,1)S(1)}, u32[]{:S(2)}, u32[]{:S(2)}) collective-permute-start(bf16[512,256]{1,0:T(8,128)(2,1)S(1)} %collective-permute-done.3.rest_4_), channel_id=1, source_target_pairs={{0,8},{4,12},{8,16},{12,20},{16,24},{20,28},{1,9},{5,13},{9,17},{1... | collective-permute-start | bytes 786440 | tf_op jit(solution)/shard_map/ppermute | solution.py:248
  55.1 19.2 %collective-permute-start.13 = (bf16[512,256]{1,0:T(8,128)(2,1)S(1)}, bf16[512,256]{1,0:T(8,128)(2,1)}, u32[]{:S(2)}, u32[]{:S(2)}) collective-permute-start(bf16[512,256]{1,0:T(8,128)(2,1)S(1)} %collective-permute-done.12.rest_6_), channel_id=1, source_target_pairs={{0,4},{4,0},{8,12},{12,8},{16,20},{20,16},{24,28},{28,24},{1,5},{5... | collective-permute-start | bytes 786440 | tf_op jit(solution)/shard_map/ppermute | solution.py:246
  57.5 41.9 %collective-permute-start = (bf16[512,256]{1,0:T(8,128)(2,1)S(1)}, bf16[512,256]{1,0:T(8,128)(2,1)}, u32[]{:S(2)}, u32[]{:S(2)}) collective-permute-start(bf16[512,256]{1,0:T(8,128)(2,1)S(1)} %get-tuple-element.9.rest_0_), channel_id=1, source_target_pairs={{0,4},{4,0},{8,12},{12,8},{16,20},{20,16},{24,28},{28,24},{1,5},{5... | collective-permute-start | bytes 786440 | tf_op jit(solution)/shard_map/ppermute | solution.py:246
  63.1 36.3 %collective-permute-start.2 = (bf16[512,256]{1,0:T(8,128)(2,1)S(1)}, bf16[512,256]{1,0:T(8,128)(2,1)}, u32[]{:S(2)}, u32[]{:S(2)}) collective-permute-start(bf16[512,256]{1,0:T(8,128)(2,1)S(1)} %collective-permute-done.1.rest_2_), channel_id=1, source_target_pairs={{0,4},{4,0},{8,12},{12,8},{16,20},{20,16},{24,28},{28,24},{1,5},{5... | collective-permute-start | bytes 786440 | tf_op jit(solution)/shard_map/ppermute | solution.py:246
  68.7 30.7 %collective-permute-start.4 = (bf16[512,256]{1,0:T(8,128)(2,1)S(1)}, bf16[512,256]{1,0:T(8,128)(2,1)}, u32[]{:S(2)}, u32[]{:S(2)}) collective-permute-start(bf16[512,256]{1,0:T(8,128)(2,1)S(1)} %collective-permute-done.3.rest_4_), channel_id=1, source_target_pairs={{0,4},{4,0},{8,12},{12,8},{16,20},{20,16},{24,28},{28,24},{1,5},{5... | collective-permute-start | bytes 786440 | tf_op jit(solution)/shard_map/ppermute | solution.py:246
  70.2 29.2 %collective-permute-start.6 = (bf16[512,256]{1,0:T(8,128)(2,1)S(1)}, bf16[512,256]{1,0:T(8,128)(2,1)}, u32[]{:S(2)}, u32[]{:S(2)}) collective-permute-start(bf16[512,256]{1,0:T(8,128)(2,1)S(1)} %collective-permute-done.5.rest_6_), channel_id=1, source_target_pairs={{0,4},{4,0},{8,12},{12,8},{16,20},{20,16},{24,28},{28,24},{1,5},{5... | collective-permute-start | bytes 786440 | tf_op jit(solution)/shard_map/ppermute | solution.py:246
  95.7 24.3 %all-to-all-start.3 = ((bf16[4,128,512]{2,1,0:T(8,128)(2,1)}), bf16[4,128,512]{2,1,0:T(8,128)(2,1)S(1)}, u32[]{:S(2)}, u32[]{:S(2)}) async-start(bf16[4,128,512]{2,1,0:T(8,128)(2,1)} %bitcast.22), calls=%async_computation.3 | async-start | bytes 1048576 | tf_op jit(solution)/shard_map/all_to_all | solution.py:266

commit v2 on v1

v2 whole, which is shorter than its diff:
```python
import functools
import math

import jax
import jax.numpy as jnp
from jax import lax
from jax.experimental import pallas as pl
from jax.experimental.pallas import tpu as pltpu
from jax.sharding import Mesh, PartitionSpec as P

BLK = 64
BIG = 1.0e30
LIVE, DEAD, OWN, PICKED = 0, 1, 2, 3
BF16, F32 = jnp.bfloat16, jnp.float32


def arrange_kernel(k_ref, v_ref, o_ref):
    width = v_ref.shape[0]
    head_dim = o_ref.shape[2] - width
    for h in range(o_ref.shape[0]):
        o_ref[h, :, :head_dim] = k_ref[:, h * head_dim : (h + 1) * head_dim]
        o_ref[h, :, head_dim:] = v_ref[:, h * head_dim : (h + 1) * head_dim].T


def arrange(keys, values, heads):
    tok, width = keys.shape
    head_dim = width // heads
    return pl.pallas_call(
        arrange_kernel,
        out_shape=jax.ShapeDtypeStruct((heads, tok, head_dim + tok), BF16),
    )(keys, values)


def step_kernel(code_ref, q_ref, pick_ref, *rest, parts, first, last, heads, head_dim, group):
    part_refs = rest[:parts]
    rest = rest[parts:]
    if first:
        acc_in = stat_in = None
    else:
        acc_in, stat_in = rest[:2]
        rest = rest[2:]
    if last:
        out_ref = rest[0]
        rest = rest[1:]
    else:
        acc_out, stat_out = rest[:2]
        rest = rest[2:]
    qext, etile, score_a, score_b = rest
    rows = BLK * group
    chunks, _, wide, _ = part_refs[0].shape
    per_chunk = wide // BLK
    per_part = chunks * per_chunk
    slots = parts * per_part
    blocks_here = q_ref.shape[0] * q_ref.shape[1] // BLK
    scale = math.log2(math.e) / math.sqrt(head_dim)

    token = lax.rem(lax.broadcasted_iota(jnp.int32, (rows, head_dim), 0), BLK)
    column = lax.broadcasted_iota(jnp.int32, (rows, head_dim), 1)
    masked = ((column < BLK) & (column > token)) | (column == BLK)
    qext[...] = jnp.where(masked, -BIG, 0.0).astype(BF16)
    key_iota = lax.broadcasted_iota(jnp.int32, (BLK, head_dim), 0)
    lane = lax.broadcasted_iota(jnp.int32, (BLK, head_dim), 1)
    etile[LIVE] = jnp.zeros((BLK, head_dim), BF16)
    etile[DEAD] = jnp.where(lane == BLK, 1.0, 0.0).astype(BF16)
    etile[OWN] = jnp.where(lane == key_iota, 1.0, 0.0).astype(BF16)

    def pair_loop(h):
        for slot in range(slots):
            etile[PICKED + slot] = pick_ref[h, slot]

        def scored(here, buffer):
            chunk = here // per_q
            start = pl.multiple_of(lax.rem(here, per_q) * BLK, BLK)
            query = jnp.concatenate(
                [
                    q_ref[chunk, pl.ds(start, BLK), pl.ds((h * group + g) * head_dim, head_dim)]
                    for g in range(group)
                ],
                axis=0,
            )
            query = jnp.concatenate([query, qext[...]], axis=1)
            at = (h * blocks_here + here) * slots
            top = jnp.full((8, rows), -jnp.inf, F32)
            size = per_part * BLK
            for p, part in enumerate(part_refs):
                left = [part[c, h, :, pl.ds(0, head_dim)] for c in range(chunks)]
                right = [etile[code_ref[at + p * per_part + i]] for i in range(per_part)]
                key = jnp.concatenate(
                    [jnp.concatenate(left, axis=0), jnp.concatenate(right, axis=0)], axis=1
                )
                tile = lax.dot_general(
                    key, query, (((1,), (1,)), ((), ())), preferred_element_type=F32
                )
                buffer[pl.ds(p * size, size), :] = tile
                top = jnp.maximum(top, jnp.max(tile.reshape(size // 8, 8, rows), axis=0))
            return jnp.max(top, axis=0, keepdims=True)

        def mixed_in(here, buffer, top):
            pair = h * blocks_here + here
            if first:
                top = jnp.broadcast_to(top, (8, rows))
                weight = jnp.zeros((8, rows), F32)
            else:
                before = stat_in[pair, :8]
                top = jnp.maximum(top, before)
                fade = jnp.exp2((before - top) * scale)
                weight = stat_in[pair, 8:] * fade
            mixed = jnp.zeros((head_dim, rows), F32)
            size = per_part * BLK
            for p, part in enumerate(part_refs):
                tile = buffer[pl.ds(p * size, size), :].reshape(size // 8, 8, rows)
                expo = jnp.exp2((tile - top[None]) * scale)
                weight = weight + jnp.sum(expo, axis=0)
                value = jnp.concatenate(
                    [part[c, h, :, pl.ds(head_dim, wide)] for c in range(chunks)], axis=1
                )
                mixed = mixed + jnp.dot(
                    value, expo.reshape(size, rows).astype(BF16), preferred_element_type=F32
                )
            if not first:
                mixed = mixed + acc_in[pair] * fade[:1]
            if not last:
                acc_out[pair] = mixed
                stat_out[pair, :8] = top
                stat_out[pair, 8:] = weight
                return
            result = (mixed / jnp.sum(weight, axis=0, keepdims=True)).T.astype(BF16)
            chunk = here // per_q
            start = pl.multiple_of(lax.rem(here, per_q) * BLK, BLK)
            for g in range(group):
                out_ref[chunk, pl.ds(start, BLK), pl.ds((h * group + g) * head_dim, head_dim)] = (
                    result[g * BLK : (g + 1) * BLK]
                )

        per_q = q_ref.shape[1] // BLK

        @pl.loop(0, blocks_here // 2)
        def _(step):
            top_a = scored(2 * step, score_a)
            top_b = scored(2 * step + 1, score_b)
            mixed_in(2 * step, score_a, top_a)
            mixed_in(2 * step + 1, score_b, top_b)

    for h in range(heads):
        pair_loop(h)


def attend_step(code, query, pick, parts, state, last, head_dim, group):
    heads = pick.shape[0]
    slots = pick.shape[1]
    blocks_here = query.shape[0] * query.shape[1] // BLK
    rows = BLK * group
    pairs = heads * blocks_here
    first = state is None
    smem = pl.BlockSpec(memory_space=pltpu.SMEM)
    vmem = pl.BlockSpec(memory_space=pltpu.VMEM)
    state_shape = (
        jax.ShapeDtypeStruct((pairs, head_dim, rows), F32),
        jax.ShapeDtypeStruct((pairs, 16, rows), F32),
    )
    state = () if first else tuple(state)
    work = pairs * rows * slots * BLK
    return pl.pallas_call(
        functools.partial(
            step_kernel,
            parts=len(parts),
            first=first,
            last=last,
            heads=heads,
            head_dim=head_dim,
            group=group,
        ),
        out_shape=jax.ShapeDtypeStruct(query.shape, BF16) if last else state_shape,
        in_specs=[smem] + [vmem] * (2 + len(parts) + len(state)),
        out_specs=vmem if last else (vmem, vmem),
        scratch_shapes=[
            pltpu.VMEM((rows, head_dim), BF16),
            pltpu.VMEM((PICKED + slots, BLK, head_dim), BF16),
            pltpu.VMEM((slots * BLK, rows), F32),
            pltpu.VMEM((slots * BLK, rows), F32),
        ],
        compiler_params=pltpu.CompilerParams(vmem_limit_bytes=40 << 20),
        cost_estimate=pl.CostEstimate(
            flops=4 * work * head_dim,
            transcendentals=work,
            bytes_accessed=8 << 20,
        ),
    )(code, query, pick, *parts, *state)


def body(queries, keys, values, vertical, slash, *, cores, chips, heads):
    tok, q_width = queries.shape
    all_heads = vertical.shape[0] * heads
    head_dim = keys.shape[1] // all_heads
    group = q_width // keys.shape[1]
    ways = cores * heads
    mine = all_heads // ways
    axes = ("head", "core") if cores > 1 else ("head",)
    groups = chips if cores > 1 else chips * 2
    per_group = tok * ways // BLK
    chip = lax.axis_index("chip")
    if cores == 1:
        chip = chip * 2 + lax.axis_index("core")
    relative = cores > 1 and chips == 8
    swap = functools.partial(
        lax.all_to_all, axis_name=axes, split_axis=0, concat_axis=0, tiled=True
    )

    if relative:
        pair = swap(arrange(keys, values, all_heads).reshape(ways, mine, tok, head_dim + tok))
    else:
        pair = jnp.concatenate(
            [keys.reshape(tok, ways, mine, head_dim), values.reshape(tok, ways, mine, head_dim)],
            axis=3,
        )
        pair = swap(pair.transpose(1, 2, 0, 3))
    query = swap(queries.reshape(tok, ways, q_width // ways).transpose(1, 0, 2))
    query = query.reshape(-1, max(tok, BLK), q_width // ways)

    along = tok // BLK
    local = jnp.arange(per_group, dtype=jnp.int32)
    if cores > 1:
        local = local.reshape(cores, heads, along).swapaxes(0, 1).reshape(-1)
    first_head = lax.axis_index("core") * mine if cores > 1 else 0
    slash = lax.dynamic_slice_in_dim(slash, first_head, mine, axis=0)
    vertical = lax.dynamic_slice_in_dim(vertical, first_head, mine, axis=0)
    lists = lax.dynamic_slice_in_dim(slash, chip * per_group, per_group, axis=1)
    if cores > 1:
        lists = (
            lists.reshape(mine, cores, heads, along, -1).swapaxes(1, 2).reshape(lists.shape)
        )
    ids = chip * per_group + local

    if relative:
        across = [(i, i ^ 1) for i in range(chips)]
        up = [(i, i + 2) for i in range(chips - 2)]
        steps = []
        part = pair
        for step in range(chips // 2):
            later = lax.ppermute(part, "chip", up) if step + 1 < chips // 2 else None
            other = lax.ppermute(part, "chip", across)
            source = chip // 2 - step
            col = jnp.stack([chip % 2, 1 - chip % 2])
            source = jnp.where(source < 0, groups, 2 * source + col)
            steps.append(((part, other), source))
            part = later
    else:
        axis = "chip" if cores > 1 else ("chip", "core")
        rows = pair.transpose(1, 0, 2, 3).reshape(mine, -1, 2 * head_dim)
        rows = lax.all_gather(rows, axis, axis=1, tiled=True)
        pieces = rows.shape[1] // (2 * BLK)
        turned = rows[..., head_dim:].reshape(mine, pieces, 2 * BLK, head_dim).swapaxes(2, 3)
        rows = rows[..., :head_dim].reshape(mine, pieces, 2 * BLK, head_dim)
        rows = jnp.concatenate([rows, turned], axis=3).swapaxes(0, 1)
        each = per_group // 2
        order = (chip + jnp.arange(groups, dtype=jnp.int32)) % groups
        rows = jnp.roll(rows.reshape((groups, each) + rows.shape[1:]), -chip, axis=0)
        many = math.gcd(groups, 4)
        steps = [
            ((rows[g : g + many].reshape((many * each,) + rows.shape[2:]),), order[g : g + many])
            for g in range(0, groups, many)
        ]

    state = None
    for n, (parts, source) in enumerate(steps):
        nat = (source[:, None] * per_group + local).reshape(-1)
        listed = jnp.any(lists[:, :, :, None] == nat, axis=2)
        slot = PICKED + jnp.arange(nat.shape[0], dtype=jnp.int32)
        code = jnp.where(
            listed,
            LIVE,
            jnp.where(nat == ids[:, None], OWN, jnp.where(nat > ids[:, None], DEAD, slot)),
        )
        position = nat[:, None] * BLK + jnp.arange(BLK, dtype=jnp.int32)
        hidden = jnp.all(vertical[:, None, None, :] != position[..., None], axis=3)
        lane = jnp.arange(head_dim, dtype=jnp.int32) == BLK
        pick = (hidden[..., None] & lane).astype(BF16)
        state = attend_step(
            code.reshape(-1), query, pick, parts, state, n + 1 == len(steps), head_dim, group
        )
    out = swap(state.reshape(ways, tok, q_width // ways))
    return out.transpose(1, 0, 2).reshape(tok, q_width)


def solution(mesh):
    seq, heads = mesh.shape["seq"], mesh.shape["head"]
    split = Mesh(mesh.devices.reshape(seq // 2, 2, heads), ("chip", "core", "head"))
    spec = P(("chip", "core", "head"), None)

    def run(queries, keys, values, vertical, slash):
        local_heads = vertical.shape[0] // heads
        tok = queries.shape[0] // (seq * heads)
        cores = 2 if local_heads % 2 == 0 and tok % BLK == 0 else 1
        return jax.shard_map(
            functools.partial(body, cores=cores, chips=seq // 2, heads=heads),
            mesh=split,
            in_specs=(spec, spec, spec, P("head", None), P("head", None, None)),
            out_specs=spec,
            check_vma=False,
        )(queries, keys, values, vertical, slash)

    return run
```

time: 135 us -> 120 us (0.89)
  starting transfers between devices: 45.7 us -> 28.3 us
  Pallas kernels: 41.8 us -> 35.3 us
  blocking collectives: 11.9 us -> 16.9 us
  local copies, waits for them, and re-layouts: 9.78 us -> 4.84 us
  waiting for transfers between devices: 23.5 us -> 28.4 us
  other arithmetic: 1.55 us -> 6 us
    ppermute x14 -> x7, starting transfers between devices: 33.8 us -> 20.5 us  [the longest x3 15.5 us: body(): later = lax.ppermute(part, 'chip', up) if step + 1 < chips // 2 else None]
    ppermute x14 -> x7, waiting for transfers between devices: 17.1 us -> 26 us  [the longest x3 26 us: body(): later = lax.ppermute(part, 'chip', up) if step + 1 < chips // 2 else None]
    pallas_call x2 -> x5, Pallas kernels: 41.8 us -> 35.3 us  [the longest x4 33.3 us: attend_step(): pl.pallas_call(functools.partial(step_kernel, parts=len(parts), first=fir...]
    all_to_all x1, blocking collectives: 11.9 us -> 16.9 us  [body(): out = swap(state.reshape(ways, tok, q_width // ways))]
    all_to_all x3 -> x2, starting transfers between devices: 12 us -> 7.76 us  [the longest x1 4.24 us: body(): swap(arrange(keys, values, all_heads).reshape(ways, mine, tok, head_dim +...]
    all_to_all x3 -> x2, waiting for transfers between devices: 6.48 us -> 2.37 us  [the longest x1 2.37 us: body(): swap(arrange(keys, values, all_heads).reshape(ways, mine, tok, head_dim +...]
    reduce_and x0 -> x1, other arithmetic: none -> 2.91 us  [body(): hidden = jnp.all(vertical[:, None, None, :] != position[..., None], axis=3)]
    all_to_all x2 -> x0, local copies, waits for them, and re-layouts: 2.08 us -> none  [the longest x1 1.06 us: body(): query = swap(queries, split_axis=1, concat_axis=0)]
  transfers between devices with their start and end apart: 17 -> 9, of which waited for: 8 -> 4; matrix products, arithmetic and copies ran while one was open for 3% -> 7% of each run, Pallas kernels for 31% -> 20%
where the time goes in v2:
time: 120 us
  Pallas kernels  35.3 us (29%)
  waiting for transfers between devices  28.4 us (24%)
  starting transfers between devices  28.3 us (24%)
  blocking collectives  16.9 us (14%)
  other arithmetic  6 us (5%)
  local copies, waits for them, and re-layouts  4.84 us (4%)
    pallas_call x4, Pallas kernels, attend_step(): pl.pallas_call(functools.partial(step_kernel, parts=len(parts), first=fir...  33.3 us
    ppermute x3, waiting for transfers between devices, body(): later = lax.ppermute(part, 'chip', up) if step + 1 < chips // 2 else None  26 us
    all_to_all x1, blocking collectives, body(): out = swap(state.reshape(ways, tok, q_width // ways))  16.9 us
    ppermute x3, starting transfers between devices, body(): later = lax.ppermute(part, 'chip', up) if step + 1 < chips // 2 else None  15.5 us
    ppermute x4, starting transfers between devices, body(): other = lax.ppermute(part, 'chip', across)  5.08 us
    all_to_all x1, starting transfers between devices, body(): swap(arrange(keys, values, all_heads).reshape(ways, mine, tok, head_dim +...  4.24 us
    all_to_all x1, starting transfers between devices, body(): query = swap(queries.reshape(tok, ways, q_width // ways).transpose(1, 0, 2))  3.52 us
    reduce_and x1, other arithmetic, body(): hidden = jnp.all(vertical[:, None, None, :] != position[..., None], axis=3)  2.91 us
  transfers between devices with their start and end apart: 9, of which 4 were waited for; matrix products, arithmetic and copies ran while one was open for 7% of the time, Pallas kernels for 20%

profile of v2, /device:TPU:0, one launch (start us, length us, event | category | flops | bytes accessed | tf_op | source)
XLA Modules:
  0.0 119.9 jit_solution(2896158634873205179)
XLA Ops:
  0.0 2.0 %shard_map.55 = bf16[8,128,256]{2,1,0:T(8,128)(2,1)} custom-call(bf16[128,1024]{1,0:T(8,128)(2,1)} %k_ref.1, bf16[128,1024]{1,0:T(8,128)(2,1)} %v_ref.1), custom_call_target="tpu_custom_call" | custom-call | tf_op jit(solution)/shard_map/pallas_call | solution.py:28
  2.0 4.2 %all-to-all-start.1 = ((bf16[4,2,128,256]{3,2,1,0:T(8,128)(2,1)}), bf16[4,2,128,256]{3,2,1,0:T(8,128)(2,1)}, u32[]{:S(2)}, u32[]{:S(2)}) async-start(bf16[4,2,128,256]{3,2,1,0:T(8,128)(2,1)} %bitcast.14), calls=%async_computation.1 | async-start | bytes 1048576 | tf_op jit(solution)/shard_map/all_to_all | solution.py:210
  6.3 0.1 reshape.485
  6.4 0.1 fusion
  6.5 0.1 broadcast_add_fusion.3
  6.5 0.1 add.330
  6.6 0.1 add.322
  6.7 0.1 add.314
  6.8 0.1 add.303
  6.9 0.1 constant_dynamic-slice_fusion.1
  7.0 0.1 copy.18
  7.0 1.3 %compare_reduce_fusion.4 = (pred[2,8,16]{2,1,0:T(8,128)(4,1)S(1)}, pred[2,8,16]{2,1,0:T(8,128)(4,1)S(1)}, pred[2,8,16]{2,1,0:T(8,128)(4,1)S(1)}, pred[2,8,16]{2,1,0:T(8,128)(4,1)S(1)}) fusion(s32[2,8,40]{2,1,0:T(8,128)S(1)} %bitcast.15, s32[16]{0:T(128)S(1)} %add.330, s32[16]{0:T(128)S(1)} %add.314, s32[16]{0:T(128)S(1)} %add.322, s32[16]{0:T(128)S(1)} %add.303), kind=kLoop, calls=%fused_computation.8 | loop fusion | flops 80896 | bytes 3840 | tf_op jit(solution)/shard_map/reduce_or | solution.py:267
  8.3 0.1 iota_add_fusion
  8.4 0.0 copy-done.2
  8.4 0.7 copy.14
  9.1 1.3 %copy.15 = bf16[128,4,1024]{2,0,1:T(8,128)(2,1)} copy(bf16[128,4,1024]{0,2,1:T(8,128)(2,1)S(1)} %bitcast.13) | data formatting | bytes 2097152 | tf_op jit(solution)/shard_map/reshape | solution.py:217
  10.4 0.1 iota_add_fusion.2
  10.5 2.9 %compare_reduce_fusion = (pred[2,16,64]{2,1,0:T(8,128)(4,1)S(1)}, pred[2,16,64]{2,1,0:T(8,128)(4,1)S(1)}, pred[2,16,64]{2,1,0:T(8,128)(4,1)S(1)}, pred[2,16,64]{2,1,0:T(8,128)(4,1)S(1)}) fusion(s32[16,64]{1,0:T(8,128)S(1)} %get-tuple-element.42, s32[2,128]{1,0:T(2,128)S(1)} %constant_dynamic-slice_fusion, s32[16,64]{1,0:T(8,128)S(1)} %get-tuple-element.44, ...), kind=kLoop, calls=%fused_computation.1 | loop fusion | flops 2088960 | bytes 25600 | tf_op jit(solution)/shard_map/reduce_and | solution.py:275
  13.4 2.4 %all-to-all-done.1.rest_0_ = bf16[4,2,128,256]{3,2,1,0:T(8,128)(2,1)} async-done(((bf16[4,2,128,256]{3,2,1,0:T(8,128)(2,1)}), bf16[4,2,128,256]{3,2,1,0:T(8,128)(2,1)}, u32[]{:S(2)}, u32[]{:S(2)}) %all-to-all-start.1) | async-done | bytes 524320 | tf_op jit(solution)/shard_map/all_to_all | solution.py:210
  15.7 3.5 %all-to-all-start = ((bf16[4,128,1024]{2,1,0:T(8,128)(2,1)}), bf16[4,128,1024]{2,1,0:T(8,128)(2,1)S(1)}, u32[]{:S(2)}, u32[]{:S(2)}) async-start(bf16[4,128,1024]{2,1,0:T(8,128)(2,1)} %bitcast.6), calls=%async_computation | async-start | bytes 2097152 | tf_op jit(solution)/shard_map/all_to_all | solution.py:217
  19.3 5.1 %collective-permute-start = (bf16[4,2,128,256]{3,2,1,0:T(8,128)(2,1)}, bf16[4,2,128,256]{3,2,1,0:T(8,128)(2,1)}, u32[]{:S(2)}, u32[]{:S(2)}) collective-permute-start(bf16[4,2,128,256]{3,2,1,0:T(8,128)(2,1)} %all-to-all-done.1.rest_0_), channel_id=1, source_target_pairs={{0,8},{4,12},{8,16},{12,20},{16,24},{20,28},{1,9},{5,13},{9,17},{1... | collective-permute-start | bytes 1572872 | tf_op jit(solution)/shard_map/ppermute | solution.py:240
  24.4 0.1 select_select_fusion
  24.4 11.2 %collective-permute-done.rest_0_ = bf16[4,2,128,256]{3,2,1,0:T(8,128)(2,1)} collective-permute-done((bf16[4,2,128,256]{3,2,1,0:T(8,128)(2,1)}, bf16[4,2,128,256]{3,2,1,0:T(8,128)(2,1)}, u32[]{:S(2)}, u32[]{:S(2)}) %collective-permute-start) | collective-permute-done | bytes 524320 | tf_op jit(solution)/shard_map/ppermute | solution.py:240
  35.7 5.2 %collective-permute-start.1 = (bf16[4,2,128,256]{3,2,1,0:T(8,128)(2,1)}, bf16[4,2,128,256]{3,2,1,0:T(8,128)(2,1)}, u32[]{:S(2)}, u32[]{:S(2)}) collective-permute-start(bf16[4,2,128,256]{3,2,1,0:T(8,128)(2,1)} %collective-permute-done.rest_0_), channel_id=1, source_target_pairs={{0,8},{4,12},{8,16},{12,20},{16,24},{20,28},{1,9},{5,13},{9,17},{1... | collective-permute-start | bytes 1572872 | tf_op jit(solution)/shard_map/ppermute | solution.py:240
  40.8 1.4 %and_convert_fusion = (bf16[2,16,64,128]{3,2,1,0:T(8,128)(2,1)S(1)}, bf16[2,16,64,128]{3,2,1,0:T(8,128)(2,1)S(1)}, bf16[2,16,64,128]{3,2,1,0:T(8,128)(2,1)S(1)}, bf16[2,16,64,128]{3,2,1,0:T(8,128)(2,1)S(1)}) fusion(pred[2,16,64]{2,1,0:T(8,128)(4,1)S(1)} %get-tuple-element.21, pred[128]{0:T(512)(128)(4,1)S(1)} %iota_compare_fusion, ...), kind=kLoop, calls=%fused_computation | loop fusion | flops 2097152 | bytes 2105472 | tf_op jit(solution)/shard_map/convert_element_type | solution.py:277
  42.3 1.6 %collective-permute-start.6 = (bf16[4,2,128,256]{3,2,1,0:T(8,128)(2,1)}, bf16[4,2,128,256]{3,2,1,0:T(8,128)(2,1)}, u32[]{:S(2)}, u32[]{:S(2)}) collective-permute-start(bf16[4,2,128,256]{3,2,1,0:T(8,128)(2,1)} %all-to-all-done.1.rest_0_), channel_id=1, source_target_pairs={{0,4},{4,0},{8,12},{12,8},{16,20},{20,16},{24,28},{28,24},{1,5},{5... | collective-permute-start | bytes 1572872 | tf_op jit(solution)/shard_map/ppermute | solution.py:241
  43.8 7.5 %collective-permute-done.1.rest_0_ = bf16[4,2,128,256]{3,2,1,0:T(8,128)(2,1)} collective-permute-done((bf16[4,2,128,256]{3,2,1,0:T(8,128)(2,1)}, bf16[4,2,128,256]{3,2,1,0:T(8,128)(2,1)}, u32[]{:S(2)}, u32[]{:S(2)}) %collective-permute-start.1) | collective-permute-done | bytes 524320 | tf_op jit(solution)/shard_map/ppermute | solution.py:240
  51.4 5.2 %collective-permute-start.2 = (bf16[4,2,128,256]{3,2,1,0:T(8,128)(2,1)}, bf16[4,2,128,256]{3,2,1,0:T(8,128)(2,1)}, u32[]{:S(2)}, u32[]{:S(2)}) collective-permute-start(bf16[4,2,128,256]{3,2,1,0:T(8,128)(2,1)} %collective-permute-done.1.rest_0_), channel_id=1, source_target_pairs={{0,8},{4,12},{8,16},{12,20},{16,24},{20,28},{1,9},{5,13},{9,17},{1... | collective-permute-start | bytes 1572872 | tf_op jit(solution)/shard_map/ppermute | solution.py:240
  56.5 1.5 %collective-permute-start.5 = (bf16[4,2,128,256]{3,2,1,0:T(8,128)(2,1)}, bf16[4,2,128,256]{3,2,1,0:T(8,128)(2,1)}, u32[]{:S(2)}, u32[]{:S(2)}) collective-permute-start(bf16[4,2,128,256]{3,2,1,0:T(8,128)(2,1)} %collective-permute-done.rest_0_), channel_id=1, source_target_pairs={{0,4},{4,0},{8,12},{12,8},{16,20},{20,16},{24,28},{28,24},{1,5},{5... | collective-permute-start | bytes 1572872 | tf_op jit(solution)/shard_map/ppermute | solution.py:241
  58.0 0.1 select_n.165.code_ref
  58.1 0.1 select_n.159.code_ref
  58.2 0.1 select_n.153.code_ref
  58.3 0.5 collective-permute-start.4
  58.8 0.1 select_n.147.code_ref
  58.9 7.3 %collective-permute-done.2.rest_0_ = bf16[4,2,128,256]{3,2,1,0:T(8,128)(2,1)} collective-permute-done((bf16[4,2,128,256]{3,2,1,0:T(8,128)(2,1)}, bf16[4,2,128,256]{3,2,1,0:T(8,128)(2,1)}, u32[]{:S(2)}, u32[]{:S(2)}) %collective-permute-start.2) | collective-permute-done | bytes 524320 | tf_op jit(solution)/shard_map/ppermute | solution.py:240
  66.2 1.5 %collective-permute-start.3 = (bf16[4,2,128,256]{3,2,1,0:T(8,128)(2,1)}, bf16[4,2,128,256]{3,2,1,0:T(8,128)(2,1)}, u32[]{:S(2)}, u32[]{:S(2)}) collective-permute-start(bf16[4,2,128,256]{3,2,1,0:T(8,128)(2,1)} %collective-permute-done.2.rest_0_), channel_id=1, source_target_pairs={{0,4},{4,0},{8,12},{12,8},{16,20},{20,16},{24,28},{28,24},{1,5},{5... | collective-permute-start | bytes 1572872 | tf_op jit(solution)/shard_map/ppermute | solution.py:241
  67.7 0.0 all-to-all-done.q_ref
  67.7 0.0 collective-permute-done.6.rest_1_
  67.7 8.2 %shard_map.56 = (f32[16,128,256]{2,1,0:T(8,128)S(1)}, f32[16,16,256]{2,1,0:T(8,128)S(1)}) custom-call(s32[256]{0:T(256)S(1)} %select_n.165.code_ref, bf16[4,128,1024]{2,1,0:T(8,128)(2,1)S(1)} %all-to-all-done.q_ref, bf16[2,16,64,128]{3,2,1,0:T(8,128)(2,1)S(1)} %get-tuple-element.31.pick_ref, bf16[4,2,128,256]{3,2,1,0:T(8,128)(2,1)} %all-to-all-done.1.rest_0_, ...), custom_call_target="tpu_custom_call" | custom-call | flops 2147483648 | bytes 8388608 | tf_op jit(solution)/shard_map/pallas_call | solution.py:163
  75.9 0.0 collective-permute-done.5.rest_1_
  75.9 8.1 %shard_map.57 = (f32[16,128,256]{2,1,0:T(8,128)S(1)}, f32[16,16,256]{2,1,0:T(8,128)S(1)}) custom-call(s32[256]{0:T(256)S(1)} %select_n.159.code_ref, bf16[4,128,1024]{2,1,0:T(8,128)(2,1)S(1)} %all-to-all-done.q_ref, bf16[2,16,64,128]{3,2,1,0:T(8,128)(2,1)S(1)} %get-tuple-element.33.pick_ref, bf16[4,2,128,256]{3,2,1,0:T(8,128)(2,1)} %collective-permute-done.rest_0_, ...), custom_call_target="tpu_custom_call" | custom-call | flops 2147483648 | bytes 8388608 | tf_op jit(solution)/shard_map/pallas_call | solution.py:163
  84.1 0.0 collective-permute-done.4.rest_1_
  84.1 8.1 %shard_map.58 = (f32[16,128,256]{2,1,0:T(8,128)S(1)}, f32[16,16,256]{2,1,0:T(8,128)S(1)}) custom-call(s32[256]{0:T(256)S(1)} %select_n.153.code_ref, bf16[4,128,1024]{2,1,0:T(8,128)(2,1)S(1)} %all-to-all-done.q_ref, bf16[2,16,64,128]{3,2,1,0:T(8,128)(2,1)S(1)} %get-tuple-element.32.pick_ref, bf16[4,2,128,256]{3,2,1,0:T(8,128)(2,1)} %collective-permute-done.1.rest_0_, ...), custom_call_target="tpu_custom_call" | custom-call | flops 2147483648 | bytes 8388608 | tf_op jit(solution)/shard_map/pallas_call | solution.py:163
  92.2 0.0 collective-permute-done.3.rest_1_
  92.2 8.8 %shard_map.59 = bf16[4,128,1024]{2,1,0:T(8,128)(2,1)S(1)} custom-call(s32[256]{0:T(256)S(1)} %select_n.147.code_ref, bf16[4,128,1024]{2,1,0:T(8,128)(2,1)S(1)} %all-to-all-done.q_ref, bf16[2,16,64,128]{3,2,1,0:T(8,128)(2,1)S(1)} %get-tuple-element.34.pick_ref, bf16[4,2,128,256]{3,2,1,0:T(8,128)(2,1)} %collective-permute-done.2.rest_0_, ...), custom_call_target="tpu_custom_call" | custom-call | flops 2147483648 | bytes 8388608 | tf_op jit(solution)/shard_map/pallas_call | solution.py:163
  101.0 16.9 %all_to_all.15 = bf16[4,128,1024]{2,1,0:T(8,128)(2,1)S(1)} all-to-all(bf16[4,128,1024]{2,1,0:T(8,128)(2,1)S(1)} %shard_map.59), channel_id=1, replica_groups=mesh['chip'=8,'core'=2,'head'=2] {'head','core'}, dimensions={0} | all-to-all | bytes 2097152 | tf_op jit(solution)/shard_map/all_to_all | solution.py:281
  117.9 0.7 copy.16
  118.6 1.3 %copy.17 = bf16[128,4096]{1,0:T(8,128)(2,1)} copy(bf16[128,4096]{0,1:T(8,128)(2,1)S(1)} %bitcast.12) | data formatting | bytes 2097152 | tf_op jit(solution)/shard_map/reshape | solution.py:282
  (20 shorter events, 0.1 us)
Async XLA Ops:
  0.0 6.9 %copy-start = (s32[4,64,40]{1,2,0:T(8,128)S(1)}, s32[4,64,40]{1,2,0:T(8,128)}, u32[]{:S(2)}) copy-start(s32[4,64,40]{1,2,0:T(8,128)} %param.9) | copy-start | bytes 122884
  0.0 8.4 %copy-start.2 = (s32[4,128]{1,0:T(4,128)S(1)}, s32[4,128]{1,0:T(4,128)}, u32[]{:S(2)}) copy-start(s32[4,128]{1,0:T(4,128)} %param.8) | copy-start | bytes 6148
  0.0 8.4 %copy-start.1 = (bf16[128,4096]{1,0:T(8,128)(2,1)S(1)}, bf16[128,4096]{1,0:T(8,128)(2,1)}, u32[]{:S(2)}) copy-start(bf16[128,4096]{1,0:T(8,128)(2,1)} %param.5) | copy-start | bytes 3145732
  2.0 13.7 %all-to-all-start.1 = ((bf16[4,2,128,256]{3,2,1,0:T(8,128)(2,1)}), bf16[4,2,128,256]{3,2,1,0:T(8,128)(2,1)}, u32[]{:S(2)}, u32[]{:S(2)}) async-start(bf16[4,2,128,256]{3,2,1,0:T(8,128)(2,1)} %bitcast.14), calls=%async_computation.1 | async-start | bytes 1048576 | tf_op jit(solution)/shard_map/all_to_all | solution.py:210
  15.7 51.9 %all-to-all-start = ((bf16[4,128,1024]{2,1,0:T(8,128)(2,1)}), bf16[4,128,1024]{2,1,0:T(8,128)(2,1)S(1)}, u32[]{:S(2)}, u32[]{:S(2)}) async-start(bf16[4,128,1024]{2,1,0:T(8,128)(2,1)} %bitcast.6), calls=%async_computation | async-start | bytes 2097152 | tf_op jit(solution)/shard_map/all_to_all | solution.py:217
  19.3 16.4 %collective-permute-start = (bf16[4,2,128,256]{3,2,1,0:T(8,128)(2,1)}, bf16[4,2,128,256]{3,2,1,0:T(8,128)(2,1)}, u32[]{:S(2)}, u32[]{:S(2)}) collective-permute-start(bf16[4,2,128,256]{3,2,1,0:T(8,128)(2,1)} %all-to-all-done.1.rest_0_), channel_id=1, source_target_pairs={{0,8},{4,12},{8,16},{12,20},{16,24},{20,28},{1,9},{5,13},{9,17},{1... | collective-permute-start | bytes 1572872 | tf_op jit(solution)/shard_map/ppermute | solution.py:240
  35.7 15.7 %collective-permute-start.1 = (bf16[4,2,128,256]{3,2,1,0:T(8,128)(2,1)}, bf16[4,2,128,256]{3,2,1,0:T(8,128)(2,1)}, u32[]{:S(2)}, u32[]{:S(2)}) collective-permute-start(bf16[4,2,128,256]{3,2,1,0:T(8,128)(2,1)} %collective-permute-done.rest_0_), channel_id=1, source_target_pairs={{0,8},{4,12},{8,16},{12,20},{16,24},{20,28},{1,9},{5,13},{9,17},{1... | collective-permute-start | bytes 1572872 | tf_op jit(solution)/shard_map/ppermute | solution.py:240
  42.3 25.4 %collective-permute-start.6 = (bf16[4,2,128,256]{3,2,1,0:T(8,128)(2,1)}, bf16[4,2,128,256]{3,2,1,0:T(8,128)(2,1)}, u32[]{:S(2)}, u32[]{:S(2)}) collective-permute-start(bf16[4,2,128,256]{3,2,1,0:T(8,128)(2,1)} %all-to-all-done.1.rest_0_), channel_id=1, source_target_pairs={{0,4},{4,0},{8,12},{12,8},{16,20},{20,16},{24,28},{28,24},{1,5},{5... | collective-permute-start | bytes 1572872 | tf_op jit(solution)/shard_map/ppermute | solution.py:241
  51.4 14.8 %collective-permute-start.2 = (bf16[4,2,128,256]{3,2,1,0:T(8,128)(2,1)}, bf16[4,2,128,256]{3,2,1,0:T(8,128)(2,1)}, u32[]{:S(2)}, u32[]{:S(2)}) collective-permute-start(bf16[4,2,128,256]{3,2,1,0:T(8,128)(2,1)} %collective-permute-done.1.rest_0_), channel_id=1, source_target_pairs={{0,8},{4,12},{8,16},{12,20},{16,24},{20,28},{1,9},{5,13},{9,17},{1... | collective-permute-start | bytes 1572872 | tf_op jit(solution)/shard_map/ppermute | solution.py:240
  56.5 19.4 %collective-permute-start.5 = (bf16[4,2,128,256]{3,2,1,0:T(8,128)(2,1)}, bf16[4,2,128,256]{3,2,1,0:T(8,128)(2,1)}, u32[]{:S(2)}, u32[]{:S(2)}) collective-permute-start(bf16[4,2,128,256]{3,2,1,0:T(8,128)(2,1)} %collective-permute-done.rest_0_), channel_id=1, source_target_pairs={{0,4},{4,0},{8,12},{12,8},{16,20},{20,16},{24,28},{28,24},{1,5},{5... | collective-permute-start | bytes 1572872 | tf_op jit(solution)/shard_map/ppermute | solution.py:241
  58.3 25.8 %collective-permute-start.4 = (bf16[4,2,128,256]{3,2,1,0:T(8,128)(2,1)}, bf16[4,2,128,256]{3,2,1,0:T(8,128)(2,1)}, u32[]{:S(2)}, u32[]{:S(2)}) collective-permute-start(bf16[4,2,128,256]{3,2,1,0:T(8,128)(2,1)} %collective-permute-done.1.rest_0_), channel_id=1, source_target_pairs={{0,4},{4,0},{8,12},{12,8},{16,20},{20,16},{24,28},{28,24},{1,5},{5... | collective-permute-start | bytes 1572872 | tf_op jit(solution)/shard_map/ppermute | solution.py:241
  66.2 26.1 %collective-permute-start.3 = (bf16[4,2,128,256]{3,2,1,0:T(8,128)(2,1)}, bf16[4,2,128,256]{3,2,1,0:T(8,128)(2,1)}, u32[]{:S(2)}, u32[]{:S(2)}) collective-permute-start(bf16[4,2,128,256]{3,2,1,0:T(8,128)(2,1)} %collective-permute-done.2.rest_0_), channel_id=1, source_target_pairs={{0,4},{4,0},{8,12},{12,8},{16,20},{20,16},{24,28},{28,24},{1,5},{5... | collective-permute-start | bytes 1572872 | tf_op jit(solution)/shard_map/ppermute | solution.py:241

commit v3 on v2

v3 whole, which is shorter than its diff:
```python
import functools
import math

import jax
import jax.numpy as jnp
from jax import lax
from jax.experimental import pallas as pl
from jax.experimental.pallas import tpu as pltpu
from jax.sharding import Mesh, PartitionSpec as P

BLK = 64
BIG = 1.0e30
LIVE, DEAD, OWN, PICKED = 0, 1, 2, 3
BF16, F32 = jnp.bfloat16, jnp.float32


def arrange_kernel(k_ref, v_ref, o_ref):
    width = v_ref.shape[0]
    head_dim = o_ref.shape[2] - width
    for h in range(o_ref.shape[0]):
        o_ref[h, :, :head_dim] = k_ref[:, h * head_dim : (h + 1) * head_dim]
        o_ref[h, :, head_dim:] = v_ref[:, h * head_dim : (h + 1) * head_dim].T


def arrange(keys, values, heads):
    tok, width = keys.shape
    head_dim = width // heads
    return pl.pallas_call(
        arrange_kernel,
        out_shape=jax.ShapeDtypeStruct((heads, tok, head_dim + tok), BF16),
    )(keys, values)


def step_kernel(code_ref, q_ref, pick_ref, *rest, parts, first, last, span, head_dim, group):
    part_refs, rest = rest[:parts], rest[parts:]
    if not first:
        (acc_in, stat_in, _), rest = rest[:3], rest[3:]
    if last:
        out_ref, rest = rest[0], rest[1:]
    else:
        (acc_out, stat_out, mark_out), rest = rest[:3], rest[3:]
        mark_out[...] = jnp.zeros(mark_out.shape, BF16)
    qext, etile, score_a, score_b = rest
    rows = BLK * group
    chunks, _, wide, _ = part_refs[0].shape
    per_part = chunks * wide // BLK
    slots = parts * per_part
    size = per_part * BLK
    per_q = q_ref.shape[1] // BLK
    blocks_here = q_ref.shape[0] * per_q
    scale = math.log2(math.e) / math.sqrt(head_dim)

    token = lax.rem(lax.broadcasted_iota(jnp.int32, (rows, head_dim), 0), BLK)
    column = lax.broadcasted_iota(jnp.int32, (rows, head_dim), 1)
    masked = ((column < BLK) & (column > token)) | (column == BLK)
    qext[...] = jnp.where(masked, -BIG, 0.0).astype(BF16)
    key_iota = lax.broadcasted_iota(jnp.int32, (BLK, head_dim), 0)
    lane = lax.broadcasted_iota(jnp.int32, (BLK, head_dim), 1)
    etile[LIVE] = jnp.zeros((BLK, head_dim), BF16)
    etile[DEAD] = jnp.where(lane == BLK, 1.0, 0.0).astype(BF16)
    etile[OWN] = jnp.where(lane == key_iota, 1.0, 0.0).astype(BF16)

    def place(here, g):
        start = pl.multiple_of(lax.rem(here, per_q) * BLK, BLK)
        return lax.div(here, per_q), pl.ds(start, BLK), pl.ds(g * head_dim, head_dim)

    def scored(head, here, buffer):
        query = jnp.concatenate(
            [q_ref[place(here, head * group + g)] for g in range(group)], axis=0
        )
        query = jnp.concatenate([query, qext[...]], axis=1)
        top = jnp.full((8, rows), -jnp.inf, F32)
        for p, part in enumerate(part_refs):
            left = [part[c, head, :, pl.ds(0, head_dim)] for c in range(chunks)]
            right = [
                etile[code_ref[head, here, p * per_part + i]] for i in range(per_part)
            ]
            key = jnp.concatenate(
                [jnp.concatenate(left, axis=0), jnp.concatenate(right, axis=0)], axis=1
            )
            tile = lax.dot_general(
                key, query, (((1,), (1,)), ((), ())), preferred_element_type=F32
            )
            buffer[pl.ds(p * size, size), :] = tile
            top = jnp.maximum(top, jnp.max(tile.reshape(size // 8, 8, rows), axis=0))
        return jnp.max(top, axis=0, keepdims=True)

    def mixed_in(head, here, buffer, top):
        at = head * blocks_here + here
        if first:
            top = jnp.broadcast_to(top, (8, rows))
            weight = jnp.zeros((8, rows), F32)
        else:
            before = stat_in[at, :8]
            top = jnp.maximum(top, before)
            fade = jnp.exp2((before - top) * scale)
            weight = stat_in[at, 8:] * fade
        mixed = jnp.zeros((head_dim, rows), F32)
        for p, part in enumerate(part_refs):
            tile = buffer[pl.ds(p * size, size), :].reshape(size // 8, 8, rows)
            expo = jnp.exp2((tile - top[None]) * scale)
            weight = weight + jnp.sum(expo, axis=0)
            value = jnp.concatenate(
                [part[c, head, :, pl.ds(head_dim, wide)] for c in range(chunks)], axis=1
            )
            mixed = mixed + jnp.dot(
                value, expo.reshape(size, rows).astype(BF16), preferred_element_type=F32
            )
        if not first:
            mixed = mixed + acc_in[at] * fade[:1]
        if not last:
            acc_out[at] = mixed
            stat_out[at, :8] = top
            stat_out[at, 8:] = weight
            return
        result = (mixed / jnp.sum(weight, axis=0, keepdims=True)).T.astype(BF16)
        for g in range(group):
            out_ref[place(here, (head - span[0]) * group + g)] = result[g * BLK : (g + 1) * BLK]

    for head in range(*span):
        for slot in range(slots):
            etile[PICKED + slot] = pick_ref[head, slot]

        @pl.loop(0, blocks_here // 2)
        def _(step):
            top_a = scored(head, 2 * step, score_a)
            top_b = scored(head, 2 * step + 1, score_b)
            mixed_in(head, 2 * step, score_a, top_a)
            mixed_in(head, 2 * step + 1, score_b, top_b)


def attend_step(code, query, pick, parts, state, span, last, head_dim, group):
    heads, slots = pick.shape[:2]
    blocks_here = query.shape[0] * query.shape[1] // BLK
    rows = BLK * group
    smem = pl.BlockSpec(memory_space=pltpu.SMEM)
    vmem = pl.BlockSpec(memory_space=pltpu.VMEM)
    carried = (
        jax.ShapeDtypeStruct((heads * blocks_here, head_dim, rows), F32),
        jax.ShapeDtypeStruct((heads * blocks_here, 16, rows), F32),
        jax.ShapeDtypeStruct((16, 128), BF16),
    )
    count = span[1] - span[0]
    out = jax.ShapeDtypeStruct(query.shape[:2] + (count * group * head_dim,), BF16)
    first = state is None
    state = () if first else tuple(state)
    work = count * blocks_here * rows * slots * BLK
    return pl.pallas_call(
        functools.partial(
            step_kernel,
            parts=len(parts),
            first=first,
            last=last,
            span=span,
            head_dim=head_dim,
            group=group,
        ),
        out_shape=out if last else carried,
        in_specs=[smem] + [vmem] * (2 + len(parts) + len(state)),
        out_specs=vmem if last else (vmem,) * 3,
        scratch_shapes=[
            pltpu.VMEM((rows, head_dim), BF16),
            pltpu.VMEM((PICKED + slots, BLK, head_dim), BF16),
            pltpu.VMEM((slots * BLK, rows), F32),
            pltpu.VMEM((slots * BLK, rows), F32),
        ],
        compiler_params=pltpu.CompilerParams(vmem_limit_bytes=16 << 20),
        cost_estimate=pl.CostEstimate(
            flops=4 * work * head_dim, transcendentals=work, bytes_accessed=8 << 20
        ),
    )(code, query, pick, *parts, *state)


def body(queries, keys, values, vertical, slash, *, cores, chips, heads):
    tok, q_width = queries.shape
    all_heads = vertical.shape[0] * heads
    head_dim = keys.shape[1] // all_heads
    group = q_width // keys.shape[1]
    ways = cores * heads
    mine = all_heads // ways
    axes = ("head", "core") if cores > 1 else ("head",)
    groups = chips if cores > 1 else chips * 2
    per_group = tok * ways // BLK
    chip = lax.axis_index("chip")
    if cores == 1:
        chip = chip * 2 + lax.axis_index("core")
    relative = cores > 1 and chips == 8
    swap = functools.partial(
        lax.all_to_all, axis_name=axes, split_axis=0, concat_axis=0, tiled=True
    )

    if relative:
        pair = swap(arrange(keys, values, all_heads).reshape(ways, mine, tok, head_dim + tok))
    else:
        pair = jnp.concatenate(
            [keys.reshape(tok, ways, mine, head_dim), values.reshape(tok, ways, mine, head_dim)],
            axis=3,
        )
        pair = swap(pair.transpose(1, 2, 0, 3))
    query = swap(queries.reshape(tok, ways, q_width // ways).transpose(1, 0, 2))
    query = query.reshape(-1, max(tok, BLK), q_width // ways)

    pair, vertical, slash = lax.optimization_barrier((pair, vertical, slash))

    along = tok // BLK
    local = jnp.arange(per_group, dtype=jnp.int32)
    if cores > 1:
        local = local.reshape(cores, heads, along).swapaxes(0, 1).reshape(-1)
    first_head = lax.axis_index("core") * mine if cores > 1 else 0
    slash = lax.dynamic_slice_in_dim(slash, first_head, mine, axis=0)
    vertical = lax.dynamic_slice_in_dim(vertical, first_head, mine, axis=0)
    lists = lax.dynamic_slice_in_dim(slash, chip * per_group, per_group, axis=1)
    if cores > 1:
        lists = (
            lists.reshape(mine, cores, heads, along, -1).swapaxes(1, 2).reshape(lists.shape)
        )
    ids = chip * per_group + local

    def masks(source):
        nat = (source[:, None] * per_group + local).reshape(-1)
        listed = jnp.any(lists[:, :, :, None] == nat, axis=2)
        slot = PICKED + jnp.arange(nat.shape[0], dtype=jnp.int32)
        code = jnp.where(
            listed,
            LIVE,
            jnp.where(nat == ids[:, None], OWN, jnp.where(nat > ids[:, None], DEAD, slot)),
        )
        position = nat[:, None] * BLK + jnp.arange(BLK, dtype=jnp.int32)
        hidden = jnp.all(vertical[:, None, None, :] != position[..., None], axis=3)
        lane = jnp.arange(head_dim, dtype=jnp.int32) == BLK
        return code, (hidden[..., None] & lane).astype(BF16)

    def attend(table, parts, state, last):
        state = None if state is None else tuple(state)
        run = functools.partial(attend_step, table[0], query, table[1], parts, state)
        if not last:
            return run((0, mine), False, head_dim, group)
        return run((0, mine), True, head_dim, group)

    state = None
    if relative:
        across = [(i, i ^ 1) for i in range(chips)]
        up = [(i, i + 2) for i in range(chips - 2)]
        final = chips // 2 - 1
        col = jnp.stack([chip % 2, 1 - chip % 2])
        tables = []
        for n in range(final + 1):
            row = chip // 2 - n
            tables.append(masks(jnp.where(row < 0, groups, 2 * row + col)))
        tables = lax.optimization_barrier(tables)
        part, waiting = pair, None
        for n in range(final + 2):
            fetched = None
            if n <= final:
                if state is not None:
                    part, mark = lax.optimization_barrier((part, state[2]))
                    state = state[:2] + (mark,)
                fetched = (part, lax.ppermute(part, "chip", across))
                part = lax.ppermute(part, "chip", up) if n < final else None
            if n:
                state = attend(tables[n - 1], waiting, state, n > final)
            waiting = fetched
    else:
        axis = "chip" if cores > 1 else ("chip", "core")
        rows = pair.transpose(1, 0, 2, 3).reshape(mine, -1, 2 * head_dim)
        rows = lax.all_gather(rows, axis, axis=1, tiled=True)
        pieces = rows.shape[1] // (2 * BLK)
        turned = rows[..., head_dim:].reshape(mine, pieces, 2 * BLK, head_dim).swapaxes(2, 3)
        rows = rows[..., :head_dim].reshape(mine, pieces, 2 * BLK, head_dim)
        rows = jnp.concatenate([rows, turned], axis=3).swapaxes(0, 1)
        each = per_group // 2
        order = (chip + jnp.arange(groups, dtype=jnp.int32)) % groups
        rows = jnp.roll(rows.reshape((groups, each) + rows.shape[1:]), -chip, axis=0)
        many = math.gcd(groups, 4)
        for g in range(0, groups, many):
            part = rows[g : g + many].reshape((many * each,) + rows.shape[2:])
            state = attend(masks(order[g : g + many]), (part,), state, g + many == groups)

    out = swap(state.reshape(ways, tok, q_width // ways))
    return out.transpose(1, 0, 2).reshape(tok, q_width)


def solution(mesh):
    seq, heads = mesh.shape["seq"], mesh.shape["head"]
    split = Mesh(mesh.devices.reshape(seq // 2, 2, heads), ("chip", "core", "head"))
    spec = P(("chip", "core", "head"), None)

    def run(queries, keys, values, vertical, slash):
        local_heads = vertical.shape[0] // heads
        tok = queries.shape[0] // (seq * heads)
        cores = 2 if local_heads % 2 == 0 and tok % BLK == 0 else 1
        return jax.shard_map(
            functools.partial(body, cores=cores, chips=seq // 2, heads=heads),
            mesh=split,
            in_specs=(spec, spec, spec, P("head", None), P("head", None, None)),
            out_specs=spec,
            check_vma=False,
        )(queries, keys, values, vertical, slash)

    return run
```

time: 120 us -> 110 us (0.917)
  waiting for transfers between devices: 28.4 us -> 20.7 us
  starting transfers between devices: 28.3 us -> 26 us
    ppermute x7, waiting for transfers between devices: 26 us -> 14.1 us  [the longest x3 10.1 us: body(): part = lax.ppermute(part, 'chip', up) if n < final else None]
    all_to_all x1, waiting for transfers between devices: 2.37 us -> 6.61 us  [body(): swap(arrange(keys, values, all_heads).reshape(ways, mine, tok, head_dim +...]
    ppermute x7, starting transfers between devices: 20.5 us -> 18.2 us  [the longest x3 12.2 us: body(): part = lax.ppermute(part, 'chip', up) if n < final else None]
  transfers between devices with their start and end apart: 9 -> 9, of which waited for: 4 -> 6; matrix products, arithmetic and copies ran while one was open for 7% -> 8% of each run, Pallas kernels for 20% -> 23%
where the time goes in v3:
time: 110 us; the launch traced here: 109 us
  Pallas kernels  35 us (32%)
  starting transfers between devices  26 us (24%)
  waiting for transfers between devices  20.7 us (19%)
  blocking collectives  16.9 us (15%)
  other arithmetic  5.99 us (5%)
  local copies, waits for them, and re-layouts  4.48 us (4%)
    pallas_call x4, Pallas kernels, attend_step(): pl.pallas_call(functools.partial(step_kernel, parts=len(parts), first=fir...  33 us
    all_to_all x1, blocking collectives, body(): out = swap(state.reshape(ways, tok, q_width // ways))  16.9 us
    ppermute x3, starting transfers between devices, body(): part = lax.ppermute(part, 'chip', up) if n < final else None  12.2 us
    ppermute x3, waiting for transfers between devices, body(): part = lax.ppermute(part, 'chip', up) if n < final else None  10.1 us
    all_to_all x1, waiting for transfers between devices, body(): swap(arrange(keys, values, all_heads).reshape(ways, mine, tok, head_dim +...  6.61 us
    ppermute x4, starting transfers between devices, body(): fetched = (part, lax.ppermute(part, 'chip', across))  6.03 us
    all_to_all x1, starting transfers between devices, body(): swap(arrange(keys, values, all_heads).reshape(ways, mine, tok, head_dim +...  4.24 us
    ppermute x4, waiting for transfers between devices, body(): fetched = (part, lax.ppermute(part, 'chip', across))  4.01 us
  transfers between devices with their start and end apart: 9, of which 6 were waited for; matrix products, arithmetic and copies ran while one was open for 8% of the time, Pallas kernels for 23%

profile of v3, /device:TPU:0, one launch (start us, length us, event | category | flops | bytes accessed | tf_op | source)
XLA Modules:
  0.0 109.2 jit_solution(18073144203844930374)
XLA Ops:
  0.0 0.0 copy-start
  0.0 0.0 copy-start.1
  0.0 2.0 %shard_map.55 = bf16[8,128,256]{2,1,0:T(8,128)(2,1)} custom-call(bf16[128,1024]{1,0:T(8,128)(2,1)} %k_ref.1, bf16[128,1024]{1,0:T(8,128)(2,1)} %v_ref.1), custom_call_target="tpu_custom_call" | custom-call | tf_op jit(solution)/shard_map/pallas_call | solution.py:28
  2.0 4.2 %all-to-all-start = ((bf16[4,2,128,256]{3,2,1,0:T(8,128)(2,1)}), bf16[4,2,128,256]{3,2,1,0:T(8,128)(2,1)}, u32[]{:S(2)}, u32[]{:S(2)}) async-start(bf16[4,2,128,256]{3,2,1,0:T(8,128)(2,1)} %bitcast.14), calls=%async_computation | async-start | bytes 1048576 | tf_op jit(solution)/shard_map/all_to_all | solution.py:193
  6.3 0.1 reshape.466
  6.4 0.1 fusion
  6.5 0.1 broadcast_add_fusion.3
  6.6 0.1 add.297
  6.6 0.1 add.308
  6.7 0.1 add.316
  6.8 0.1 add.324
  6.9 0.0 copy-done.1
  6.9 0.7 copy.14
  7.6 0.0 copy-start.2
  7.6 1.3 %copy.15 = bf16[128,4,1024]{2,0,1:T(8,128)(2,1)} copy(bf16[128,4,1024]{0,2,1:T(8,128)(2,1)S(1)} %bitcast.13) | data formatting | bytes 2097152 | tf_op jit(solution)/shard_map/reshape | solution.py:200
  8.9 0.1 iota_add_fusion.2
  9.0 0.1 iota_add_fusion
  9.1 0.1 select_select_fusion
  9.1 6.6 %all-to-all-done.rest_0_ = bf16[4,2,128,256]{3,2,1,0:T(8,128)(2,1)} async-done(((bf16[4,2,128,256]{3,2,1,0:T(8,128)(2,1)}), bf16[4,2,128,256]{3,2,1,0:T(8,128)(2,1)}, u32[]{:S(2)}, u32[]{:S(2)}) %all-to-all-start) | async-done | bytes 524320 | tf_op jit(solution)/shard_map/all_to_all | solution.py:193
  15.7 3.5 %all-to-all-start.1 = ((bf16[4,128,1024]{2,1,0:T(8,128)(2,1)}), bf16[4,128,1024]{2,1,0:T(8,128)(2,1)S(1)}, u32[]{:S(2)}, u32[]{:S(2)}) async-start(bf16[4,128,1024]{2,1,0:T(8,128)(2,1)} %bitcast.7), calls=%async_computation.1 | async-start | bytes 2097152 | tf_op jit(solution)/shard_map/all_to_all | solution.py:200
  19.3 2.4 %collective-permute-start.2 = (bf16[4,2,128,256]{3,2,1,0:T(8,128)(2,1)}, bf16[4,2,128,256]{3,2,1,0:T(8,128)(2,1)}, u32[]{:S(2)}, u32[]{:S(2)}) collective-permute-start(bf16[4,2,128,256]{3,2,1,0:T(8,128)(2,1)} %all-to-all-done.rest_0_), channel_id=1, source_target_pairs={{0,4},{4,0},{8,12},{12,8},{16,20},{20,16},{24,28},{28,24},{1,5},{5... | collective-permute-start | bytes 1572872 | tf_op jit(solution)/shard_map/ppermute | solution.py:258
  21.6 4.3 %collective-permute-start = (bf16[4,2,128,256]{3,2,1,0:T(8,128)(2,1)}, bf16[4,2,128,256]{3,2,1,0:T(8,128)(2,1)}, u32[]{:S(2)}, u32[]{:S(2)}) collective-permute-start(bf16[4,2,128,256]{3,2,1,0:T(8,128)(2,1)} %all-to-all-done.rest_0_), channel_id=1, source_target_pairs={{0,8},{4,12},{8,16},{12,20},{16,24},{20,28},{1,9},{5,13},{9,17},{1... | collective-permute-start | bytes 1572872 | tf_op jit(solution)/shard_map/ppermute | solution.py:259
  25.9 0.0 copy-done.2
  25.9 0.1 copy.12
  26.0 1.2 %compare_reduce_fusion.4 = (pred[2,8,16]{2,1,0:T(8,128)(4,1)S(1)}, pred[2,8,16]{2,1,0:T(8,128)(4,1)S(1)}, pred[2,8,16]{2,1,0:T(8,128)(4,1)S(1)}, pred[2,8,16]{2,1,0:T(8,128)(4,1)S(1)}) fusion(s32[2,8,40]{2,1,0:T(8,128)S(1)} %bitcast.15, s32[16]{0:T(128)S(1)} %add.324, s32[16]{0:T(128)S(1)} %add.308, s32[16]{0:T(128)S(1)} %add.316, s32[16]{0:T(128)S(1)} %add.297), kind=kLoop, calls=%fused_computation.8 | loop fusion | flops 80896 | bytes 3840 | tf_op jit(solution)/shard_map/reduce_or | solution.py:221
  27.3 0.0 copy-done
  27.3 9.6 %collective-permute-done.rest_0_ = bf16[4,2,128,256]{3,2,1,0:T(8,128)(2,1)} collective-permute-done((bf16[4,2,128,256]{3,2,1,0:T(8,128)(2,1)}, bf16[4,2,128,256]{3,2,1,0:T(8,128)(2,1)}, u32[]{:S(2)}, u32[]{:S(2)}) %collective-permute-start) | collective-permute-done | bytes 524320 | tf_op jit(solution)/shard_map/ppermute | solution.py:259
  36.9 5.2 %collective-permute-start.1 = (bf16[4,2,128,256]{3,2,1,0:T(8,128)(2,1)}, bf16[4,2,128,256]{3,2,1,0:T(8,128)(2,1)}, u32[]{:S(2)}, u32[]{:S(2)}) collective-permute-start(bf16[4,2,128,256]{3,2,1,0:T(8,128)(2,1)} %collective-permute-done.rest_0_), channel_id=1, source_target_pairs={{0,8},{4,12},{8,16},{12,20},{16,24},{20,28},{1,9},{5,13},{9,17},{1... | collective-permute-start | bytes 1572872 | tf_op jit(solution)/shard_map/ppermute | solution.py:259
  42.1 2.9 %compare_reduce_fusion = (pred[2,16,64]{2,1,0:T(8,128)(4,1)S(1)}, pred[2,16,64]{2,1,0:T(8,128)(4,1)S(1)}, pred[2,16,64]{2,1,0:T(8,128)(4,1)S(1)}, pred[2,16,64]{2,1,0:T(8,128)(4,1)S(1)}) fusion(s32[16,64]{1,0:T(8,128)S(1)} %get-tuple-element.82, s32[2,128]{1,0:T(2,128)S(1)} %constant_dynamic-slice_fusion, s32[16,64]{1,0:T(8,128)S(1)} %get-tuple-element.84, ...), kind=kLoop, calls=%fused_computation.1 | loop fusion | flops 2088960 | bytes 25600 | tf_op jit(solution)/shard_map/reduce_and | solution.py:229
  45.0 1.4 %and_convert_fusion = (bf16[2,16,64,128]{3,2,1,0:T(8,128)(2,1)S(1)}, bf16[2,16,64,128]{3,2,1,0:T(8,128)(2,1)S(1)}, bf16[2,16,64,128]{3,2,1,0:T(8,128)(2,1)S(1)}, bf16[2,16,64,128]{3,2,1,0:T(8,128)(2,1)S(1)}) fusion(pred[2,16,64]{2,1,0:T(8,128)(4,1)S(1)} %get-tuple-element.57, pred[128]{0:T(512)(128)(4,1)S(1)} %iota_compare_fusion, ...), kind=kLoop, calls=%fused_computation | loop fusion | flops 2097152 | bytes 2105472 | tf_op jit(solution)/shard_map/convert_element_type | solution.py:231
  46.4 0.6 collective-permute-start.4
  47.0 0.0 all-to-all-done.1.q_ref
  47.0 0.0 collective-permute-done.2.rest_1_
  47.0 8.3 %shard_map.56 = (f32[16,128,256]{2,1,0:T(8,128)S(1)}, f32[16,16,256]{2,1,0:T(8,128)S(1)}, bf16[16,128]{1,0:T(8,128)(2,1)S(1)}) custom-call(s32[2,8,16]{2,1,0:T(8,128)S(1)} %get-tuple-element.34.code_ref, bf16[4,128,1024]{2,1,0:T(8,128)(2,1)S(1)} %all-to-all-done.1.q_ref, bf16[2,16,64,128]{3,2,1,0:T(8,128)(2,1)S(1)} %get-tuple-element.35.pick_ref, ...), custom_call_target="tpu_custom_call" | custom-call | flops 2147483648 | bytes 8388608 | tf_op jit(solution)/shard_map/pallas_call | solution.py:148
  55.4 0.0 collective-permute-done.1.rest_0_
  55.4 2.7 %collective-permute-start.3 = (bf16[4,2,128,256]{3,2,1,0:T(8,128)(2,1)}, bf16[4,2,128,256]{3,2,1,0:T(8,128)(2,1)S(1)}, u32[]{:S(2)}, u32[]{:S(2)}) collective-permute-start(bf16[4,2,128,256]{3,2,1,0:T(8,128)(2,1)} %collective-permute-done.1.rest_0_), channel_id=1, source_target_pairs={{0,8},{4,12},{8,16},{12,20},{16,24},{20,28},{1,9},{5,13},{9,17},{1... | collective-permute-start | bytes 1572872 | tf_op jit(solution)/shard_map/ppermute | solution.py:259
  58.1 1.5 %collective-permute-start.6 = (bf16[4,2,128,256]{3,2,1,0:T(8,128)(2,1)}, bf16[4,2,128,256]{3,2,1,0:T(8,128)(2,1)S(1)}, u32[]{:S(2)}, u32[]{:S(2)}) collective-permute-start(bf16[4,2,128,256]{3,2,1,0:T(8,128)(2,1)} %collective-permute-done.1.rest_0_), channel_id=1, source_target_pairs={{0,4},{4,0},{8,12},{12,8},{16,20},{20,16},{24,28},{28,24},{1,5},{5... | collective-permute-start | bytes 1572872 | tf_op jit(solution)/shard_map/ppermute | solution.py:258
  59.7 0.1 collective-permute-done.4.rest_1_
  59.7 8.2 %shard_map.57 = (f32[16,128,256]{2,1,0:T(8,128)S(1)}, f32[16,16,256]{2,1,0:T(8,128)S(1)}, bf16[16,128]{1,0:T(8,128)(2,1)S(1)}) custom-call(s32[2,8,16]{2,1,0:T(8,128)S(1)} %get-tuple-element.38.code_ref, bf16[4,128,1024]{2,1,0:T(8,128)(2,1)S(1)} %all-to-all-done.1.q_ref, bf16[2,16,64,128]{3,2,1,0:T(8,128)(2,1)S(1)} %get-tuple-element.39.pick_ref, ...), custom_call_target="tpu_custom_call" | custom-call | flops 2147483648 | bytes 8388608 | tf_op jit(solution)/shard_map/pallas_call | solution.py:148
  67.9 0.5 collective-permute-done.3.rest_0_
  68.5 1.5 %collective-permute-start.5 = (bf16[4,2,128,256]{3,2,1,0:T(8,128)(2,1)S(1)}, bf16[4,2,128,256]{3,2,1,0:T(8,128)(2,1)S(1)}, u32[]{:S(2)}, u32[]{:S(2)}) collective-permute-start(bf16[4,2,128,256]{3,2,1,0:T(8,128)(2,1)S(1)} %collective-permute-done.3.rest_0_), channel_id=1, source_target_pairs={{0,4},{4,0},{8,12},{12,8},{16,20},{20,16},{24,28},{28,24},{1,5},{5... | collective-permute-start | bytes 1572872 | tf_op jit(solution)/shard_map/ppermute | solution.py:258
  70.0 2.7 %collective-permute-done.6.rest_1_ = bf16[4,2,128,256]{3,2,1,0:T(8,128)(2,1)S(1)} collective-permute-done((bf16[4,2,128,256]{3,2,1,0:T(8,128)(2,1)}, bf16[4,2,128,256]{3,2,1,0:T(8,128)(2,1)S(1)}, u32[]{:S(2)}, u32[]{:S(2)}) %collective-permute-start.6) | collective-permute-done | bytes 524320 | tf_op jit(solution)/shard_map/ppermute | solution.py:258
  72.7 8.1 %shard_map.58 = (f32[16,128,256]{2,1,0:T(8,128)S(1)}, f32[16,16,256]{2,1,0:T(8,128)S(1)}, bf16[16,128]{1,0:T(8,128)(2,1)S(1)}) custom-call(s32[2,8,16]{2,1,0:T(8,128)S(1)} %get-tuple-element.45.code_ref, bf16[4,128,1024]{2,1,0:T(8,128)(2,1)S(1)} %all-to-all-done.1.q_ref, bf16[2,16,64,128]{3,2,1,0:T(8,128)(2,1)S(1)} %get-tuple-element.46.pick_ref, ...), custom_call_target="tpu_custom_call" | custom-call | flops 2147483648 | bytes 8388608 | tf_op jit(solution)/shard_map/pallas_call | solution.py:148
  80.8 1.2 %collective-permute-done.5.rest_1_ = bf16[4,2,128,256]{3,2,1,0:T(8,128)(2,1)S(1)} collective-permute-done((bf16[4,2,128,256]{3,2,1,0:T(8,128)(2,1)S(1)}, bf16[4,2,128,256]{3,2,1,0:T(8,128)(2,1)S(1)}, u32[]{:S(2)}, u32[]{:S(2)}) %collective-permute-start.5) | collective-permute-done | bytes 524320 | tf_op jit(solution)/shard_map/ppermute | solution.py:258
  82.0 8.3 %shard_map.59 = bf16[4,128,1024]{2,1,0:T(8,128)(2,1)S(1)} custom-call(s32[2,8,16]{2,1,0:T(8,128)S(1)} %get-tuple-element.31.code_ref, bf16[4,128,1024]{2,1,0:T(8,128)(2,1)S(1)} %all-to-all-done.1.q_ref, bf16[2,16,64,128]{3,2,1,0:T(8,128)(2,1)S(1)} %get-tuple-element.32.pick_ref, bf16[4,2,128,256]{3,2,1,0:T(8,128)(2,1)S(1)} %collective-permute-done.3.rest_0_, ...), custom_call_target="tpu_custom_call" | custom-call | flops 2147483648 | bytes 8388608 | tf_op jit(solution)/shard_map/pallas_call | solution.py:148
  90.4 16.9 %all_to_all.15 = bf16[4,128,1024]{2,1,0:T(8,128)(2,1)S(1)} all-to-all(bf16[4,128,1024]{2,1,0:T(8,128)(2,1)S(1)} %shard_map.59), channel_id=1, replica_groups=mesh['chip'=8,'core'=2,'head'=2] {'head','core'}, dimensions={0} | all-to-all | bytes 2097152 | tf_op jit(solution)/shard_map/all_to_all | solution.py:279
  107.3 0.7 copy.16
  107.9 1.3 %copy.17 = bf16[128,4096]{1,0:T(8,128)(2,1)} copy(bf16[128,4096]{0,1:T(8,128)(2,1)S(1)} %bitcast.12) | data formatting | bytes 2097152 | tf_op jit(solution)/shard_map/reshape | solution.py:280
  (14 shorter events, 0.1 us)
Async XLA Ops:
  0.0 27.3 %copy-start = (s32[4,128]{1,0:T(4,128)S(1)}, s32[4,128]{1,0:T(4,128)}, u32[]{:S(2)}) copy-start(s32[4,128]{1,0:T(4,128)} %param.8) | copy-start | bytes 6148
  0.0 6.9 %copy-start.1 = (bf16[128,4096]{1,0:T(8,128)(2,1)S(1)}, bf16[128,4096]{1,0:T(8,128)(2,1)}, u32[]{:S(2)}) copy-start(bf16[128,4096]{1,0:T(8,128)(2,1)} %param.5) | copy-start | bytes 3145732
  2.0 13.7 %all-to-all-start = ((bf16[4,2,128,256]{3,2,1,0:T(8,128)(2,1)}), bf16[4,2,128,256]{3,2,1,0:T(8,128)(2,1)}, u32[]{:S(2)}, u32[]{:S(2)}) async-start(bf16[4,2,128,256]{3,2,1,0:T(8,128)(2,1)} %bitcast.14), calls=%async_computation | async-start | bytes 1048576 | tf_op jit(solution)/shard_map/all_to_all | solution.py:193
  7.6 18.3 %copy-start.2 = (s32[4,64,40]{1,2,0:T(8,128)S(1)}, s32[4,64,40]{1,2,0:T(8,128)}, u32[]{:S(2)}) copy-start(s32[4,64,40]{1,2,0:T(8,128)} %param.9) | copy-start | bytes 122884
  15.7 31.3 %all-to-all-start.1 = ((bf16[4,128,1024]{2,1,0:T(8,128)(2,1)}), bf16[4,128,1024]{2,1,0:T(8,128)(2,1)S(1)}, u32[]{:S(2)}, u32[]{:S(2)}) async-start(bf16[4,128,1024]{2,1,0:T(8,128)(2,1)} %bitcast.7), calls=%async_computation.1 | async-start | bytes 2097152 | tf_op jit(solution)/shard_map/all_to_all | solution.py:200
  19.3 27.8 %collective-permute-start.2 = (bf16[4,2,128,256]{3,2,1,0:T(8,128)(2,1)}, bf16[4,2,128,256]{3,2,1,0:T(8,128)(2,1)}, u32[]{:S(2)}, u32[]{:S(2)}) collective-permute-start(bf16[4,2,128,256]{3,2,1,0:T(8,128)(2,1)} %all-to-all-done.rest_0_), channel_id=1, source_target_pairs={{0,4},{4,0},{8,12},{12,8},{16,20},{20,16},{24,28},{28,24},{1,5},{5... | collective-permute-start | bytes 1572872 | tf_op jit(solution)/shard_map/ppermute | solution.py:258
  21.6 15.3 %collective-permute-start = (bf16[4,2,128,256]{3,2,1,0:T(8,128)(2,1)}, bf16[4,2,128,256]{3,2,1,0:T(8,128)(2,1)}, u32[]{:S(2)}, u32[]{:S(2)}) collective-permute-start(bf16[4,2,128,256]{3,2,1,0:T(8,128)(2,1)} %all-to-all-done.rest_0_), channel_id=1, source_target_pairs={{0,8},{4,12},{8,16},{12,20},{16,24},{20,28},{1,9},{5,13},{9,17},{1... | collective-permute-start | bytes 1572872 | tf_op jit(solution)/shard_map/ppermute | solution.py:259
  36.9 18.5 %collective-permute-start.1 = (bf16[4,2,128,256]{3,2,1,0:T(8,128)(2,1)}, bf16[4,2,128,256]{3,2,1,0:T(8,128)(2,1)}, u32[]{:S(2)}, u32[]{:S(2)}) collective-permute-start(bf16[4,2,128,256]{3,2,1,0:T(8,128)(2,1)} %collective-permute-done.rest_0_), channel_id=1, source_target_pairs={{0,8},{4,12},{8,16},{12,20},{16,24},{20,28},{1,9},{5,13},{9,17},{1... | collective-permute-start | bytes 1572872 | tf_op jit(solution)/shard_map/ppermute | solution.py:259
  46.4 13.3 %collective-permute-start.4 = (bf16[4,2,128,256]{3,2,1,0:T(8,128)(2,1)}, bf16[4,2,128,256]{3,2,1,0:T(8,128)(2,1)}, u32[]{:S(2)}, u32[]{:S(2)}) collective-permute-start(bf16[4,2,128,256]{3,2,1,0:T(8,128)(2,1)} %collective-permute-done.rest_0_), channel_id=1, source_target_pairs={{0,4},{4,0},{8,12},{12,8},{16,20},{20,16},{24,28},{28,24},{1,5},{5... | collective-permute-start | bytes 1572872 | tf_op jit(solution)/shard_map/ppermute | solution.py:258
  55.4 13.1 %collective-permute-start.3 = (bf16[4,2,128,256]{3,2,1,0:T(8,128)(2,1)}, bf16[4,2,128,256]{3,2,1,0:T(8,128)(2,1)S(1)}, u32[]{:S(2)}, u32[]{:S(2)}) collective-permute-start(bf16[4,2,128,256]{3,2,1,0:T(8,128)(2,1)} %collective-permute-done.1.rest_0_), channel_id=1, source_target_pairs={{0,8},{4,12},{8,16},{12,20},{16,24},{20,28},{1,9},{5,13},{9,17},{1... | collective-permute-start | bytes 1572872 | tf_op jit(solution)/shard_map/ppermute | solution.py:259
  58.1 14.6 %collective-permute-start.6 = (bf16[4,2,128,256]{3,2,1,0:T(8,128)(2,1)}, bf16[4,2,128,256]{3,2,1,0:T(8,128)(2,1)S(1)}, u32[]{:S(2)}, u32[]{:S(2)}) collective-permute-start(bf16[4,2,128,256]{3,2,1,0:T(8,128)(2,1)} %collective-permute-done.1.rest_0_), channel_id=1, source_target_pairs={{0,4},{4,0},{8,12},{12,8},{16,20},{20,16},{24,28},{28,24},{1,5},{5... | collective-permute-start | bytes 1572872 | tf_op jit(solution)/shard_map/ppermute | solution.py:258
  68.5 13.6 %collective-permute-start.5 = (bf16[4,2,128,256]{3,2,1,0:T(8,128)(2,1)S(1)}, bf16[4,2,128,256]{3,2,1,0:T(8,128)(2,1)S(1)}, u32[]{:S(2)}, u32[]{:S(2)}) collective-permute-start(bf16[4,2,128,256]{3,2,1,0:T(8,128)(2,1)S(1)} %collective-permute-done.3.rest_0_), channel_id=1, source_target_pairs={{0,4},{4,0},{8,12},{12,8},{16,20},{20,16},{24,28},{28,24},{1,5},{5... | collective-permute-start | bytes 1572872 | tf_op jit(solution)/shard_map/ppermute | solution.py:258

commit v4 on v3

--- a/solution.py
+++ b/solution.py
@@ -197,8 +197,7 @@
             axis=3,
         )
         pair = swap(pair.transpose(1, 2, 0, 3))
-    query = swap(queries.reshape(tok, ways, q_width // ways).transpose(1, 0, 2))
-    query = query.reshape(-1, max(tok, BLK), q_width // ways)
+    query = queries.reshape(tok, ways, q_width // ways).transpose(1, 0, 2)
 
     pair, vertical, slash = lax.optimization_barrier((pair, vertical, slash))
 
@@ -230,7 +229,7 @@
         lane = jnp.arange(head_dim, dtype=jnp.int32) == BLK
         return code, (hidden[..., None] & lane).astype(BF16)
 
-    def attend(table, parts, state, last):
+    def attend(query, table, parts, state, last):
         state = None if state is None else tuple(state)
         run = functools.partial(attend_step, table[0], query, table[1], parts, state)
         if not last:
@@ -247,20 +246,25 @@
         for n in range(final + 1):
             row = chip // 2 - n
             tables.append(masks(jnp.where(row < 0, groups, 2 * row + col)))
-        tables = lax.optimization_barrier(tables)
+        code, query = lax.optimization_barrier((tables[0][0], query))
+        tables[0] = (code, tables[0][1])
+        query = swap(query).reshape(-1, max(tok, BLK), q_width // ways)
         part, waiting = pair, None
         for n in range(final + 2):
             fetched = None
             if n <= final:
+                if n == 1:
+                    part, tables = lax.optimization_barrier((part, tables))
                 if state is not None:
                     part, mark = lax.optimization_barrier((part, state[2]))
                     state = state[:2] + (mark,)
                 fetched = (part, lax.ppermute(part, "chip", across))
                 part = lax.ppermute(part, "chip", up) if n < final else None
             if n:
-                state = attend(tables[n - 1], waiting, state, n > final)
+                state = attend(query, tables[n - 1], waiting, state, n > final)
             waiting = fetched
     else:
+        query = swap(query).reshape(-1, max(tok, BLK), q_width // ways)
         axis = "chip" if cores > 1 else ("chip", "core")
         rows = pair.transpose(1, 0, 2, 3).reshape(mine, -1, 2 * head_dim)
         rows = lax.all_gather(rows, axis, axis=1, tiled=True)
@@ -274,7 +278,7 @@
         many = math.gcd(groups, 4)
         for g in range(0, groups, many):
             part = rows[g : g + many].reshape((many * each,) + rows.shape[2:])
-            state = attend(masks(order[g : g + many]), (part,), state, g + many == groups)
+            state = attend(query, masks(order[g : g + many]), (part,), state, g + many == groups)
 
     out = swap(state.reshape(ways, tok, q_width // ways))
     return out.transpose(1, 0, 2).reshape(tok, q_width)

time: 110 us -> 105 us (0.955)
  waiting for transfers between devices: 20.7 us -> 18.2 us
  starting transfers between devices: 26 us -> 23.9 us
    ppermute x3, waiting for transfers between devices: 10.1 us -> 3.42 us  [body(): part = lax.ppermute(part, 'chip', up) if n < final else None]
    all_to_all x1, waiting for transfers between devices: 0.01 us -> 3.46 us  [body(): query = swap(query).reshape(-1, max(tok, BLK), q_width // ways)]
    ppermute x4, starting transfers between devices: 6.03 us -> 4.02 us  [body(): fetched = (part, lax.ppermute(part, 'chip', across))]
  transfers between devices with their start and end apart: 9 -> 9, of which waited for: 6 -> 6; matrix products, arithmetic and copies ran while one was open for 8% -> 8% of each run, Pallas kernels for 23% -> 24%
where the time goes in v4:
time: 105 us
  Pallas kernels  35.1 us (33%)
  starting transfers between devices  23.9 us (23%)
  waiting for transfers between devices  18.2 us (17%)
  blocking collectives  16.9 us (16%)
  other arithmetic  6.01 us (6%)
  local copies, waits for them, and re-layouts  4.47 us (4%)
    pallas_call x4, Pallas kernels, attend_step(): pl.pallas_call(functools.partial(step_kernel, parts=len(parts), first=fir...  33 us
    all_to_all x1, blocking collectives, body(): out = swap(state.reshape(ways, tok, q_width // ways))  16.9 us
    ppermute x3, starting transfers between devices, body(): part = lax.ppermute(part, 'chip', up) if n < final else None  12.1 us
    all_to_all x1, waiting for transfers between devices, body(): swap(arrange(keys, values, all_heads).reshape(ways, mine, tok, head_dim +...  6.59 us
    ppermute x4, waiting for transfers between devices, body(): fetched = (part, lax.ppermute(part, 'chip', across))  4.74 us
    all_to_all x1, starting transfers between devices, body(): swap(arrange(keys, values, all_heads).reshape(ways, mine, tok, head_dim +...  4.24 us
    ppermute x4, starting transfers between devices, body(): fetched = (part, lax.ppermute(part, 'chip', across))  4.02 us
    all_to_all x1, starting transfers between devices, body(): query = swap(query).reshape(-1, max(tok, BLK), q_width // ways)  3.53 us
  transfers between devices with their start and end apart: 9, of which 6 were waited for; matrix products, arithmetic and copies ran while one was open for 8% of the time, Pallas kernels for 24%

profile of v4, /device:TPU:0, one launch (start us, length us, event | category | flops | bytes accessed | tf_op | source)
XLA Modules:
  0.0 104.8 jit_solution(8373219754991967748)
XLA Ops:
  0.0 0.0 copy-start
  0.0 0.0 copy-start.1
  0.0 2.0 %shard_map.55 = bf16[8,128,256]{2,1,0:T(8,128)(2,1)} custom-call(bf16[128,1024]{1,0:T(8,128)(2,1)} %k_ref.1, bf16[128,1024]{1,0:T(8,128)(2,1)} %v_ref.1), custom_call_target="tpu_custom_call" | custom-call | tf_op jit(solution)/shard_map/pallas_call | solution.py:28
  2.0 4.2 %all-to-all-start = ((bf16[4,2,128,256]{3,2,1,0:T(8,128)(2,1)}), bf16[4,2,128,256]{3,2,1,0:T(8,128)(2,1)}, u32[]{:S(2)}, u32[]{:S(2)}) async-start(bf16[4,2,128,256]{3,2,1,0:T(8,128)(2,1)} %bitcast.14), calls=%async_computation | async-start | bytes 1048576 | tf_op jit(solution)/shard_map/all_to_all | solution.py:193
  6.3 0.1 reshape.466
  6.4 0.1 fusion
  6.5 0.1 broadcast_add_fusion.3
  6.6 0.1 add.297
  6.6 0.1 add.308
  6.7 0.1 add.316
  6.8 0.1 add.324
  6.9 0.0 copy-done.1
  6.9 0.0 copy-start.2
  6.9 0.7 copy.14
  7.6 1.3 %copy.15 = bf16[128,4,1024]{2,0,1:T(8,128)(2,1)} copy(bf16[128,4,1024]{0,2,1:T(8,128)(2,1)S(1)} %bitcast.13) | data formatting | bytes 2097152 | tf_op jit(solution)/shard_map/reshape | solution.py:200
  8.9 0.1 iota_add_fusion.2
  9.0 0.1 iota_add_fusion
  9.0 0.1 select_select_fusion
  9.1 6.6 %all-to-all-done.rest_0_ = bf16[4,2,128,256]{3,2,1,0:T(8,128)(2,1)} async-done(((bf16[4,2,128,256]{3,2,1,0:T(8,128)(2,1)}), bf16[4,2,128,256]{3,2,1,0:T(8,128)(2,1)}, u32[]{:S(2)}, u32[]{:S(2)}) %all-to-all-start) | async-done | bytes 524320 | tf_op jit(solution)/shard_map/all_to_all | solution.py:193
  15.7 2.3 %collective-permute-start.2 = (bf16[4,2,128,256]{3,2,1,0:T(8,128)(2,1)}, bf16[4,2,128,256]{3,2,1,0:T(8,128)(2,1)}, u32[]{:S(2)}, u32[]{:S(2)}) collective-permute-start(bf16[4,2,128,256]{3,2,1,0:T(8,128)(2,1)} %all-to-all-done.rest_0_), channel_id=1, source_target_pairs={{0,4},{4,0},{8,12},{12,8},{16,20},{20,16},{24,28},{28,24},{1,5},{5... | collective-permute-start | bytes 1572872 | tf_op jit(solution)/shard_map/ppermute | solution.py:261
  18.0 4.3 %collective-permute-start = (bf16[4,2,128,256]{3,2,1,0:T(8,128)(2,1)}, bf16[4,2,128,256]{3,2,1,0:T(8,128)(2,1)}, u32[]{:S(2)}, u32[]{:S(2)}) collective-permute-start(bf16[4,2,128,256]{3,2,1,0:T(8,128)(2,1)} %all-to-all-done.rest_0_), channel_id=1, source_target_pairs={{0,8},{4,12},{8,16},{12,20},{16,24},{20,28},{1,9},{5,13},{9,17},{1... | collective-permute-start | bytes 1572872 | tf_op jit(solution)/shard_map/ppermute | solution.py:262
  22.3 0.0 copy-done
  22.3 0.0 copy-done.2
  22.3 0.1 copy.12
  22.4 1.2 %compare_reduce_fusion.4 = (pred[2,8,16]{2,1,0:T(8,128)(4,1)S(1)}, pred[2,8,16]{2,1,0:T(8,128)(4,1)S(1)}, pred[2,8,16]{2,1,0:T(8,128)(4,1)S(1)}, pred[2,8,16]{2,1,0:T(8,128)(4,1)S(1)}) fusion(s32[2,8,40]{2,1,0:T(8,128)S(1)} %bitcast.15, s32[16]{0:T(128)S(1)} %add.324, s32[16]{0:T(128)S(1)} %add.308, s32[16]{0:T(128)S(1)} %add.316, s32[16]{0:T(128)S(1)} %add.297), kind=kLoop, calls=%fused_computation.8 | loop fusion | flops 80896 | bytes 3840 | tf_op jit(solution)/shard_map/reduce_or | solution.py:220
  23.7 3.5 %all-to-all-start.1 = ((bf16[4,128,1024]{2,1,0:T(8,128)(2,1)}), bf16[4,128,1024]{2,1,0:T(8,128)(2,1)S(1)}, u32[]{:S(2)}, u32[]{:S(2)}) async-start(bf16[4,128,1024]{2,1,0:T(8,128)(2,1)} %bitcast.7), calls=%async_computation.1 | async-start | bytes 2097152 | tf_op jit(solution)/shard_map/all_to_all | solution.py:251
  27.2 2.9 %compare_reduce_fusion = (pred[2,16,64]{2,1,0:T(8,128)(4,1)S(1)}, pred[2,16,64]{2,1,0:T(8,128)(4,1)S(1)}, pred[2,16,64]{2,1,0:T(8,128)(4,1)S(1)}, pred[2,16,64]{2,1,0:T(8,128)(4,1)S(1)}) fusion(s32[16,64]{1,0:T(8,128)S(1)} %get-tuple-element.86, s32[2,128]{1,0:T(2,128)S(1)} %constant_dynamic-slice_fusion, s32[16,64]{1,0:T(8,128)S(1)} %get-tuple-element.88, ...), kind=kLoop, calls=%fused_computation.1 | loop fusion | flops 2088960 | bytes 25600 | tf_op jit(solution)/shard_map/reduce_and | solution.py:228
  30.2 1.4 %and_convert_fusion = (bf16[2,16,64,128]{3,2,1,0:T(8,128)(2,1)S(1)}, bf16[2,16,64,128]{3,2,1,0:T(8,128)(2,1)S(1)}, bf16[2,16,64,128]{3,2,1,0:T(8,128)(2,1)S(1)}, bf16[2,16,64,128]{3,2,1,0:T(8,128)(2,1)S(1)}) fusion(pred[2,16,64]{2,1,0:T(8,128)(4,1)S(1)} %get-tuple-element.63, pred[128]{0:T(512)(128)(4,1)S(1)} %iota_compare_fusion, ...), kind=kLoop, calls=%fused_computation | loop fusion | flops 2097152 | bytes 2105472 | tf_op jit(solution)/shard_map/convert_element_type | solution.py:230
  31.6 0.9 collective-permute-done.rest_0_
  32.5 5.2 %collective-permute-start.1 = (bf16[4,2,128,256]{3,2,1,0:T(8,128)(2,1)}, bf16[4,2,128,256]{3,2,1,0:T(8,128)(2,1)}, u32[]{:S(2)}, u32[]{:S(2)}) collective-permute-start(bf16[4,2,128,256]{3,2,1,0:T(8,128)(2,1)} %collective-permute-done.rest_0_), channel_id=1, source_target_pairs={{0,8},{4,12},{8,16},{12,20},{16,24},{20,28},{1,9},{5,13},{9,17},{1... | collective-permute-start | bytes 1572872 | tf_op jit(solution)/shard_map/ppermute | solution.py:262
  37.7 0.5 collective-permute-start.4
  38.2 0.0 collective-permute-done.2.rest_1_
  38.2 3.5 %all-to-all-done.1.q_ref = bf16[4,128,1024]{2,1,0:T(8,128)(2,1)S(1)} async-done(((bf16[4,128,1024]{2,1,0:T(8,128)(2,1)}), bf16[4,128,1024]{2,1,0:T(8,128)(2,1)S(1)}, u32[]{:S(2)}, u32[]{:S(2)}) %all-to-all-start.1) | async-done | bytes 1048608 | tf_op jit(solution)/shard_map/all_to_all | solution.py:251
  41.7 8.3 %shard_map.56 = (f32[16,128,256]{2,1,0:T(8,128)S(1)}, f32[16,16,256]{2,1,0:T(8,128)S(1)}, bf16[16,128]{1,0:T(8,128)(2,1)S(1)}) custom-call(s32[2,8,16]{2,1,0:T(8,128)S(1)} %broadcast_select_fusion.3.code_ref, bf16[4,128,1024]{2,1,0:T(8,128)(2,1)S(1)} %all-to-all-done.1.q_ref, bf16[2,16,64,128]{3,2,1,0:T(8,128)(2,1)S(1)} %get-tuple-element.41.pick_ref, ...), custom_call_target="tpu_custom_call" | custom-call | flops 2147483648 | bytes 8388608 | tf_op jit(solution)/shard_map/pallas_call | solution.py:148
  50.0 0.0 collective-permute-done.1.rest_0_
  50.0 2.7 %collective-permute-start.3 = (bf16[4,2,128,256]{3,2,1,0:T(8,128)(2,1)}, bf16[4,2,128,256]{3,2,1,0:T(8,128)(2,1)S(1)}, u32[]{:S(2)}, u32[]{:S(2)}) collective-permute-start(bf16[4,2,128,256]{3,2,1,0:T(8,128)(2,1)} %collective-permute-done.1.rest_0_), channel_id=1, source_target_pairs={{0,8},{4,12},{8,16},{12,20},{16,24},{20,28},{1,9},{5,13},{9,17},{1... | collective-permute-start | bytes 1572872 | tf_op jit(solution)/shard_map/ppermute | solution.py:262
  52.7 0.6 collective-permute-start.6
  53.3 0.0 collective-permute-done.4.rest_1_
  53.3 8.2 %shard_map.57 = (f32[16,128,256]{2,1,0:T(8,128)S(1)}, f32[16,16,256]{2,1,0:T(8,128)S(1)}, bf16[16,128]{1,0:T(8,128)(2,1)S(1)}) custom-call(s32[2,8,16]{2,1,0:T(8,128)S(1)} %broadcast_select_fusion.2.code_ref, bf16[4,128,1024]{2,1,0:T(8,128)(2,1)S(1)} %all-to-all-done.1.q_ref, bf16[2,16,64,128]{3,2,1,0:T(8,128)(2,1)S(1)} %get-tuple-element.45.pick_ref, ...), custom_call_target="tpu_custom_call" | custom-call | flops 2147483648 | bytes 8388608 | tf_op jit(solution)/shard_map/pallas_call | solution.py:148
  61.5 2.5 %collective-permute-done.3.rest_0_ = bf16[4,2,128,256]{3,2,1,0:T(8,128)(2,1)S(1)} collective-permute-done((bf16[4,2,128,256]{3,2,1,0:T(8,128)(2,1)}, bf16[4,2,128,256]{3,2,1,0:T(8,128)(2,1)S(1)}, u32[]{:S(2)}, u32[]{:S(2)}) %collective-permute-start.3) | collective-permute-done | bytes 524320 | tf_op jit(solution)/shard_map/ppermute | solution.py:262
  64.1 0.6 collective-permute-start.5
  64.6 2.3 %collective-permute-done.6.rest_1_ = bf16[4,2,128,256]{3,2,1,0:T(8,128)(2,1)S(1)} collective-permute-done((bf16[4,2,128,256]{3,2,1,0:T(8,128)(2,1)}, bf16[4,2,128,256]{3,2,1,0:T(8,128)(2,1)S(1)}, u32[]{:S(2)}, u32[]{:S(2)}) %collective-permute-start.6) | collective-permute-done | bytes 524320 | tf_op jit(solution)/shard_map/ppermute | solution.py:261
  67.0 8.1 %shard_map.58 = (f32[16,128,256]{2,1,0:T(8,128)S(1)}, f32[16,16,256]{2,1,0:T(8,128)S(1)}, bf16[16,128]{1,0:T(8,128)(2,1)S(1)}) custom-call(s32[2,8,16]{2,1,0:T(8,128)S(1)} %get-tuple-element.51.code_ref, bf16[4,128,1024]{2,1,0:T(8,128)(2,1)S(1)} %all-to-all-done.1.q_ref, bf16[2,16,64,128]{3,2,1,0:T(8,128)(2,1)S(1)} %get-tuple-element.52.pick_ref, ...), custom_call_target="tpu_custom_call" | custom-call | flops 2147483648 | bytes 8388608 | tf_op jit(solution)/shard_map/pallas_call | solution.py:148
  75.1 2.4 %collective-permute-done.5.rest_1_ = bf16[4,2,128,256]{3,2,1,0:T(8,128)(2,1)S(1)} collective-permute-done((bf16[4,2,128,256]{3,2,1,0:T(8,128)(2,1)S(1)}, bf16[4,2,128,256]{3,2,1,0:T(8,128)(2,1)S(1)}, u32[]{:S(2)}, u32[]{:S(2)}) %collective-permute-start.5) | collective-permute-done | bytes 524320 | tf_op jit(solution)/shard_map/ppermute | solution.py:261
  77.5 8.4 %shard_map.59 = bf16[4,128,1024]{2,1,0:T(8,128)(2,1)S(1)} custom-call(s32[2,8,16]{2,1,0:T(8,128)S(1)} %get-tuple-element.36.code_ref, bf16[4,128,1024]{2,1,0:T(8,128)(2,1)S(1)} %all-to-all-done.1.q_ref, bf16[2,16,64,128]{3,2,1,0:T(8,128)(2,1)S(1)} %get-tuple-element.38.pick_ref, bf16[4,2,128,256]{3,2,1,0:T(8,128)(2,1)S(1)} %collective-permute-done.3.rest_0_, ...), custom_call_target="tpu_custom_call" | custom-call | flops 2147483648 | bytes 8388608 | tf_op jit(solution)/shard_map/pallas_call | solution.py:148
  85.9 16.9 %all_to_all.15 = bf16[4,128,1024]{2,1,0:T(8,128)(2,1)S(1)} all-to-all(bf16[4,128,1024]{2,1,0:T(8,128)(2,1)S(1)} %shard_map.59), channel_id=1, replica_groups=mesh['chip'=8,'core'=2,'head'=2] {'head','core'}, dimensions={0} | all-to-all | bytes 2097152 | tf_op jit(solution)/shard_map/all_to_all | solution.py:283
  102.8 0.7 copy.16
  103.5 1.3 %copy.17 = bf16[128,4096]{1,0:T(8,128)(2,1)} copy(bf16[128,4096]{0,1:T(8,128)(2,1)S(1)} %bitcast.12) | data formatting | bytes 2097152 | tf_op jit(solution)/shard_map/reshape | solution.py:284
  (15 shorter events, 0.1 us)
Async XLA Ops:
  0.0 22.3 %copy-start = (s32[4,128]{1,0:T(4,128)S(1)}, s32[4,128]{1,0:T(4,128)}, u32[]{:S(2)}) copy-start(s32[4,128]{1,0:T(4,128)} %param.8) | copy-start | bytes 6148
  0.0 6.9 %copy-start.1 = (bf16[128,4096]{1,0:T(8,128)(2,1)S(1)}, bf16[128,4096]{1,0:T(8,128)(2,1)}, u32[]{:S(2)}) copy-start(bf16[128,4096]{1,0:T(8,128)(2,1)} %param.5) | copy-start | bytes 3145732
  2.0 13.7 %all-to-all-start = ((bf16[4,2,128,256]{3,2,1,0:T(8,128)(2,1)}), bf16[4,2,128,256]{3,2,1,0:T(8,128)(2,1)}, u32[]{:S(2)}, u32[]{:S(2)}) async-start(bf16[4,2,128,256]{3,2,1,0:T(8,128)(2,1)} %bitcast.14), calls=%async_computation | async-start | bytes 1048576 | tf_op jit(solution)/shard_map/all_to_all | solution.py:193
  6.9 15.4 %copy-start.2 = (s32[4,64,40]{1,2,0:T(8,128)S(1)}, s32[4,64,40]{1,2,0:T(8,128)}, u32[]{:S(2)}) copy-start(s32[4,64,40]{1,2,0:T(8,128)} %param.9) | copy-start | bytes 122884
  15.7 22.5 %collective-permute-start.2 = (bf16[4,2,128,256]{3,2,1,0:T(8,128)(2,1)}, bf16[4,2,128,256]{3,2,1,0:T(8,128)(2,1)}, u32[]{:S(2)}, u32[]{:S(2)}) collective-permute-start(bf16[4,2,128,256]{3,2,1,0:T(8,128)(2,1)} %all-to-all-done.rest_0_), channel_id=1, source_target_pairs={{0,4},{4,0},{8,12},{12,8},{16,20},{20,16},{24,28},{28,24},{1,5},{5... | collective-permute-start | bytes 1572872 | tf_op jit(solution)/shard_map/ppermute | solution.py:261
  18.0 14.5 %collective-permute-start = (bf16[4,2,128,256]{3,2,1,0:T(8,128)(2,1)}, bf16[4,2,128,256]{3,2,1,0:T(8,128)(2,1)}, u32[]{:S(2)}, u32[]{:S(2)}) collective-permute-start(bf16[4,2,128,256]{3,2,1,0:T(8,128)(2,1)} %all-to-all-done.rest_0_), channel_id=1, source_target_pairs={{0,8},{4,12},{8,16},{12,20},{16,24},{20,28},{1,9},{5,13},{9,17},{1... | collective-permute-start | bytes 1572872 | tf_op jit(solution)/shard_map/ppermute | solution.py:262
  23.7 18.0 %all-to-all-start.1 = ((bf16[4,128,1024]{2,1,0:T(8,128)(2,1)}), bf16[4,128,1024]{2,1,0:T(8,128)(2,1)S(1)}, u32[]{:S(2)}, u32[]{:S(2)}) async-start(bf16[4,128,1024]{2,1,0:T(8,128)(2,1)} %bitcast.7), calls=%async_computation.1 | async-start | bytes 2097152 | tf_op jit(solution)/shard_map/all_to_all | solution.py:251
  32.5 17.5 %collective-permute-start.1 = (bf16[4,2,128,256]{3,2,1,0:T(8,128)(2,1)}, bf16[4,2,128,256]{3,2,1,0:T(8,128)(2,1)}, u32[]{:S(2)}, u32[]{:S(2)}) collective-permute-start(bf16[4,2,128,256]{3,2,1,0:T(8,128)(2,1)} %collective-permute-done.rest_0_), channel_id=1, source_target_pairs={{0,8},{4,12},{8,16},{12,20},{16,24},{20,28},{1,9},{5,13},{9,17},{1... | collective-permute-start | bytes 1572872 | tf_op jit(solution)/shard_map/ppermute | solution.py:262
  37.7 15.7 %collective-permute-start.4 = (bf16[4,2,128,256]{3,2,1,0:T(8,128)(2,1)}, bf16[4,2,128,256]{3,2,1,0:T(8,128)(2,1)}, u32[]{:S(2)}, u32[]{:S(2)}) collective-permute-start(bf16[4,2,128,256]{3,2,1,0:T(8,128)(2,1)} %collective-permute-done.rest_0_), channel_id=1, source_target_pairs={{0,4},{4,0},{8,12},{12,8},{16,20},{20,16},{24,28},{28,24},{1,5},{5... | collective-permute-start | bytes 1572872 | tf_op jit(solution)/shard_map/ppermute | solution.py:261
  50.0 14.1 %collective-permute-start.3 = (bf16[4,2,128,256]{3,2,1,0:T(8,128)(2,1)}, bf16[4,2,128,256]{3,2,1,0:T(8,128)(2,1)S(1)}, u32[]{:S(2)}, u32[]{:S(2)}) collective-permute-start(bf16[4,2,128,256]{3,2,1,0:T(8,128)(2,1)} %collective-permute-done.1.rest_0_), channel_id=1, source_target_pairs={{0,8},{4,12},{8,16},{12,20},{16,24},{20,28},{1,9},{5,13},{9,17},{1... | collective-permute-start | bytes 1572872 | tf_op jit(solution)/shard_map/ppermute | solution.py:262
  52.7 14.3 %collective-permute-start.6 = (bf16[4,2,128,256]{3,2,1,0:T(8,128)(2,1)}, bf16[4,2,128,256]{3,2,1,0:T(8,128)(2,1)S(1)}, u32[]{:S(2)}, u32[]{:S(2)}) collective-permute-start(bf16[4,2,128,256]{3,2,1,0:T(8,128)(2,1)} %collective-permute-done.1.rest_0_), channel_id=1, source_target_pairs={{0,4},{4,0},{8,12},{12,8},{16,20},{20,16},{24,28},{28,24},{1,5},{5... | collective-permute-start | bytes 1572872 | tf_op jit(solution)/shard_map/ppermute | solution.py:261
  64.1 13.4 %collective-permute-start.5 = (bf16[4,2,128,256]{3,2,1,0:T(8,128)(2,1)S(1)}, bf16[4,2,128,256]{3,2,1,0:T(8,128)(2,1)S(1)}, u32[]{:S(2)}, u32[]{:S(2)}) collective-permute-start(bf16[4,2,128,256]{3,2,1,0:T(8,128)(2,1)S(1)} %collective-permute-done.3.rest_0_), channel_id=1, source_target_pairs={{0,4},{4,0},{8,12},{12,8},{16,20},{20,16},{24,28},{28,24},{1,5},{5... | collective-permute-start | bytes 1572872 | tf_op jit(solution)/shard_map/ppermute | solution.py:261

commit v5 on v4

--- a/solution.py
+++ b/solution.py
@@ -64,16 +64,22 @@
         start = pl.multiple_of(lax.rem(here, per_q) * BLK, BLK)
         return lax.div(here, per_q), pl.ds(start, BLK), pl.ds(g * head_dim, head_dim)
 
-    def scored(head, here, buffer):
+    def stage(head, ahead, ahead_buffer, here, buffer, top):
         query = jnp.concatenate(
-            [q_ref[place(here, head * group + g)] for g in range(group)], axis=0
+            [q_ref[place(ahead, head * group + g)] for g in range(group)], axis=0
         )
         query = jnp.concatenate([query, qext[...]], axis=1)
-        top = jnp.full((8, rows), -jnp.inf, F32)
+        at = head * blocks_here + here if here is not None else None
+        if here is not None and not first:
+            before = stat_in[at, :8]
+            top = jnp.maximum(top, before)
+            fade = jnp.exp2((before - top) * scale)
+        ahead_top = jnp.full((8, rows), -jnp.inf, F32)
+        shares, values = [], []
         for p, part in enumerate(part_refs):
             left = [part[c, head, :, pl.ds(0, head_dim)] for c in range(chunks)]
             right = [
-                etile[code_ref[head, here, p * per_part + i]] for i in range(per_part)
+                etile[code_ref[head, ahead, p * per_part + i]] for i in range(per_part)
             ]
             key = jnp.concatenate(
                 [jnp.concatenate(left, axis=0), jnp.concatenate(right, axis=0)], axis=1
@@ -81,52 +87,46 @@
             tile = lax.dot_general(
                 key, query, (((1,), (1,)), ((), ())), preferred_element_type=F32
             )
-            buffer[pl.ds(p * size, size), :] = tile
-            top = jnp.maximum(top, jnp.max(tile.reshape(size // 8, 8, rows), axis=0))
-        return jnp.max(top, axis=0, keepdims=True)
-
-    def mixed_in(head, here, buffer, top):
-        at = head * blocks_here + here
-        if first:
-            top = jnp.broadcast_to(top, (8, rows))
-            weight = jnp.zeros((8, rows), F32)
-        else:
-            before = stat_in[at, :8]
-            top = jnp.maximum(top, before)
-            fade = jnp.exp2((before - top) * scale)
-            weight = stat_in[at, 8:] * fade
-        mixed = jnp.zeros((head_dim, rows), F32)
-        for p, part in enumerate(part_refs):
-            tile = buffer[pl.ds(p * size, size), :].reshape(size // 8, 8, rows)
-            expo = jnp.exp2((tile - top[None]) * scale)
-            weight = weight + jnp.sum(expo, axis=0)
-            value = jnp.concatenate(
-                [part[c, head, :, pl.ds(head_dim, wide)] for c in range(chunks)], axis=1
+            ahead_buffer[pl.ds(p * size, size), :] = tile
+            ahead_top = jnp.maximum(
+                ahead_top, jnp.max(tile.reshape(size // 8, 8, rows), axis=0)
             )
-            mixed = mixed + jnp.dot(
-                value, expo.reshape(size, rows).astype(BF16), preferred_element_type=F32
-            )
+            if here is not None:
+                tile = buffer[pl.ds(p * size, size), :].reshape(size // 8, 8, rows)
+                expo = jnp.exp2((tile - top[None]) * scale)
+                shares.append(expo.reshape(size, rows).astype(BF16))
+                values += [part[c, head, :, pl.ds(head_dim, wide)] for c in range(chunks)]
+        ahead_top = jnp.broadcast_to(jnp.max(ahead_top, axis=0, keepdims=True), (8, rows))
+        if here is None:
+            return ahead_top
+        value = jnp.concatenate(values, axis=1)
+        value = jnp.concatenate([value, jnp.ones((16, value.shape[1]), BF16)], axis=0)
+        both = jnp.dot(value, jnp.concatenate(shares, axis=0), preferred_element_type=F32)
+        mixed, weight = both[:head_dim], both[head_dim : head_dim + 8]
         if not first:
             mixed = mixed + acc_in[at] * fade[:1]
+            weight = weight + stat_in[at, 8:] * fade
         if not last:
             acc_out[at] = mixed
             stat_out[at, :8] = top
             stat_out[at, 8:] = weight
-            return
-        result = (mixed / jnp.sum(weight, axis=0, keepdims=True)).T.astype(BF16)
+            return ahead_top
+        result = (mixed / weight[:1]).T.astype(BF16)
         for g in range(group):
             out_ref[place(here, (head - span[0]) * group + g)] = result[g * BLK : (g + 1) * BLK]
+        return ahead_top
 
     for head in range(*span):
         for slot in range(slots):
             etile[PICKED + slot] = pick_ref[head, slot]
 
-        @pl.loop(0, blocks_here // 2)
-        def _(step):
-            top_a = scored(head, 2 * step, score_a)
-            top_b = scored(head, 2 * step + 1, score_b)
-            mixed_in(head, 2 * step, score_a, top_a)
-            mixed_in(head, 2 * step + 1, score_b, top_b)
+        def two(step, top):
+            top = stage(head, 2 * step + 1, score_b, 2 * step, score_a, top)
+            ahead = jnp.minimum(2 * step + 2, blocks_here - 1)
+            return stage(head, ahead, score_a, 2 * step + 1, score_b, top)
+
+        top = stage(head, 0, score_a, None, None, None)
+        lax.fori_loop(0, blocks_here // 2, two, top)
 
 
 def attend_step(code, query, pick, parts, state, span, last, head_dim, group):

time: 105 us -> 104 us (level)
  Pallas kernels: 35.1 us -> 32.4 us
  waiting for transfers between devices: 18.2 us -> 19.6 us
    pallas_call x4, Pallas kernels: 33 us -> 30.4 us  [attend_step(): pl.pallas_call(functools.partial(step_kernel, parts=len(parts), first=fir...]
  transfers between devices with their start and end apart: 9 -> 9, of which waited for: 6 -> 6; matrix products, arithmetic and copies ran while one was open for 8% -> 8% of each run, Pallas kernels for 24% -> 22%
where the time goes in v5:
time: 104 us; the launch traced here: 103 us
  Pallas kernels  32.4 us (31%)
  starting transfers between devices  23.9 us (23%)
  waiting for transfers between devices  19.6 us (19%)
  blocking collectives  16.9 us (16%)
  other arithmetic  6.01 us (6%)
  local copies, waits for them, and re-layouts  4.47 us (4%)
    pallas_call x4, Pallas kernels, attend_step(): pl.pallas_call(functools.partial(step_kernel, parts=len(parts), first=fir...  30.4 us
    all_to_all x1, blocking collectives, body(): out = swap(state.reshape(ways, tok, q_width // ways))  16.9 us
    ppermute x3, starting transfers between devices, body(): part = lax.ppermute(part, 'chip', up) if n < final else None  12.2 us
    all_to_all x1, waiting for transfers between devices, body(): swap(arrange(keys, values, all_heads).reshape(ways, mine, tok, head_dim +...  6.59 us
    ppermute x4, waiting for transfers between devices, body(): fetched = (part, lax.ppermute(part, 'chip', across))  5.47 us
    all_to_all x1, starting transfers between devices, body(): swap(arrange(keys, values, all_heads).reshape(ways, mine, tok, head_dim +...  4.24 us
    ppermute x3, waiting for transfers between devices, body(): part = lax.ppermute(part, 'chip', up) if n < final else None  4.04 us
    ppermute x4, starting transfers between devices, body(): fetched = (part, lax.ppermute(part, 'chip', across))  3.97 us
  transfers between devices with their start and end apart: 9, of which 6 were waited for; matrix products, arithmetic and copies ran while one was open for 8% of the time, Pallas kernels for 22%

profile of v5, /device:TPU:0, one launch (start us, length us, event | category | flops | bytes accessed | tf_op | source)
XLA Modules:
  0.0 103.5 jit_solution(4029535521418547627)
XLA Ops:
  0.0 0.0 copy-start
  0.0 0.0 copy-start.1
  0.0 2.0 %shard_map.55 = bf16[8,128,256]{2,1,0:T(8,128)(2,1)} custom-call(bf16[128,1024]{1,0:T(8,128)(2,1)} %k_ref.1, bf16[128,1024]{1,0:T(8,128)(2,1)} %v_ref.1), custom_call_target="tpu_custom_call" | custom-call | tf_op jit(solution)/shard_map/pallas_call | solution.py:28
  2.0 4.2 %all-to-all-start = ((bf16[4,2,128,256]{3,2,1,0:T(8,128)(2,1)}), bf16[4,2,128,256]{3,2,1,0:T(8,128)(2,1)}, u32[]{:S(2)}, u32[]{:S(2)}) async-start(bf16[4,2,128,256]{3,2,1,0:T(8,128)(2,1)} %bitcast.14), calls=%async_computation | async-start | bytes 1048576 | tf_op jit(solution)/shard_map/all_to_all | solution.py:193
  6.3 0.1 reshape.466
  6.4 0.1 fusion
  6.5 0.1 broadcast_add_fusion.3
  6.6 0.1 add.297
  6.6 0.1 add.308
  6.7 0.1 add.316
  6.8 0.1 add.324
  6.9 0.0 copy-done.1
  6.9 0.0 copy-start.2
  6.9 0.7 copy.14
  7.6 1.3 %copy.15 = bf16[128,4,1024]{2,0,1:T(8,128)(2,1)} copy(bf16[128,4,1024]{0,2,1:T(8,128)(2,1)S(1)} %bitcast.13) | data formatting | bytes 2097152 | tf_op jit(solution)/shard_map/reshape | solution.py:200
  8.9 0.1 iota_add_fusion.2
  9.0 0.1 iota_add_fusion
  9.0 0.1 select_select_fusion
  9.1 6.6 %all-to-all-done.rest_0_ = bf16[4,2,128,256]{3,2,1,0:T(8,128)(2,1)} async-done(((bf16[4,2,128,256]{3,2,1,0:T(8,128)(2,1)}), bf16[4,2,128,256]{3,2,1,0:T(8,128)(2,1)}, u32[]{:S(2)}, u32[]{:S(2)}) %all-to-all-start) | async-done | bytes 524320 | tf_op jit(solution)/shard_map/all_to_all | solution.py:193
  15.7 2.3 %collective-permute-start.2 = (bf16[4,2,128,256]{3,2,1,0:T(8,128)(2,1)}, bf16[4,2,128,256]{3,2,1,0:T(8,128)(2,1)}, u32[]{:S(2)}, u32[]{:S(2)}) collective-permute-start(bf16[4,2,128,256]{3,2,1,0:T(8,128)(2,1)} %all-to-all-done.rest_0_), channel_id=1, source_target_pairs={{0,4},{4,0},{8,12},{12,8},{16,20},{20,16},{24,28},{28,24},{1,5},{5... | collective-permute-start | bytes 1572872 | tf_op jit(solution)/shard_map/ppermute | solution.py:261
  18.0 4.3 %collective-permute-start = (bf16[4,2,128,256]{3,2,1,0:T(8,128)(2,1)}, bf16[4,2,128,256]{3,2,1,0:T(8,128)(2,1)}, u32[]{:S(2)}, u32[]{:S(2)}) collective-permute-start(bf16[4,2,128,256]{3,2,1,0:T(8,128)(2,1)} %all-to-all-done.rest_0_), channel_id=1, source_target_pairs={{0,8},{4,12},{8,16},{12,20},{16,24},{20,28},{1,9},{5,13},{9,17},{1... | collective-permute-start | bytes 1572872 | tf_op jit(solution)/shard_map/ppermute | solution.py:262
  22.3 0.0 copy-done
  22.3 0.0 copy-done.2
  22.3 0.1 copy.12
  22.4 1.2 %compare_reduce_fusion.4 = (pred[2,8,16]{2,1,0:T(8,128)(4,1)S(1)}, pred[2,8,16]{2,1,0:T(8,128)(4,1)S(1)}, pred[2,8,16]{2,1,0:T(8,128)(4,1)S(1)}, pred[2,8,16]{2,1,0:T(8,128)(4,1)S(1)}) fusion(s32[2,8,40]{2,1,0:T(8,128)S(1)} %bitcast.15, s32[16]{0:T(128)S(1)} %add.324, s32[16]{0:T(128)S(1)} %add.308, s32[16]{0:T(128)S(1)} %add.316, s32[16]{0:T(128)S(1)} %add.297), kind=kLoop, calls=%fused_computation.8 | loop fusion | flops 80896 | bytes 3840 | tf_op jit(solution)/shard_map/reduce_or | solution.py:220
  23.7 3.5 %all-to-all-start.1 = ((bf16[4,128,1024]{2,1,0:T(8,128)(2,1)}), bf16[4,128,1024]{2,1,0:T(8,128)(2,1)S(1)}, u32[]{:S(2)}, u32[]{:S(2)}) async-start(bf16[4,128,1024]{2,1,0:T(8,128)(2,1)} %bitcast.7), calls=%async_computation.1 | async-start | bytes 2097152 | tf_op jit(solution)/shard_map/all_to_all | solution.py:251
  27.2 2.9 %compare_reduce_fusion = (pred[2,16,64]{2,1,0:T(8,128)(4,1)S(1)}, pred[2,16,64]{2,1,0:T(8,128)(4,1)S(1)}, pred[2,16,64]{2,1,0:T(8,128)(4,1)S(1)}, pred[2,16,64]{2,1,0:T(8,128)(4,1)S(1)}) fusion(s32[16,64]{1,0:T(8,128)S(1)} %get-tuple-element.86, s32[2,128]{1,0:T(2,128)S(1)} %constant_dynamic-slice_fusion, s32[16,64]{1,0:T(8,128)S(1)} %get-tuple-element.88, ...), kind=kLoop, calls=%fused_computation.1 | loop fusion | flops 2088960 | bytes 25600 | tf_op jit(solution)/shard_map/reduce_and | solution.py:228
  30.2 1.4 %and_convert_fusion = (bf16[2,16,64,128]{3,2,1,0:T(8,128)(2,1)S(1)}, bf16[2,16,64,128]{3,2,1,0:T(8,128)(2,1)S(1)}, bf16[2,16,64,128]{3,2,1,0:T(8,128)(2,1)S(1)}, bf16[2,16,64,128]{3,2,1,0:T(8,128)(2,1)S(1)}) fusion(pred[2,16,64]{2,1,0:T(8,128)(4,1)S(1)} %get-tuple-element.63, pred[128]{0:T(512)(128)(4,1)S(1)} %iota_compare_fusion, ...), kind=kLoop, calls=%fused_computation | loop fusion | flops 2097152 | bytes 2105472 | tf_op jit(solution)/shard_map/convert_element_type | solution.py:230
  31.6 0.9 collective-permute-done.rest_0_
  32.5 5.2 %collective-permute-start.1 = (bf16[4,2,128,256]{3,2,1,0:T(8,128)(2,1)}, bf16[4,2,128,256]{3,2,1,0:T(8,128)(2,1)}, u32[]{:S(2)}, u32[]{:S(2)}) collective-permute-start(bf16[4,2,128,256]{3,2,1,0:T(8,128)(2,1)} %collective-permute-done.rest_0_), channel_id=1, source_target_pairs={{0,8},{4,12},{8,16},{12,20},{16,24},{20,28},{1,9},{5,13},{9,17},{1... | collective-permute-start | bytes 1572872 | tf_op jit(solution)/shard_map/ppermute | solution.py:262
  37.7 0.5 collective-permute-start.4
  38.2 0.0 collective-permute-done.2.rest_1_
  38.2 3.5 %all-to-all-done.1.q_ref = bf16[4,128,1024]{2,1,0:T(8,128)(2,1)S(1)} async-done(((bf16[4,128,1024]{2,1,0:T(8,128)(2,1)}), bf16[4,128,1024]{2,1,0:T(8,128)(2,1)S(1)}, u32[]{:S(2)}, u32[]{:S(2)}) %all-to-all-start.1) | async-done | bytes 1048608 | tf_op jit(solution)/shard_map/all_to_all | solution.py:251
  41.7 7.5 %shard_map.56 = (f32[16,128,256]{2,1,0:T(8,128)S(1)}, f32[16,16,256]{2,1,0:T(8,128)S(1)}, bf16[16,128]{1,0:T(8,128)(2,1)S(1)}) custom-call(s32[2,8,16]{2,1,0:T(8,128)S(1)} %broadcast_select_fusion.3.code_ref, bf16[4,128,1024]{2,1,0:T(8,128)(2,1)S(1)} %all-to-all-done.1.q_ref, bf16[2,16,64,128]{3,2,1,0:T(8,128)(2,1)S(1)} %get-tuple-element.41.pick_ref, ...), custom_call_target="tpu_custom_call" | custom-call | flops 2147483648 | bytes 8388608 | tf_op jit(solution)/shard_map/pallas_call | solution.py:148
  49.2 0.0 collective-permute-done.1.rest_0_
  49.2 2.7 %collective-permute-start.3 = (bf16[4,2,128,256]{3,2,1,0:T(8,128)(2,1)}, bf16[4,2,128,256]{3,2,1,0:T(8,128)(2,1)S(1)}, u32[]{:S(2)}, u32[]{:S(2)}) collective-permute-start(bf16[4,2,128,256]{3,2,1,0:T(8,128)(2,1)} %collective-permute-done.1.rest_0_), channel_id=1, source_target_pairs={{0,8},{4,12},{8,16},{12,20},{16,24},{20,28},{1,9},{5,13},{9,17},{1... | collective-permute-start | bytes 1572872 | tf_op jit(solution)/shard_map/ppermute | solution.py:262
  51.9 0.6 collective-permute-start.6
  52.5 0.0 collective-permute-done.4.rest_1_
  52.5 7.6 %shard_map.57 = (f32[16,128,256]{2,1,0:T(8,128)S(1)}, f32[16,16,256]{2,1,0:T(8,128)S(1)}, bf16[16,128]{1,0:T(8,128)(2,1)S(1)}) custom-call(s32[2,8,16]{2,1,0:T(8,128)S(1)} %broadcast_select_fusion.2.code_ref, bf16[4,128,1024]{2,1,0:T(8,128)(2,1)S(1)} %all-to-all-done.1.q_ref, bf16[2,16,64,128]{3,2,1,0:T(8,128)(2,1)S(1)} %get-tuple-element.45.pick_ref, ...), custom_call_target="tpu_custom_call" | custom-call | flops 2147483648 | bytes 8388608 | tf_op jit(solution)/shard_map/pallas_call | solution.py:148
  60.1 3.2 %collective-permute-done.3.rest_0_ = bf16[4,2,128,256]{3,2,1,0:T(8,128)(2,1)S(1)} collective-permute-done((bf16[4,2,128,256]{3,2,1,0:T(8,128)(2,1)}, bf16[4,2,128,256]{3,2,1,0:T(8,128)(2,1)S(1)}, u32[]{:S(2)}, u32[]{:S(2)}) %collective-permute-start.3) | collective-permute-done | bytes 524320 | tf_op jit(solution)/shard_map/ppermute | solution.py:262
  63.3 0.5 collective-permute-start.5
  63.8 2.4 %collective-permute-done.6.rest_1_ = bf16[4,2,128,256]{3,2,1,0:T(8,128)(2,1)S(1)} collective-permute-done((bf16[4,2,128,256]{3,2,1,0:T(8,128)(2,1)}, bf16[4,2,128,256]{3,2,1,0:T(8,128)(2,1)S(1)}, u32[]{:S(2)}, u32[]{:S(2)}) %collective-permute-start.6) | collective-permute-done | bytes 524320 | tf_op jit(solution)/shard_map/ppermute | solution.py:261
  66.2 7.4 %shard_map.58 = (f32[16,128,256]{2,1,0:T(8,128)S(1)}, f32[16,16,256]{2,1,0:T(8,128)S(1)}, bf16[16,128]{1,0:T(8,128)(2,1)S(1)}) custom-call(s32[2,8,16]{2,1,0:T(8,128)S(1)} %get-tuple-element.51.code_ref, bf16[4,128,1024]{2,1,0:T(8,128)(2,1)S(1)} %all-to-all-done.1.q_ref, bf16[2,16,64,128]{3,2,1,0:T(8,128)(2,1)S(1)} %get-tuple-element.52.pick_ref, ...), custom_call_target="tpu_custom_call" | custom-call | flops 2147483648 | bytes 8388608 | tf_op jit(solution)/shard_map/pallas_call | solution.py:148
  73.6 3.1 %collective-permute-done.5.rest_1_ = bf16[4,2,128,256]{3,2,1,0:T(8,128)(2,1)S(1)} collective-permute-done((bf16[4,2,128,256]{3,2,1,0:T(8,128)(2,1)S(1)}, bf16[4,2,128,256]{3,2,1,0:T(8,128)(2,1)S(1)}, u32[]{:S(2)}, u32[]{:S(2)}) %collective-permute-start.5) | collective-permute-done | bytes 524320 | tf_op jit(solution)/shard_map/ppermute | solution.py:261
  76.7 7.9 %shard_map.59 = bf16[4,128,1024]{2,1,0:T(8,128)(2,1)S(1)} custom-call(s32[2,8,16]{2,1,0:T(8,128)S(1)} %get-tuple-element.36.code_ref, bf16[4,128,1024]{2,1,0:T(8,128)(2,1)S(1)} %all-to-all-done.1.q_ref, bf16[2,16,64,128]{3,2,1,0:T(8,128)(2,1)S(1)} %get-tuple-element.38.pick_ref, bf16[4,2,128,256]{3,2,1,0:T(8,128)(2,1)S(1)} %collective-permute-done.3.rest_0_, ...), custom_call_target="tpu_custom_call" | custom-call | flops 2147483648 | bytes 8388608 | tf_op jit(solution)/shard_map/pallas_call | solution.py:148
  84.6 16.9 %all_to_all.15 = bf16[4,128,1024]{2,1,0:T(8,128)(2,1)S(1)} all-to-all(bf16[4,128,1024]{2,1,0:T(8,128)(2,1)S(1)} %shard_map.59), channel_id=1, replica_groups=mesh['chip'=8,'core'=2,'head'=2] {'head','core'}, dimensions={0} | all-to-all | bytes 2097152 | tf_op jit(solution)/shard_map/all_to_all | solution.py:283
  101.5 0.7 copy.16
  102.2 1.3 %copy.17 = bf16[128,4096]{1,0:T(8,128)(2,1)} copy(bf16[128,4096]{0,1:T(8,128)(2,1)S(1)} %bitcast.12) | data formatting | bytes 2097152 | tf_op jit(solution)/shard_map/reshape | solution.py:284
  (15 shorter events, 0.1 us)
Async XLA Ops:
  0.0 22.3 %copy-start = (s32[4,128]{1,0:T(4,128)S(1)}, s32[4,128]{1,0:T(4,128)}, u32[]{:S(2)}) copy-start(s32[4,128]{1,0:T(4,128)} %param.8) | copy-start | bytes 6148
  0.0 6.9 %copy-start.1 = (bf16[128,4096]{1,0:T(8,128)(2,1)S(1)}, bf16[128,4096]{1,0:T(8,128)(2,1)}, u32[]{:S(2)}) copy-start(bf16[128,4096]{1,0:T(8,128)(2,1)} %param.5) | copy-start | bytes 3145732
  2.0 13.7 %all-to-all-start = ((bf16[4,2,128,256]{3,2,1,0:T(8,128)(2,1)}), bf16[4,2,128,256]{3,2,1,0:T(8,128)(2,1)}, u32[]{:S(2)}, u32[]{:S(2)}) async-start(bf16[4,2,128,256]{3,2,1,0:T(8,128)(2,1)} %bitcast.14), calls=%async_computation | async-start | bytes 1048576 | tf_op jit(solution)/shard_map/all_to_all | solution.py:193
  6.9 15.4 %copy-start.2 = (s32[4,64,40]{1,2,0:T(8,128)S(1)}, s32[4,64,40]{1,2,0:T(8,128)}, u32[]{:S(2)}) copy-start(s32[4,64,40]{1,2,0:T(8,128)} %param.9) | copy-start | bytes 122884
  15.7 22.5 %collective-permute-start.2 = (bf16[4,2,128,256]{3,2,1,0:T(8,128)(2,1)}, bf16[4,2,128,256]{3,2,1,0:T(8,128)(2,1)}, u32[]{:S(2)}, u32[]{:S(2)}) collective-permute-start(bf16[4,2,128,256]{3,2,1,0:T(8,128)(2,1)} %all-to-all-done.rest_0_), channel_id=1, source_target_pairs={{0,4},{4,0},{8,12},{12,8},{16,20},{20,16},{24,28},{28,24},{1,5},{5... | collective-permute-start | bytes 1572872 | tf_op jit(solution)/shard_map/ppermute | solution.py:261
  18.0 14.5 %collective-permute-start = (bf16[4,2,128,256]{3,2,1,0:T(8,128)(2,1)}, bf16[4,2,128,256]{3,2,1,0:T(8,128)(2,1)}, u32[]{:S(2)}, u32[]{:S(2)}) collective-permute-start(bf16[4,2,128,256]{3,2,1,0:T(8,128)(2,1)} %all-to-all-done.rest_0_), channel_id=1, source_target_pairs={{0,8},{4,12},{8,16},{12,20},{16,24},{20,28},{1,9},{5,13},{9,17},{1... | collective-permute-start | bytes 1572872 | tf_op jit(solution)/shard_map/ppermute | solution.py:262
  23.7 18.0 %all-to-all-start.1 = ((bf16[4,128,1024]{2,1,0:T(8,128)(2,1)}), bf16[4,128,1024]{2,1,0:T(8,128)(2,1)S(1)}, u32[]{:S(2)}, u32[]{:S(2)}) async-start(bf16[4,128,1024]{2,1,0:T(8,128)(2,1)} %bitcast.7), calls=%async_computation.1 | async-start | bytes 2097152 | tf_op jit(solution)/shard_map/all_to_all | solution.py:251
  32.5 16.7 %collective-permute-start.1 = (bf16[4,2,128,256]{3,2,1,0:T(8,128)(2,1)}, bf16[4,2,128,256]{3,2,1,0:T(8,128)(2,1)}, u32[]{:S(2)}, u32[]{:S(2)}) collective-permute-start(bf16[4,2,128,256]{3,2,1,0:T(8,128)(2,1)} %collective-permute-done.rest_0_), channel_id=1, source_target_pairs={{0,8},{4,12},{8,16},{12,20},{16,24},{20,28},{1,9},{5,13},{9,17},{1... | collective-permute-start | bytes 1572872 | tf_op jit(solution)/shard_map/ppermute | solution.py:262
  37.7 14.9 %collective-permute-start.4 = (bf16[4,2,128,256]{3,2,1,0:T(8,128)(2,1)}, bf16[4,2,128,256]{3,2,1,0:T(8,128)(2,1)}, u32[]{:S(2)}, u32[]{:S(2)}) collective-permute-start(bf16[4,2,128,256]{3,2,1,0:T(8,128)(2,1)} %collective-permute-done.rest_0_), channel_id=1, source_target_pairs={{0,4},{4,0},{8,12},{12,8},{16,20},{20,16},{24,28},{28,24},{1,5},{5... | collective-permute-start | bytes 1572872 | tf_op jit(solution)/shard_map/ppermute | solution.py:261
  49.2 14.1 %collective-permute-start.3 = (bf16[4,2,128,256]{3,2,1,0:T(8,128)(2,1)}, bf16[4,2,128,256]{3,2,1,0:T(8,128)(2,1)S(1)}, u32[]{:S(2)}, u32[]{:S(2)}) collective-permute-start(bf16[4,2,128,256]{3,2,1,0:T(8,128)(2,1)} %collective-permute-done.1.rest_0_), channel_id=1, source_target_pairs={{0,8},{4,12},{8,16},{12,20},{16,24},{20,28},{1,9},{5,13},{9,17},{1... | collective-permute-start | bytes 1572872 | tf_op jit(solution)/shard_map/ppermute | solution.py:262
  51.9 14.3 %collective-permute-start.6 = (bf16[4,2,128,256]{3,2,1,0:T(8,128)(2,1)}, bf16[4,2,128,256]{3,2,1,0:T(8,128)(2,1)S(1)}, u32[]{:S(2)}, u32[]{:S(2)}) collective-permute-start(bf16[4,2,128,256]{3,2,1,0:T(8,128)(2,1)} %collective-permute-done.1.rest_0_), channel_id=1, source_target_pairs={{0,4},{4,0},{8,12},{12,8},{16,20},{20,16},{24,28},{28,24},{1,5},{5... | collective-permute-start | bytes 1572872 | tf_op jit(solution)/shard_map/ppermute | solution.py:261
  63.3 13.4 %collective-permute-start.5 = (bf16[4,2,128,256]{3,2,1,0:T(8,128)(2,1)S(1)}, bf16[4,2,128,256]{3,2,1,0:T(8,128)(2,1)S(1)}, u32[]{:S(2)}, u32[]{:S(2)}) collective-permute-start(bf16[4,2,128,256]{3,2,1,0:T(8,128)(2,1)S(1)} %collective-permute-done.3.rest_0_), channel_id=1, source_target_pairs={{0,4},{4,0},{8,12},{12,8},{16,20},{20,16},{24,28},{28,24},{1,5},{5... | collective-permute-start | bytes 1572872 | tf_op jit(solution)/shard_map/ppermute | solution.py:261

commit v6 on v5

--- a/solution.py
+++ b/solution.py
@@ -32,7 +32,10 @@
 
 
 def step_kernel(code_ref, q_ref, pick_ref, *rest, parts, first, last, span, head_dim, group):
-    part_refs, rest = rest[:parts], rest[parts:]
+    part_refs = []
+    for count in parts:
+        part_refs.append(rest[:count])
+        rest = rest[count:]
     if not first:
         (acc_in, stat_in, _), rest = rest[:3], rest[3:]
     if last:
@@ -42,9 +45,9 @@
         mark_out[...] = jnp.zeros(mark_out.shape, BF16)
     qext, etile, score_a, score_b = rest
     rows = BLK * group
-    chunks, _, wide, _ = part_refs[0].shape
+    chunks, _, wide, _ = part_refs[0][0].shape
     per_part = chunks * wide // BLK
-    slots = parts * per_part
+    slots = len(parts) * per_part
     size = per_part * BLK
     per_q = q_ref.shape[1] // BLK
     blocks_here = q_ref.shape[0] * per_q
@@ -59,6 +62,12 @@
     etile[LIVE] = jnp.zeros((BLK, head_dim), BF16)
     etile[DEAD] = jnp.where(lane == BLK, 1.0, 0.0).astype(BF16)
     etile[OWN] = jnp.where(lane == key_iota, 1.0, 0.0).astype(BF16)
+
+    def held(p, head, c):
+        for ref in part_refs[p]:
+            if head < ref.shape[1]:
+                return ref.at[c, head]
+            head -= ref.shape[1]
 
     def place(here, g):
         start = pl.multiple_of(lax.rem(here, per_q) * BLK, BLK)
@@ -76,8 +85,8 @@
             fade = jnp.exp2((before - top) * scale)
         ahead_top = jnp.full((8, rows), -jnp.inf, F32)
         shares, values = [], []
-        for p, part in enumerate(part_refs):
-            left = [part[c, head, :, pl.ds(0, head_dim)] for c in range(chunks)]
+        for p in range(len(parts)):
+            left = [held(p, head, c)[:, pl.ds(0, head_dim)] for c in range(chunks)]
             right = [
                 etile[code_ref[head, ahead, p * per_part + i]] for i in range(per_part)
             ]
@@ -95,7 +104,7 @@
                 tile = buffer[pl.ds(p * size, size), :].reshape(size // 8, 8, rows)
                 expo = jnp.exp2((tile - top[None]) * scale)
                 shares.append(expo.reshape(size, rows).astype(BF16))
-                values += [part[c, head, :, pl.ds(head_dim, wide)] for c in range(chunks)]
+                values += [held(p, head, c)[:, pl.ds(head_dim, wide)] for c in range(chunks)]
         ahead_top = jnp.broadcast_to(jnp.max(ahead_top, axis=0, keepdims=True), (8, rows))
         if here is None:
             return ahead_top
@@ -142,13 +151,14 @@
     )
     count = span[1] - span[0]
     out = jax.ShapeDtypeStruct(query.shape[:2] + (count * group * head_dim,), BF16)
+    arrays = [x for part in parts for x in part]
     first = state is None
     state = () if first else tuple(state)
     work = count * blocks_here * rows * slots * BLK
     return pl.pallas_call(
         functools.partial(
             step_kernel,
-            parts=len(parts),
+            parts=tuple(len(part) for part in parts),
             first=first,
             last=last,
             span=span,
@@ -156,7 +166,7 @@
             group=group,
         ),
         out_shape=out if last else carried,
-        in_specs=[smem] + [vmem] * (2 + len(parts) + len(state)),
+        in_specs=[smem] + [vmem] * (2 + len(arrays) + len(state)),
         out_specs=vmem if last else (vmem,) * 3,
         scratch_shapes=[
             pltpu.VMEM((rows, head_dim), BF16),
@@ -168,7 +178,7 @@
         cost_estimate=pl.CostEstimate(
             flops=4 * work * head_dim, transcendentals=work, bytes_accessed=8 << 20
         ),
-    )(code, query, pick, *parts, *state)
+    )(code, query, pick, *arrays, *state)
 
 
 def body(queries, keys, values, vertical, slash, *, cores, chips, heads):
@@ -258,7 +268,15 @@
                 if state is not None:
                     part, mark = lax.optimization_barrier((part, state[2]))
                     state = state[:2] + (mark,)
-                fetched = (part, lax.ppermute(part, "chip", across))
+                if n < final or mine == 1:
+                    other = (lax.ppermute(part, "chip", across),)
+                else:
+                    cut = (mine + 1) // 2
+                    other = (
+                        lax.ppermute(part[:, :cut], "chip", across),
+                        lax.ppermute(waiting[1][0][:, cut:], "chip", up),
+                    )
+                fetched = ((part,), other)
                 part = lax.ppermute(part, "chip", up) if n < final else None
             if n:
                 state = attend(query, tables[n - 1], waiting, state, n > final)
@@ -278,7 +296,7 @@
         many = math.gcd(groups, 4)
         for g in range(0, groups, many):
             part = rows[g : g + many].reshape((many * each,) + rows.shape[2:])
-            state = attend(query, masks(order[g : g + many]), (part,), state, g + many == groups)
+            state = attend(query, masks(order[g : g + many]), ((part,),), state, g + many == groups)
 
     out = swap(state.reshape(ways, tok, q_width // ways))
     return out.transpose(1, 0, 2).reshape(tok, q_width)

time: 104 us -> 101 us (0.971)
  waiting for transfers between devices: 19.6 us -> 13.8 us
  starting transfers between devices: 23.9 us -> 26.8 us
    ppermute x3, waiting for transfers between devices: 4.04 us -> 0.88 us  [body(): part = lax.ppermute(part, 'chip', up) if n < final else None]
    ppermute x4 -> x5, starting transfers between devices: 3.97 us -> 6.84 us  [the longest x3 3.42 us: body(): other = (lax.ppermute(part, 'chip', across),)]
    ppermute x4 -> x5, waiting for transfers between devices: 5.47 us -> 2.82 us  [the longest x3 2.82 us: body(): other = (lax.ppermute(part, 'chip', across),)]
  transfers between devices with their start and end apart: 9 -> 10, of which waited for: 6 -> 4; matrix products, arithmetic and copies ran while one was open for 8% -> 8% of each run, Pallas kernels for 22% -> 22%
where the time goes in v6:
time: 101 us
  Pallas kernels  32.5 us (32%)
  starting transfers between devices  26.8 us (27%)
  blocking collectives  16.9 us (17%)
  waiting for transfers between devices  13.8 us (14%)
  other arithmetic  6.01 us (6%)
  local copies, waits for them, and re-layouts  4.51 us (4%)
    pallas_call x4, Pallas kernels, attend_step(): pl.pallas_call(functools.partial(step_kernel, parts=tuple((len(part) for...  30.4 us
    all_to_all x1, blocking collectives, body(): out = swap(state.reshape(ways, tok, q_width // ways))  16.9 us
    ppermute x3, starting transfers between devices, body(): part = lax.ppermute(part, 'chip', up) if n < final else None  12.2 us
    all_to_all x1, waiting for transfers between devices, body(): swap(arrange(keys, values, all_heads).reshape(ways, mine, tok, head_dim +...  6.61 us
    all_to_all x1, starting transfers between devices, body(): swap(arrange(keys, values, all_heads).reshape(ways, mine, tok, head_dim +...  4.24 us
    all_to_all x1, starting transfers between devices, body(): query = swap(query).reshape(-1, max(tok, BLK), q_width // ways)  3.53 us
    all_to_all x1, waiting for transfers between devices, body(): query = swap(query).reshape(-1, max(tok, BLK), q_width // ways)  3.45 us
    ppermute x3, starting transfers between devices, body(): other = (lax.ppermute(part, 'chip', across),)  3.42 us
  transfers between devices with their start and end apart: 10, of which 4 were waited for; matrix products, arithmetic and copies ran while one was open for 8% of the time, Pallas kernels for 22%

profile of v6, /device:TPU:0, one launch (start us, length us, event | category | flops | bytes accessed | tf_op | source)
XLA Modules:
  0.0 100.7 jit_solution(15019175376789111109)
XLA Ops:
  0.0 0.0 copy-start
  0.0 2.0 %shard_map.55 = bf16[8,128,256]{2,1,0:T(8,128)(2,1)} custom-call(bf16[128,1024]{1,0:T(8,128)(2,1)} %k_ref.1, bf16[128,1024]{1,0:T(8,128)(2,1)} %v_ref.1), custom_call_target="tpu_custom_call" | custom-call | tf_op jit(solution)/shard_map/pallas_call | solution.py:28
  2.0 4.2 %all-to-all-start = ((bf16[4,2,128,256]{3,2,1,0:T(8,128)(2,1)}), bf16[4,2,128,256]{3,2,1,0:T(8,128)(2,1)}, u32[]{:S(2)}, u32[]{:S(2)}) async-start(bf16[4,2,128,256]{3,2,1,0:T(8,128)(2,1)} %bitcast.14), calls=%async_computation | async-start | bytes 1048576 | tf_op jit(solution)/shard_map/all_to_all | solution.py:203
  6.3 0.1 reshape.466
  6.4 0.1 fusion
  6.5 0.1 broadcast_add_fusion.3
  6.6 0.1 add.297
  6.6 0.1 add.308
  6.7 0.1 add.316
  6.8 0.1 add.324
  6.9 0.0 copy-done.1
  6.9 0.0 copy-start.2
  6.9 0.7 copy.14
  7.6 1.3 %copy.15 = bf16[128,4,1024]{2,0,1:T(8,128)(2,1)} copy(bf16[128,4,1024]{0,2,1:T(8,128)(2,1)S(1)} %bitcast.13) | data formatting | bytes 2097152 | tf_op jit(solution)/shard_map/reshape | solution.py:210
  8.9 0.1 iota_add_fusion.2
  9.0 0.1 iota_add_fusion
  9.1 0.1 select_select_fusion
  9.1 6.6 %all-to-all-done.rest_0_ = bf16[4,2,128,256]{3,2,1,0:T(8,128)(2,1)} async-done(((bf16[4,2,128,256]{3,2,1,0:T(8,128)(2,1)}), bf16[4,2,128,256]{3,2,1,0:T(8,128)(2,1)}, u32[]{:S(2)}, u32[]{:S(2)}) %all-to-all-start) | async-done | bytes 524320 | tf_op jit(solution)/shard_map/all_to_all | solution.py:203
  15.7 2.3 %collective-permute-start.2 = (bf16[4,2,128,256]{3,2,1,0:T(8,128)(2,1)}, bf16[4,2,128,256]{3,2,1,0:T(8,128)(2,1)}, u32[]{:S(2)}, u32[]{:S(2)}) collective-permute-start(bf16[4,2,128,256]{3,2,1,0:T(8,128)(2,1)} %all-to-all-done.rest_0_), channel_id=1, source_target_pairs={{0,4},{4,0},{8,12},{12,8},{16,20},{20,16},{24,28},{28,24},{1,5},{5... | collective-permute-start | bytes 1572872 | tf_op jit(solution)/shard_map/ppermute | solution.py:272
  18.0 4.3 %collective-permute-start = (bf16[4,2,128,256]{3,2,1,0:T(8,128)(2,1)}, bf16[4,2,128,256]{3,2,1,0:T(8,128)(2,1)}, u32[]{:S(2)}, u32[]{:S(2)}) collective-permute-start(bf16[4,2,128,256]{3,2,1,0:T(8,128)(2,1)} %all-to-all-done.rest_0_), channel_id=1, source_target_pairs={{0,8},{4,12},{8,16},{12,20},{16,24},{20,28},{1,9},{5,13},{9,17},{1... | collective-permute-start | bytes 1572872 | tf_op jit(solution)/shard_map/ppermute | solution.py:280
  22.3 0.0 copy-done
  22.3 0.1 copy.12
  22.5 1.2 %compare_reduce_fusion.4 = (pred[2,8,16]{2,1,0:T(8,128)(4,1)S(1)}, pred[2,8,16]{2,1,0:T(8,128)(4,1)S(1)}, pred[2,8,16]{2,1,0:T(8,128)(4,1)S(1)}, pred[2,8,16]{2,1,0:T(8,128)(4,1)S(1)}) fusion(s32[2,8,40]{2,1,0:T(8,128)S(1)} %bitcast.15, s32[16]{0:T(128)S(1)} %add.324, s32[16]{0:T(128)S(1)} %add.308, s32[16]{0:T(128)S(1)} %add.316, s32[16]{0:T(128)S(1)} %add.297), kind=kLoop, calls=%fused_computation.8 | loop fusion | flops 80896 | bytes 3840 | tf_op jit(solution)/shard_map/reduce_or | solution.py:230
  23.7 3.5 %all-to-all-start.1 = ((bf16[4,128,1024]{2,1,0:T(8,128)(2,1)}), bf16[4,128,1024]{2,1,0:T(8,128)(2,1)S(1)}, u32[]{:S(2)}, u32[]{:S(2)}) async-start(bf16[4,128,1024]{2,1,0:T(8,128)(2,1)} %bitcast.7), calls=%async_computation.1 | async-start | bytes 2097152 | tf_op jit(solution)/shard_map/all_to_all | solution.py:261
  27.3 2.9 %compare_reduce_fusion = (pred[2,16,64]{2,1,0:T(8,128)(4,1)S(1)}, pred[2,16,64]{2,1,0:T(8,128)(4,1)S(1)}, pred[2,16,64]{2,1,0:T(8,128)(4,1)S(1)}, pred[2,16,64]{2,1,0:T(8,128)(4,1)S(1)}) fusion(s32[16,64]{1,0:T(8,128)S(1)} %get-tuple-element.86, s32[2,128]{1,0:T(2,128)S(1)} %constant_dynamic-slice_fusion, s32[16,64]{1,0:T(8,128)S(1)} %get-tuple-element.88, ...), kind=kLoop, calls=%fused_computation.1 | loop fusion | flops 2088960 | bytes 25600 | tf_op jit(solution)/shard_map/reduce_and | solution.py:238
  30.2 1.4 %and_convert_fusion = (bf16[2,16,64,128]{3,2,1,0:T(8,128)(2,1)S(1)}, bf16[2,16,64,128]{3,2,1,0:T(8,128)(2,1)S(1)}, bf16[2,16,64,128]{3,2,1,0:T(8,128)(2,1)S(1)}, bf16[2,16,64,128]{3,2,1,0:T(8,128)(2,1)S(1)}) fusion(pred[2,16,64]{2,1,0:T(8,128)(4,1)S(1)} %get-tuple-element.63, pred[128]{0:T(512)(128)(4,1)S(1)} %iota_compare_fusion, ...), kind=kLoop, calls=%fused_computation | loop fusion | flops 2097152 | bytes 2105472 | tf_op jit(solution)/shard_map/convert_element_type | solution.py:240
  31.6 0.9 collective-permute-done.rest_0_
  32.5 5.2 %collective-permute-start.1 = (bf16[4,2,128,256]{3,2,1,0:T(8,128)(2,1)}, bf16[4,2,128,256]{3,2,1,0:T(8,128)(2,1)}, u32[]{:S(2)}, u32[]{:S(2)}) collective-permute-start(bf16[4,2,128,256]{3,2,1,0:T(8,128)(2,1)} %collective-permute-done.rest_0_), channel_id=1, source_target_pairs={{0,8},{4,12},{8,16},{12,20},{16,24},{20,28},{1,9},{5,13},{9,17},{1... | collective-permute-start | bytes 1572872 | tf_op jit(solution)/shard_map/ppermute | solution.py:280
  37.7 0.5 collective-permute-start.4
  38.2 0.0 collective-permute-done.2.rest_1_
  38.2 3.5 %all-to-all-done.1.q_ref = bf16[4,128,1024]{2,1,0:T(8,128)(2,1)S(1)} async-done(((bf16[4,128,1024]{2,1,0:T(8,128)(2,1)}), bf16[4,128,1024]{2,1,0:T(8,128)(2,1)S(1)}, u32[]{:S(2)}, u32[]{:S(2)}) %all-to-all-start.1) | async-done | bytes 1048608 | tf_op jit(solution)/shard_map/all_to_all | solution.py:261
  41.7 7.5 %shard_map.56 = (f32[16,128,256]{2,1,0:T(8,128)S(1)}, f32[16,16,256]{2,1,0:T(8,128)S(1)}, bf16[16,128]{1,0:T(8,128)(2,1)S(1)}) custom-call(s32[2,8,16]{2,1,0:T(8,128)S(1)} %broadcast_select_fusion.3.code_ref, bf16[4,128,1024]{2,1,0:T(8,128)(2,1)S(1)} %all-to-all-done.1.q_ref, bf16[2,16,64,128]{3,2,1,0:T(8,128)(2,1)S(1)} %get-tuple-element.41.pick_ref, ...), custom_call_target="tpu_custom_call" | custom-call | flops 2147483648 | bytes 8388608 | tf_op jit(solution)/shard_map/pallas_call | solution.py:158
  49.2 0.0 collective-permute-done.1.rest_0_
  49.2 0.6 collective-permute-start.6
  49.8 2.7 %collective-permute-start.3 = (bf16[4,2,128,256]{3,2,1,0:T(8,128)(2,1)}, bf16[4,2,128,256]{3,2,1,0:T(8,128)(2,1)S(1)}, u32[]{:S(2)}, u32[]{:S(2)}) collective-permute-start(bf16[4,2,128,256]{3,2,1,0:T(8,128)(2,1)} %collective-permute-done.1.rest_0_), channel_id=1, source_target_pairs={{0,8},{4,12},{8,16},{12,20},{16,24},{20,28},{1,9},{5,13},{9,17},{1... | collective-permute-start | bytes 1572872 | tf_op jit(solution)/shard_map/ppermute | solution.py:280
  52.5 0.0 collective-permute-done.4.rest_1_
  52.5 7.6 %shard_map.57 = (f32[16,128,256]{2,1,0:T(8,128)S(1)}, f32[16,16,256]{2,1,0:T(8,128)S(1)}, bf16[16,128]{1,0:T(8,128)(2,1)S(1)}) custom-call(s32[2,8,16]{2,1,0:T(8,128)S(1)} %broadcast_select_fusion.2.code_ref, bf16[4,128,1024]{2,1,0:T(8,128)(2,1)S(1)} %all-to-all-done.1.q_ref, bf16[2,16,64,128]{3,2,1,0:T(8,128)(2,1)S(1)} %get-tuple-element.45.pick_ref, ...), custom_call_target="tpu_custom_call" | custom-call | flops 2147483648 | bytes 8388608 | tf_op jit(solution)/shard_map/pallas_call | solution.py:158
  60.1 2.8 %collective-permute-done.6.rest_1_ = bf16[4,2,128,256]{3,2,1,0:T(8,128)(2,1)S(1)} collective-permute-done((bf16[4,2,128,256]{3,2,1,0:T(8,128)(2,1)}, bf16[4,2,128,256]{3,2,1,0:T(8,128)(2,1)S(1)}, u32[]{:S(2)}, u32[]{:S(2)}) %collective-permute-start.6) | collective-permute-done | bytes 524320 | tf_op jit(solution)/shard_map/ppermute | solution.py:272
  63.0 2.8 %collective-permute-start.7 = (bf16[4,1,128,256]{3,2,1,0:T(8,128)(2,1)S(1)}, bf16[4,1,128,256]{3,2,1,0:T(8,128)(2,1)S(1)}, u32[]{:S(2)}, u32[]{:S(2)}) collective-permute-start(bf16[4,1,128,256]{3,2,1,0:T(8,128)(2,1)S(1)} %slice.8), channel_id=1, source_target_pairs={{0,8},{4,12},{8,16},{12,20},{16,24},{20,28},{1,9},{5,13},{9,17},{1... | collective-permute-start | bytes 786440 | tf_op jit(solution)/shard_map/ppermute | solution.py:277
  65.8 0.0 collective-permute-done.3.rest_0_
  65.8 0.6 collective-permute-start.5
  66.4 7.5 %shard_map.58 = (f32[16,128,256]{2,1,0:T(8,128)S(1)}, f32[16,16,256]{2,1,0:T(8,128)S(1)}, bf16[16,128]{1,0:T(8,128)(2,1)S(1)}) custom-call(s32[2,8,16]{2,1,0:T(8,128)S(1)} %get-tuple-element.51.code_ref, bf16[4,128,1024]{2,1,0:T(8,128)(2,1)S(1)} %all-to-all-done.1.q_ref, bf16[2,16,64,128]{3,2,1,0:T(8,128)(2,1)S(1)} %get-tuple-element.52.pick_ref, ...), custom_call_target="tpu_custom_call" | custom-call | flops 2147483648 | bytes 8388608 | tf_op jit(solution)/shard_map/pallas_call | solution.py:158
  73.9 0.0 collective-permute-done.7.rest_2_
  73.9 0.0 collective-permute-done.5.rest_1_
  73.9 7.9 %shard_map.59 = bf16[4,128,1024]{2,1,0:T(8,128)(2,1)S(1)} custom-call(s32[2,8,16]{2,1,0:T(8,128)S(1)} %get-tuple-element.36.code_ref, bf16[4,128,1024]{2,1,0:T(8,128)(2,1)S(1)} %all-to-all-done.1.q_ref, bf16[2,16,64,128]{3,2,1,0:T(8,128)(2,1)S(1)} %get-tuple-element.38.pick_ref, bf16[4,2,128,256]{3,2,1,0:T(8,128)(2,1)S(1)} %collective-permute-done.3.rest_0_, ...), custom_call_target="tpu_custom_call" | custom-call | flops 2147483648 | bytes 8388608 | tf_op jit(solution)/shard_map/pallas_call | solution.py:158
  81.8 16.9 %all_to_all.15 = bf16[4,128,1024]{2,1,0:T(8,128)(2,1)S(1)} all-to-all(bf16[4,128,1024]{2,1,0:T(8,128)(2,1)S(1)} %shard_map.59), channel_id=1, replica_groups=mesh['chip'=8,'core'=2,'head'=2] {'head','core'}, dimensions={0} | all-to-all | bytes 2097152 | tf_op jit(solution)/shard_map/all_to_all | solution.py:301
  98.7 0.7 copy.16
  99.4 1.3 %copy.17 = bf16[128,4096]{1,0:T(8,128)(2,1)} copy(bf16[128,4096]{0,1:T(8,128)(2,1)S(1)} %bitcast.12) | data formatting | bytes 2097152 | tf_op jit(solution)/shard_map/reshape | solution.py:302
  (19 shorter events, 0.1 us)
Async XLA Ops:
  0.0 22.3 %copy-start = (s32[4,128]{1,0:T(4,128)S(1)}, s32[4,128]{1,0:T(4,128)}, u32[]{:S(2)}) copy-start(s32[4,128]{1,0:T(4,128)} %param.8) | copy-start | bytes 6148
  0.0 6.9 %copy-start.1 = (bf16[128,4096]{1,0:T(8,128)(2,1)S(1)}, bf16[128,4096]{1,0:T(8,128)(2,1)}, u32[]{:S(2)}) copy-start(bf16[128,4096]{1,0:T(8,128)(2,1)} %param.5) | copy-start | bytes 3145732
  2.0 13.7 %all-to-all-start = ((bf16[4,2,128,256]{3,2,1,0:T(8,128)(2,1)}), bf16[4,2,128,256]{3,2,1,0:T(8,128)(2,1)}, u32[]{:S(2)}, u32[]{:S(2)}) async-start(bf16[4,2,128,256]{3,2,1,0:T(8,128)(2,1)} %bitcast.14), calls=%async_computation | async-start | bytes 1048576 | tf_op jit(solution)/shard_map/all_to_all | solution.py:203
  6.9 15.4 %copy-start.2 = (s32[4,64,40]{1,2,0:T(8,128)S(1)}, s32[4,64,40]{1,2,0:T(8,128)}, u32[]{:S(2)}) copy-start(s32[4,64,40]{1,2,0:T(8,128)} %param.9) | copy-start | bytes 122884
  15.7 22.5 %collective-permute-start.2 = (bf16[4,2,128,256]{3,2,1,0:T(8,128)(2,1)}, bf16[4,2,128,256]{3,2,1,0:T(8,128)(2,1)}, u32[]{:S(2)}, u32[]{:S(2)}) collective-permute-start(bf16[4,2,128,256]{3,2,1,0:T(8,128)(2,1)} %all-to-all-done.rest_0_), channel_id=1, source_target_pairs={{0,4},{4,0},{8,12},{12,8},{16,20},{20,16},{24,28},{28,24},{1,5},{5... | collective-permute-start | bytes 1572872 | tf_op jit(solution)/shard_map/ppermute | solution.py:272
  18.0 14.5 %collective-permute-start = (bf16[4,2,128,256]{3,2,1,0:T(8,128)(2,1)}, bf16[4,2,128,256]{3,2,1,0:T(8,128)(2,1)}, u32[]{:S(2)}, u32[]{:S(2)}) collective-permute-start(bf16[4,2,128,256]{3,2,1,0:T(8,128)(2,1)} %all-to-all-done.rest_0_), channel_id=1, source_target_pairs={{0,8},{4,12},{8,16},{12,20},{16,24},{20,28},{1,9},{5,13},{9,17},{1... | collective-permute-start | bytes 1572872 | tf_op jit(solution)/shard_map/ppermute | solution.py:280
  23.7 18.0 %all-to-all-start.1 = ((bf16[4,128,1024]{2,1,0:T(8,128)(2,1)}), bf16[4,128,1024]{2,1,0:T(8,128)(2,1)S(1)}, u32[]{:S(2)}, u32[]{:S(2)}) async-start(bf16[4,128,1024]{2,1,0:T(8,128)(2,1)} %bitcast.7), calls=%async_computation.1 | async-start | bytes 2097152 | tf_op jit(solution)/shard_map/all_to_all | solution.py:261
  32.5 16.7 %collective-permute-start.1 = (bf16[4,2,128,256]{3,2,1,0:T(8,128)(2,1)}, bf16[4,2,128,256]{3,2,1,0:T(8,128)(2,1)}, u32[]{:S(2)}, u32[]{:S(2)}) collective-permute-start(bf16[4,2,128,256]{3,2,1,0:T(8,128)(2,1)} %collective-permute-done.rest_0_), channel_id=1, source_target_pairs={{0,8},{4,12},{8,16},{12,20},{16,24},{20,28},{1,9},{5,13},{9,17},{1... | collective-permute-start | bytes 1572872 | tf_op jit(solution)/shard_map/ppermute | solution.py:280
  37.7 14.8 %collective-permute-start.4 = (bf16[4,2,128,256]{3,2,1,0:T(8,128)(2,1)}, bf16[4,2,128,256]{3,2,1,0:T(8,128)(2,1)}, u32[]{:S(2)}, u32[]{:S(2)}) collective-permute-start(bf16[4,2,128,256]{3,2,1,0:T(8,128)(2,1)} %collective-permute-done.rest_0_), channel_id=1, source_target_pairs={{0,4},{4,0},{8,12},{12,8},{16,20},{20,16},{24,28},{28,24},{1,5},{5... | collective-permute-start | bytes 1572872 | tf_op jit(solution)/shard_map/ppermute | solution.py:272
  49.2 13.7 %collective-permute-start.6 = (bf16[4,2,128,256]{3,2,1,0:T(8,128)(2,1)}, bf16[4,2,128,256]{3,2,1,0:T(8,128)(2,1)S(1)}, u32[]{:S(2)}, u32[]{:S(2)}) collective-permute-start(bf16[4,2,128,256]{3,2,1,0:T(8,128)(2,1)} %collective-permute-done.1.rest_0_), channel_id=1, source_target_pairs={{0,4},{4,0},{8,12},{12,8},{16,20},{20,16},{24,28},{28,24},{1,5},{5... | collective-permute-start | bytes 1572872 | tf_op jit(solution)/shard_map/ppermute | solution.py:272
  49.8 16.0 %collective-permute-start.3 = (bf16[4,2,128,256]{3,2,1,0:T(8,128)(2,1)}, bf16[4,2,128,256]{3,2,1,0:T(8,128)(2,1)S(1)}, u32[]{:S(2)}, u32[]{:S(2)}) collective-permute-start(bf16[4,2,128,256]{3,2,1,0:T(8,128)(2,1)} %collective-permute-done.1.rest_0_), channel_id=1, source_target_pairs={{0,8},{4,12},{8,16},{12,20},{16,24},{20,28},{1,9},{5,13},{9,17},{1... | collective-permute-start | bytes 1572872 | tf_op jit(solution)/shard_map/ppermute | solution.py:280
  63.0 11.0 %collective-permute-start.7 = (bf16[4,1,128,256]{3,2,1,0:T(8,128)(2,1)S(1)}, bf16[4,1,128,256]{3,2,1,0:T(8,128)(2,1)S(1)}, u32[]{:S(2)}, u32[]{:S(2)}) collective-permute-start(bf16[4,1,128,256]{3,2,1,0:T(8,128)(2,1)S(1)} %slice.8), channel_id=1, source_target_pairs={{0,8},{4,12},{8,16},{12,20},{16,24},{20,28},{1,9},{5,13},{9,17},{1... | collective-permute-start | bytes 786440 | tf_op jit(solution)/shard_map/ppermute | solution.py:277
  65.8 8.1 %collective-permute-start.5 = (bf16[4,1,128,256]{3,2,1,0:T(8,128)(2,1)S(1)}, bf16[4,1,128,256]{3,2,1,0:T(8,128)(2,1)S(1)}, u32[]{:S(2)}, u32[]{:S(2)}) collective-permute-start(bf16[4,1,128,256]{3,2,1,0:T(8,128)(2,1)S(1)} %slice.6), channel_id=1, source_target_pairs={{0,4},{4,0},{8,12},{12,8},{16,20},{20,16},{24,28},{28,24},{1,5},{5... | collective-permute-start | bytes 786440 | tf_op jit(solution)/shard_map/ppermute | solution.py:276

commit v7 on v6

--- a/solution.py
+++ b/solution.py
@@ -14,21 +14,27 @@
 BF16, F32 = jnp.bfloat16, jnp.float32
 
 
-def arrange_kernel(k_ref, v_ref, o_ref):
-    width = v_ref.shape[0]
-    head_dim = o_ref.shape[2] - width
-    for h in range(o_ref.shape[0]):
-        o_ref[h, :, :head_dim] = k_ref[:, h * head_dim : (h + 1) * head_dim]
-        o_ref[h, :, head_dim:] = v_ref[:, h * head_dim : (h + 1) * head_dim].T
-
-
-def arrange(keys, values, heads):
-    tok, width = keys.shape
-    head_dim = width // heads
+def arrange_kernel(me_ref, k_ref, v_ref, *o_refs):
+    mine, width, _ = o_refs[0].shape
+    head_dim = o_refs[0].shape[2] - width
+    for m, o_ref in enumerate(o_refs):
+        device = lax.bitwise_xor(me_ref[0], m)
+        first = (lax.rem(device, 2) * 2 + lax.div(device, 2)) * mine
+        for h in range(mine):
+            columns = pl.ds(pl.multiple_of((first + h) * head_dim, head_dim), head_dim)
+            o_ref[h, :, :head_dim] = k_ref[:, columns]
+            o_ref[h, :, head_dim:] = v_ref[:, columns].T
+
+
+def arrange(me, keys, values, mine, head_dim):
+    tok = keys.shape[0]
+    vmem = pl.BlockSpec(memory_space=pltpu.VMEM)
     return pl.pallas_call(
         arrange_kernel,
-        out_shape=jax.ShapeDtypeStruct((heads, tok, head_dim + tok), BF16),
-    )(keys, values)
+        out_shape=[jax.ShapeDtypeStruct((mine, tok, head_dim + tok), BF16)] * 4,
+        in_specs=[pl.BlockSpec(memory_space=pltpu.SMEM), vmem, vmem],
+        out_specs=[vmem] * 4,
+    )(me, keys, values)
 
 
 def step_kernel(code_ref, q_ref, pick_ref, *rest, parts, first, last, span, head_dim, group):
@@ -194,13 +200,19 @@
     chip = lax.axis_index("chip")
     if cores == 1:
         chip = chip * 2 + lax.axis_index("core")
-    relative = cores > 1 and chips == 8
+    relative = cores > 1 and chips == 8 and heads == 2
     swap = functools.partial(
         lax.all_to_all, axis_name=axes, split_axis=0, concat_axis=0, tiled=True
     )
 
     if relative:
-        pair = swap(arrange(keys, values, all_heads).reshape(ways, mine, tok, head_dim + tok))
+        me = lax.axis_index("core") * 2 + lax.axis_index("head")
+        pieces = arrange(me[None].astype(jnp.int32), keys, values, mine, head_dim)
+        pair = [pieces[0]] + [
+            lax.ppermute(pieces[m], ("core", "head"), [(i, i ^ m) for i in range(4)])
+            for m in (1, 3, 2)
+        ]
+        pair = jnp.stack([pair[0], pair[1], pair[3], pair[2]])
     else:
         pair = jnp.concatenate(
             [keys.reshape(tok, ways, mine, head_dim), values.reshape(tok, ways, mine, head_dim)],
@@ -215,6 +227,10 @@
     local = jnp.arange(per_group, dtype=jnp.int32)
     if cores > 1:
         local = local.reshape(cores, heads, along).swapaxes(0, 1).reshape(-1)
+    local_keys = local
+    if relative:
+        order = jnp.stack([me ^ m for m in range(4)]).astype(jnp.int32)
+        local_keys = (order[:, None] * along + jnp.arange(along, dtype=jnp.int32)).reshape(-1)
     first_head = lax.axis_index("core") * mine if cores > 1 else 0
     slash = lax.dynamic_slice_in_dim(slash, first_head, mine, axis=0)
     vertical = lax.dynamic_slice_in_dim(vertical, first_head, mine, axis=0)
@@ -226,7 +242,7 @@
     ids = chip * per_group + local
 
     def masks(source):
-        nat = (source[:, None] * per_group + local).reshape(-1)
+        nat = (source[:, None] * per_group + local_keys).reshape(-1)
         listed = jnp.any(lists[:, :, :, None] == nat, axis=2)
         slot = PICKED + jnp.arange(nat.shape[0], dtype=jnp.int32)
         code = jnp.where(

time: 101 us -> 97.3 us (0.963)
  waiting for transfers between devices: 13.8 us -> 7.86 us
  local copies, waits for them, and re-layouts: 4.51 us -> 5.65 us
  other arithmetic: 6.01 us -> 7.03 us
    all_to_all x1 -> x0, waiting for transfers between devices: 6.61 us -> none  [body(): swap(arrange(keys, values, all_heads).reshape(ways, mine, tok, head_dim +...]
    all_to_all x1 -> x0, starting transfers between devices: 4.24 us -> none  [body(): swap(arrange(keys, values, all_heads).reshape(ways, mine, tok, head_dim +...]
    ppermute x0 -> x3, starting transfers between devices: none -> 3.08 us  [body(): lax.ppermute(pieces[m], ('core', 'head'), [(i, i ^ m) for i in range(4)])]
    ppermute x0 -> x3, waiting for transfers between devices: none -> 1.86 us  [body(): lax.ppermute(pieces[m], ('core', 'head'), [(i, i ^ m) for i in range(4)])]
    ppermute x3, starting transfers between devices: 12.2 us -> 13.6 us  [body(): part = lax.ppermute(part, 'chip', up) if n < final else None]
    ppermute x3, waiting for transfers between devices: 2.82 us -> 1.66 us  [body(): other = (lax.ppermute(part, 'chip', across),)]
    unnamed x7, local copies, waits for them, and re-layouts: 0.68 us -> 1.7 us
  transfers between devices with their start and end apart: 10 -> 12, of which waited for: 4 -> 4; matrix products, arithmetic and copies ran while one was open for 8% -> 10% of each run, Pallas kernels for 22% -> 23%
where the time goes in v7:
time: 97.3 us; the launch traced here: 96.9 us
  Pallas kernels  32.1 us (33%)
  starting transfers between devices  26.2 us (27%)
  blocking collectives  17.8 us (18%)
  waiting for transfers between devices  7.86 us (8%)
  other arithmetic  7.03 us (7%)
  local copies, waits for them, and re-layouts  5.65 us (6%)
    pallas_call x4, Pallas kernels, attend_step(): pl.pallas_call(functools.partial(step_kernel, parts=tuple((len(part) for...  30.1 us
    all_to_all x1, blocking collectives, body(): out = swap(state.reshape(ways, tok, q_width // ways))  17.8 us
    ppermute x3, starting transfers between devices, body(): part = lax.ppermute(part, 'chip', up) if n < final else None  13.6 us
    all_to_all x1, starting transfers between devices, body(): query = swap(query).reshape(-1, max(tok, BLK), q_width // ways)  3.53 us
    ppermute x3, starting transfers between devices, body(): lax.ppermute(pieces[m], ('core', 'head'), [(i, i ^ m) for i in range(4)])  3.08 us
    reduce_and x1, other arithmetic, masks(): hidden = jnp.all(vertical[:, None, None, :] != position[..., None], axis=3)  2.92 us
    ppermute x1, starting transfers between devices, body(): lax.ppermute(waiting[1][0][:, cut:], 'chip', up)  2.84 us
    ppermute x3, starting transfers between devices, body(): other = (lax.ppermute(part, 'chip', across),)  2.53 us
  transfers between devices with their start and end apart: 12, of which 4 were waited for; matrix products, arithmetic and copies ran while one was open for 10% of the time, Pallas kernels for 23%

profile of v7, /device:TPU:0, one launch (start us, length us, event | category | flops | bytes accessed | tf_op | source)
XLA Modules:
  0.0 96.9 jit_solution(5137951795628638112)
XLA Ops:
  0.0 2.0 %shard_map.55 = (bf16[2,128,256]{2,1,0:T(8,128)(2,1)}, bf16[2,128,256]{2,1,0:T(8,128)(2,1)}, bf16[2,128,256]{2,1,0:T(8,128)(2,1)}, bf16[2,128,256]{2,1,0:T(8,128)(2,1)}) custom-call(s32[1]{0:T(128)} %bitcast.me_ref, bf16[128,1024]{1,0:T(8,128)(2,1)} %k_ref.1, bf16[128,1024]{1,0:T(8,128)(2,1)} %v_ref.1), custom_call_target="tpu_custom_call" | custom-call | tf_op jit(solution)/shard_map/pallas_call | solution.py:32
  2.0 3.0 %collective-permute-start = (bf16[2,128,256]{2,1,0:T(8,128)(2,1)}, bf16[2,128,256]{2,1,0:T(8,128)(2,1)S(1)}, u32[]{:S(2)}, u32[]{:S(2)}) collective-permute-start(bf16[2,128,256]{2,1,0:T(8,128)(2,1)} %get-tuple-element.37), channel_id=1, source_target_pairs={{0,1},{1,0},{2,3},{3,2},{4,5},{5,4},{6,7},{7,6},{8,9},{9,8},{10,11... | collective-permute-start | bytes 393224 | tf_op jit(solution)/shard_map/ppermute | solution.py:212
  4.9 0.0 collective-permute-start.1
  4.9 0.1 collective-permute-start.2
  5.1 0.1 add_multiply_fusion
  5.1 0.1 iota_add_fusion.4
  5.2 0.1 add.311
  5.3 0.1 add.317
  5.4 0.1 fusion
  5.5 0.1 broadcast_add_fusion.3
  5.6 0.1 add.314
  5.6 0.1 add.326
  5.7 0.1 add.334
  5.8 0.1 add.342
  5.9 0.1 select_select_fusion
  6.0 0.1 iota_add_fusion.2
  6.1 0.1 iota_add_fusion
  6.1 1.7 %copy.14 = bf16[128,4096]{0,1:T(8,128)(2,1)S(1)} copy(bf16[128,4096]{1,0:T(8,128)(2,1)} %param.5) | data formatting | bytes 2097152 | tf_op args[0]
  7.8 0.0 copy-start.2
  7.8 1.3 %copy.15 = bf16[128,4,1024]{2,0,1:T(8,128)(2,1)} copy(bf16[128,4,1024]{0,2,1:T(8,128)(2,1)S(1)} %bitcast.20) | data formatting | bytes 2097152 | tf_op jit(solution)/shard_map/reshape | solution.py:222
  9.1 0.0 collective-permute-done
  9.2 1.8 %collective-permute-done.2 = bf16[2,128,256]{2,1,0:T(8,128)(2,1)S(1)} collective-permute-done((bf16[2,128,256]{2,1,0:T(8,128)(2,1)}, bf16[2,128,256]{2,1,0:T(8,128)(2,1)S(1)}, u32[]{:S(2)}, u32[]{:S(2)}) %collective-permute-start.2) | collective-permute-done | bytes 131104 | tf_op jit(solution)/shard_map/ppermute | solution.py:212
  11.0 0.9 pad_maximum_fusion.rest_0_
  11.9 1.4 %collective-permute-start.5 = (bf16[4,2,128,256]{3,2,1,0:T(8,128)(2,1)}, bf16[4,2,128,256]{3,2,1,0:T(8,128)(2,1)}, u32[]{:S(2)}, u32[]{:S(2)}) collective-permute-start(bf16[4,2,128,256]{3,2,1,0:T(8,128)(2,1)} %pad_maximum_fusion.rest_0_), channel_id=1, source_target_pairs={{0,4},{4,0},{8,12},{12,8},{16,20},{20,16},{24,28},{28,24},{1,5},{5... | collective-permute-start | bytes 1572872 | tf_op jit(solution)/shard_map/ppermute | solution.py:288
  13.3 4.3 %collective-permute-start.3 = (bf16[4,2,128,256]{3,2,1,0:T(8,128)(2,1)}, bf16[4,2,128,256]{3,2,1,0:T(8,128)(2,1)}, u32[]{:S(2)}, u32[]{:S(2)}) collective-permute-start(bf16[4,2,128,256]{3,2,1,0:T(8,128)(2,1)} %pad_maximum_fusion.rest_0_), channel_id=1, source_target_pairs={{0,8},{4,12},{8,16},{12,20},{16,24},{20,28},{1,9},{5,13},{9,17},{1... | collective-permute-start | bytes 1572872 | tf_op jit(solution)/shard_map/ppermute | solution.py:296
  17.6 0.1 copy.12
  17.7 1.2 %compare_reduce_fusion.4 = (pred[2,8,16]{2,1,0:T(8,128)(4,1)S(1)}, pred[2,8,16]{2,1,0:T(8,128)(4,1)S(1)}, pred[2,8,16]{2,1,0:T(8,128)(4,1)S(1)}, pred[2,8,16]{2,1,0:T(8,128)(4,1)S(1)}) fusion(s32[2,8,40]{2,1,0:T(8,128)S(1)} %bitcast.25, s32[16]{0:T(128)S(1)} %add.342, s32[16]{0:T(128)S(1)} %add.326, s32[16]{0:T(128)S(1)} %add.334, s32[16]{0:T(128)S(1)} %add.314), kind=kLoop, calls=%fused_computation.9 | loop fusion | flops 80896 | bytes 3840 | tf_op jit(solution)/shard_map/reduce_or | solution.py:246
  19.0 3.5 %all-to-all-start = ((bf16[4,128,1024]{2,1,0:T(8,128)(2,1)}), bf16[4,128,1024]{2,1,0:T(8,128)(2,1)S(1)}, u32[]{:S(2)}, u32[]{:S(2)}) async-start(bf16[4,128,1024]{2,1,0:T(8,128)(2,1)} %bitcast.14), calls=%async_computation | async-start | bytes 2097152 | tf_op jit(solution)/shard_map/all_to_all | solution.py:277
  22.5 2.9 %compare_reduce_fusion = (pred[2,16,64]{2,1,0:T(8,128)(4,1)S(1)}, pred[2,16,64]{2,1,0:T(8,128)(4,1)S(1)}, pred[2,16,64]{2,1,0:T(8,128)(4,1)S(1)}, pred[2,16,64]{2,1,0:T(8,128)(4,1)S(1)}) fusion(s32[16,64]{1,0:T(8,128)S(1)} %get-tuple-element.94, s32[2,128]{1,0:T(2,128)S(1)} %constant_dynamic-slice_fusion, s32[16,64]{1,0:T(8,128)S(1)} %get-tuple-element.96, ...), kind=kLoop, calls=%fused_computation.1 | loop fusion | flops 2088960 | bytes 25600 | tf_op jit(solution)/shard_map/reduce_and | solution.py:254
  25.4 1.4 %and_convert_fusion = (bf16[2,16,64,128]{3,2,1,0:T(8,128)(2,1)S(1)}, bf16[2,16,64,128]{3,2,1,0:T(8,128)(2,1)S(1)}, bf16[2,16,64,128]{3,2,1,0:T(8,128)(2,1)S(1)}, bf16[2,16,64,128]{3,2,1,0:T(8,128)(2,1)S(1)}) fusion(pred[2,16,64]{2,1,0:T(8,128)(4,1)S(1)} %get-tuple-element.71, pred[128]{0:T(512)(128)(4,1)S(1)} %iota_compare_fusion, ...), kind=kLoop, calls=%fused_computation | loop fusion | flops 2097152 | bytes 2105472 | tf_op jit(solution)/shard_map/convert_element_type | solution.py:256
  26.9 1.8 %collective-permute-done.3.rest_0_ = bf16[4,2,128,256]{3,2,1,0:T(8,128)(2,1)} collective-permute-done((bf16[4,2,128,256]{3,2,1,0:T(8,128)(2,1)}, bf16[4,2,128,256]{3,2,1,0:T(8,128)(2,1)}, u32[]{:S(2)}, u32[]{:S(2)}) %collective-permute-start.3) | collective-permute-done | bytes 524320 | tf_op jit(solution)/shard_map/ppermute | solution.py:296
  28.7 5.2 %collective-permute-start.4 = (bf16[4,2,128,256]{3,2,1,0:T(8,128)(2,1)}, bf16[4,2,128,256]{3,2,1,0:T(8,128)(2,1)}, u32[]{:S(2)}, u32[]{:S(2)}) collective-permute-start(bf16[4,2,128,256]{3,2,1,0:T(8,128)(2,1)} %collective-permute-done.3.rest_0_), channel_id=1, source_target_pairs={{0,8},{4,12},{8,16},{12,20},{16,24},{20,28},{1,9},{5,13},{9,17},{1... | collective-permute-start | bytes 1572872 | tf_op jit(solution)/shard_map/ppermute | solution.py:296
  33.9 0.5 collective-permute-start.7
  34.4 2.5 %all-to-all-done.q_ref = bf16[4,128,1024]{2,1,0:T(8,128)(2,1)S(1)} async-done(((bf16[4,128,1024]{2,1,0:T(8,128)(2,1)}), bf16[4,128,1024]{2,1,0:T(8,128)(2,1)S(1)}, u32[]{:S(2)}, u32[]{:S(2)}) %all-to-all-start) | async-done | bytes 1048608 | tf_op jit(solution)/shard_map/all_to_all | solution.py:277
  36.9 7.4 %shard_map.56 = (f32[16,128,256]{2,1,0:T(8,128)S(1)}, f32[16,16,256]{2,1,0:T(8,128)S(1)}, bf16[16,128]{1,0:T(8,128)(2,1)S(1)}) custom-call(s32[2,8,16]{2,1,0:T(8,128)S(1)} %broadcast_select_fusion.3.code_ref, bf16[4,128,1024]{2,1,0:T(8,128)(2,1)S(1)} %all-to-all-done.q_ref, bf16[2,16,64,128]{3,2,1,0:T(8,128)(2,1)S(1)} %get-tuple-element.49.pick_ref, ...), custom_call_target="tpu_custom_call" | custom-call | flops 2147483648 | bytes 8388608 | tf_op jit(solution)/shard_map/pallas_call | solution.py:164
  44.4 0.0 collective-permute-done.4.rest_0_
  44.4 0.6 collective-permute-start.9
  45.0 4.2 %collective-permute-start.6 = (bf16[4,2,128,256]{3,2,1,0:T(8,128)(2,1)}, bf16[4,2,128,256]{3,2,1,0:T(8,128)(2,1)S(1)}, u32[]{:S(2)}, u32[]{:S(2)}) collective-permute-start(bf16[4,2,128,256]{3,2,1,0:T(8,128)(2,1)} %collective-permute-done.4.rest_0_), channel_id=1, source_target_pairs={{0,8},{4,12},{8,16},{12,20},{16,24},{20,28},{1,9},{5,13},{9,17},{1... | collective-permute-start | bytes 1572872 | tf_op jit(solution)/shard_map/ppermute | solution.py:296
  49.2 7.5 %shard_map.57 = (f32[16,128,256]{2,1,0:T(8,128)S(1)}, f32[16,16,256]{2,1,0:T(8,128)S(1)}, bf16[16,128]{1,0:T(8,128)(2,1)S(1)}) custom-call(s32[2,8,16]{2,1,0:T(8,128)S(1)} %broadcast_select_fusion.2.code_ref, bf16[4,128,1024]{2,1,0:T(8,128)(2,1)S(1)} %all-to-all-done.q_ref, bf16[2,16,64,128]{3,2,1,0:T(8,128)(2,1)S(1)} %get-tuple-element.53.pick_ref, ...), custom_call_target="tpu_custom_call" | custom-call | flops 2147483648 | bytes 8388608 | tf_op jit(solution)/shard_map/pallas_call | solution.py:164
  56.7 1.7 %collective-permute-done.9.rest_1_ = bf16[4,2,128,256]{3,2,1,0:T(8,128)(2,1)S(1)} collective-permute-done((bf16[4,2,128,256]{3,2,1,0:T(8,128)(2,1)}, bf16[4,2,128,256]{3,2,1,0:T(8,128)(2,1)S(1)}, u32[]{:S(2)}, u32[]{:S(2)}) %collective-permute-start.9) | collective-permute-done | bytes 524320 | tf_op jit(solution)/shard_map/ppermute | solution.py:288
  58.4 2.8 %collective-permute-start.10 = (bf16[4,1,128,256]{3,2,1,0:T(8,128)(2,1)S(1)}, bf16[4,1,128,256]{3,2,1,0:T(8,128)(2,1)S(1)}, u32[]{:S(2)}, u32[]{:S(2)}) collective-permute-start(bf16[4,1,128,256]{3,2,1,0:T(8,128)(2,1)S(1)} %slice.8), channel_id=1, source_target_pairs={{0,8},{4,12},{8,16},{12,20},{16,24},{20,28},{1,9},{5,13},{9,17},{1... | collective-permute-start | bytes 786440 | tf_op jit(solution)/shard_map/ppermute | solution.py:293
  61.3 0.6 collective-permute-start.8
  61.9 7.3 %shard_map.58 = (f32[16,128,256]{2,1,0:T(8,128)S(1)}, f32[16,16,256]{2,1,0:T(8,128)S(1)}, bf16[16,128]{1,0:T(8,128)(2,1)S(1)}) custom-call(s32[2,8,16]{2,1,0:T(8,128)S(1)} %get-tuple-element.59.code_ref, bf16[4,128,1024]{2,1,0:T(8,128)(2,1)S(1)} %all-to-all-done.q_ref, bf16[2,16,64,128]{3,2,1,0:T(8,128)(2,1)S(1)} %get-tuple-element.60.pick_ref, ...), custom_call_target="tpu_custom_call" | custom-call | flops 2147483648 | bytes 8388608 | tf_op jit(solution)/shard_map/pallas_call | solution.py:164
  69.2 0.0 collective-permute-done.8.rest_1_
  69.2 7.8 %shard_map.59 = bf16[4,128,1024]{2,1,0:T(8,128)(2,1)S(1)} custom-call(s32[2,8,16]{2,1,0:T(8,128)S(1)} %get-tuple-element.44.code_ref, bf16[4,128,1024]{2,1,0:T(8,128)(2,1)S(1)} %all-to-all-done.q_ref, bf16[2,16,64,128]{3,2,1,0:T(8,128)(2,1)S(1)} %get-tuple-element.46.pick_ref, bf16[4,2,128,256]{3,2,1,0:T(8,128)(2,1)S(1)} %collective-permute-done.6.rest_0_, ...), custom_call_target="tpu_custom_call" | custom-call | flops 2147483648 | bytes 8388608 | tf_op jit(solution)/shard_map/pallas_call | solution.py:164
  77.1 17.8 %all_to_all.10 = bf16[4,128,1024]{2,1,0:T(8,128)(2,1)S(1)} all-to-all(bf16[4,128,1024]{2,1,0:T(8,128)(2,1)S(1)} %shard_map.59), channel_id=1, replica_groups=mesh['chip'=8,'core'=2,'head'=2] {'head','core'}, dimensions={0} | all-to-all | bytes 2097152 | tf_op jit(solution)/shard_map/all_to_all | solution.py:317
  94.9 0.7 copy.16
  95.6 1.3 %copy.17 = bf16[128,4096]{1,0:T(8,128)(2,1)} copy(bf16[128,4096]{0,1:T(8,128)(2,1)S(1)} %bitcast.19) | data formatting | bytes 2097152 | tf_op jit(solution)/shard_map/reshape | solution.py:318
  (26 shorter events, 0.1 us)
Async XLA Ops:
  0.0 17.6 %copy-start = (s32[4,128]{1,0:T(4,128)S(1)}, s32[4,128]{1,0:T(4,128)}, u32[]{:S(2)}) copy-start(s32[4,128]{1,0:T(4,128)} %param.8) | copy-start | bytes 6148
  2.0 7.2 %collective-permute-start = (bf16[2,128,256]{2,1,0:T(8,128)(2,1)}, bf16[2,128,256]{2,1,0:T(8,128)(2,1)S(1)}, u32[]{:S(2)}, u32[]{:S(2)}) collective-permute-start(bf16[2,128,256]{2,1,0:T(8,128)(2,1)} %get-tuple-element.37), channel_id=1, source_target_pairs={{0,1},{1,0},{2,3},{3,2},{4,5},{5,4},{6,7},{7,6},{8,9},{9,8},{10,11... | collective-permute-start | bytes 393224 | tf_op jit(solution)/shard_map/ppermute | solution.py:212
  4.9 4.2 %collective-permute-start.1 = (bf16[2,128,256]{2,1,0:T(8,128)(2,1)}, bf16[2,128,256]{2,1,0:T(8,128)(2,1)S(1)}, u32[]{:S(2)}, u32[]{:S(2)}) collective-permute-start(bf16[2,128,256]{2,1,0:T(8,128)(2,1)} %get-tuple-element.38), channel_id=1, source_target_pairs={{0,2},{1,3},{2,0},{3,1},{4,6},{5,7},{6,4},{7,5},{8,10},{9,11},{10,... | collective-permute-start | bytes 393224 | tf_op jit(solution)/shard_map/ppermute | solution.py:212
  4.9 6.1 %collective-permute-start.2 = (bf16[2,128,256]{2,1,0:T(8,128)(2,1)}, bf16[2,128,256]{2,1,0:T(8,128)(2,1)S(1)}, u32[]{:S(2)}, u32[]{:S(2)}) collective-permute-start(bf16[2,128,256]{2,1,0:T(8,128)(2,1)} %get-tuple-element.39), channel_id=1, source_target_pairs={{0,3},{1,2},{2,1},{3,0},{4,7},{5,6},{6,5},{7,4},{8,11},{9,10},{10,... | collective-permute-start | bytes 393224 | tf_op jit(solution)/shard_map/ppermute | solution.py:212
  6.1 4.9 %copy-start.1 = (bf16[2,128,256]{2,1,0:T(8,128)(2,1)S(1)}, bf16[2,128,256]{2,1,0:T(8,128)(2,1)}, u32[]{:S(2)}) copy-start(bf16[2,128,256]{2,1,0:T(8,128)(2,1)} %get-tuple-element.36) | copy-start | bytes 393220
  7.8 9.8 %copy-start.2 = (s32[4,64,40]{1,2,0:T(8,128)S(1)}, s32[4,64,40]{1,2,0:T(8,128)}, u32[]{:S(2)}) copy-start(s32[4,64,40]{1,2,0:T(8,128)} %param.9) | copy-start | bytes 122884
  11.9 22.5 %collective-permute-start.5 = (bf16[4,2,128,256]{3,2,1,0:T(8,128)(2,1)}, bf16[4,2,128,256]{3,2,1,0:T(8,128)(2,1)}, u32[]{:S(2)}, u32[]{:S(2)}) collective-permute-start(bf16[4,2,128,256]{3,2,1,0:T(8,128)(2,1)} %pad_maximum_fusion.rest_0_), channel_id=1, source_target_pairs={{0,4},{4,0},{8,12},{12,8},{16,20},{20,16},{24,28},{28,24},{1,5},{5... | collective-permute-start | bytes 1572872 | tf_op jit(solution)/shard_map/ppermute | solution.py:288
  13.3 15.4 %collective-permute-start.3 = (bf16[4,2,128,256]{3,2,1,0:T(8,128)(2,1)}, bf16[4,2,128,256]{3,2,1,0:T(8,128)(2,1)}, u32[]{:S(2)}, u32[]{:S(2)}) collective-permute-start(bf16[4,2,128,256]{3,2,1,0:T(8,128)(2,1)} %pad_maximum_fusion.rest_0_), channel_id=1, source_target_pairs={{0,8},{4,12},{8,16},{12,20},{16,24},{20,28},{1,9},{5,13},{9,17},{1... | collective-permute-start | bytes 1572872 | tf_op jit(solution)/shard_map/ppermute | solution.py:296
  19.0 18.0 %all-to-all-start = ((bf16[4,128,1024]{2,1,0:T(8,128)(2,1)}), bf16[4,128,1024]{2,1,0:T(8,128)(2,1)S(1)}, u32[]{:S(2)}, u32[]{:S(2)}) async-start(bf16[4,128,1024]{2,1,0:T(8,128)(2,1)} %bitcast.14), calls=%async_computation | async-start | bytes 2097152 | tf_op jit(solution)/shard_map/all_to_all | solution.py:277
  28.7 15.7 %collective-permute-start.4 = (bf16[4,2,128,256]{3,2,1,0:T(8,128)(2,1)}, bf16[4,2,128,256]{3,2,1,0:T(8,128)(2,1)}, u32[]{:S(2)}, u32[]{:S(2)}) collective-permute-start(bf16[4,2,128,256]{3,2,1,0:T(8,128)(2,1)} %collective-permute-done.3.rest_0_), channel_id=1, source_target_pairs={{0,8},{4,12},{8,16},{12,20},{16,24},{20,28},{1,9},{5,13},{9,17},{1... | collective-permute-start | bytes 1572872 | tf_op jit(solution)/shard_map/ppermute | solution.py:296
  33.9 15.3 %collective-permute-start.7 = (bf16[4,2,128,256]{3,2,1,0:T(8,128)(2,1)}, bf16[4,2,128,256]{3,2,1,0:T(8,128)(2,1)}, u32[]{:S(2)}, u32[]{:S(2)}) collective-permute-start(bf16[4,2,128,256]{3,2,1,0:T(8,128)(2,1)} %collective-permute-done.3.rest_0_), channel_id=1, source_target_pairs={{0,4},{4,0},{8,12},{12,8},{16,20},{20,16},{24,28},{28,24},{1,5},{5... | collective-permute-start | bytes 1572872 | tf_op jit(solution)/shard_map/ppermute | solution.py:288
  44.4 14.0 %collective-permute-start.9 = (bf16[4,2,128,256]{3,2,1,0:T(8,128)(2,1)}, bf16[4,2,128,256]{3,2,1,0:T(8,128)(2,1)S(1)}, u32[]{:S(2)}, u32[]{:S(2)}) collective-permute-start(bf16[4,2,128,256]{3,2,1,0:T(8,128)(2,1)} %collective-permute-done.4.rest_0_), channel_id=1, source_target_pairs={{0,4},{4,0},{8,12},{12,8},{16,20},{20,16},{24,28},{28,24},{1,5},{5... | collective-permute-start | bytes 1572872 | tf_op jit(solution)/shard_map/ppermute | solution.py:288
  45.0 16.3 %collective-permute-start.6 = (bf16[4,2,128,256]{3,2,1,0:T(8,128)(2,1)}, bf16[4,2,128,256]{3,2,1,0:T(8,128)(2,1)S(1)}, u32[]{:S(2)}, u32[]{:S(2)}) collective-permute-start(bf16[4,2,128,256]{3,2,1,0:T(8,128)(2,1)} %collective-permute-done.4.rest_0_), channel_id=1, source_target_pairs={{0,8},{4,12},{8,16},{12,20},{16,24},{20,28},{1,9},{5,13},{9,17},{1... | collective-permute-start | bytes 1572872 | tf_op jit(solution)/shard_map/ppermute | solution.py:296
  58.4 10.8 %collective-permute-start.10 = (bf16[4,1,128,256]{3,2,1,0:T(8,128)(2,1)S(1)}, bf16[4,1,128,256]{3,2,1,0:T(8,128)(2,1)S(1)}, u32[]{:S(2)}, u32[]{:S(2)}) collective-permute-start(bf16[4,1,128,256]{3,2,1,0:T(8,128)(2,1)S(1)} %slice.8), channel_id=1, source_target_pairs={{0,8},{4,12},{8,16},{12,20},{16,24},{20,28},{1,9},{5,13},{9,17},{1... | collective-permute-start | bytes 786440 | tf_op jit(solution)/shard_map/ppermute | solution.py:293
  61.3 8.0 %collective-permute-start.8 = (bf16[4,1,128,256]{3,2,1,0:T(8,128)(2,1)S(1)}, bf16[4,1,128,256]{3,2,1,0:T(8,128)(2,1)S(1)}, u32[]{:S(2)}, u32[]{:S(2)}) collective-permute-start(bf16[4,1,128,256]{3,2,1,0:T(8,128)(2,1)S(1)} %slice.6), channel_id=1, source_target_pairs={{0,4},{4,0},{8,12},{12,8},{16,20},{20,16},{24,28},{28,24},{1,5},{5... | collective-permute-start | bytes 786440 | tf_op jit(solution)/shard_map/ppermute | solution.py:292

commit v8 on v7

--- a/solution.py
+++ b/solution.py
@@ -19,7 +19,7 @@
     head_dim = o_refs[0].shape[2] - width
     for m, o_ref in enumerate(o_refs):
         device = lax.bitwise_xor(me_ref[0], m)
-        first = (lax.rem(device, 2) * 2 + lax.div(device, 2)) * mine
+        first = way_of(device) * mine
         for h in range(mine):
             columns = pl.ds(pl.multiple_of((first + h) * head_dim, head_dim), head_dim)
             o_ref[h, :, :head_dim] = k_ref[:, columns]
@@ -35,6 +35,32 @@
         in_specs=[pl.BlockSpec(memory_space=pltpu.SMEM), vmem, vmem],
         out_specs=[vmem] * 4,
     )(me, keys, values)
+
+
+def way_of(device):
+    return lax.rem(device, 2) * 2 + lax.div(device, 2)
+
+
+def collect_kernel(me_ref, own_ref, *rest):
+    pieces, out_ref = rest[:3], rest[3]
+    width = own_ref.shape[2]
+    me = me_ref[0]
+    for m in range(4):
+        way = way_of(lax.bitwise_xor(me, m))
+        columns = pl.ds(pl.multiple_of(way * width, width), width)
+        out_ref[:, columns] = own_ref[way] if m == 0 else pieces[m - 1][...]
+
+
+def collect(me, own, pieces):
+    ways, tok, width = own.shape
+    vmem = pl.BlockSpec(memory_space=pltpu.VMEM)
+    return pl.pallas_call(
+        collect_kernel,
+        out_shape=jax.ShapeDtypeStruct((tok, ways * width), own.dtype),
+        compiler_params=pltpu.CompilerParams(vmem_limit_bytes=8 << 20),
+        in_specs=[pl.BlockSpec(memory_space=pltpu.SMEM)] + [vmem] * 4,
+        out_specs=vmem,
+    )(me, own, *pieces)
 
 
 def step_kernel(code_ref, q_ref, pick_ref, *rest, parts, first, last, span, head_dim, group):
@@ -207,7 +233,8 @@
 
     if relative:
         me = lax.axis_index("core") * 2 + lax.axis_index("head")
-        pieces = arrange(me[None].astype(jnp.int32), keys, values, mine, head_dim)
+        me = me.astype(jnp.int32)
+        pieces = arrange(me[None], keys, values, mine, head_dim)
         pair = [pieces[0]] + [
             lax.ppermute(pieces[m], ("core", "head"), [(i, i ^ m) for i in range(4)])
             for m in (1, 3, 2)
@@ -275,12 +302,13 @@
         code, query = lax.optimization_barrier((tables[0][0], query))
         tables[0] = (code, tables[0][1])
         query = swap(query).reshape(-1, max(tok, BLK), q_width // ways)
+        outward = [((me ^ m) & 1) * 2 + ((me ^ m) >> 1) for m in (1, 3, 2)]
         part, waiting = pair, None
         for n in range(final + 2):
             fetched = None
             if n <= final:
                 if n == 1:
-                    part, tables = lax.optimization_barrier((part, tables))
+                    part, tables, outward = lax.optimization_barrier((part, tables, outward))
                 if state is not None:
                     part, mark = lax.optimization_barrier((part, state[2]))
                     state = state[:2] + (mark,)
@@ -314,6 +342,15 @@
             part = rows[g : g + many].reshape((many * each,) + rows.shape[2:])
             state = attend(query, masks(order[g : g + many]), ((part,),), state, g + many == groups)
 
+    if relative:
+        pieces = {}
+        zero = jnp.zeros((), jnp.int32)
+        for m, way in zip((1, 3, 2), outward):
+            piece = lax.dynamic_slice(
+                state, (way, zero, zero), (1,) + state.shape[1:], allow_negative_indices=False
+            )[0]
+            pieces[m] = lax.ppermute(piece, ("core", "head"), [(i, i ^ m) for i in range(4)])
+        return collect(me[None], state, [pieces[m] for m in (1, 2, 3)])
     out = swap(state.reshape(ways, tok, q_width // ways))
     return out.transpose(1, 0, 2).reshape(tok, q_width)
 

time: 97.3 us -> 92.7 us (0.953)
  blocking collectives: 17.8 us -> 0 us
  waiting for transfers between devices: 7.86 us -> 19.6 us
  starting transfers between devices: 26.2 us -> 28.8 us
  local copies, waits for them, and re-layouts: 5.65 us -> 3.72 us
    all_to_all x1 -> x0, blocking collectives: 17.8 us -> none  [body(): out = swap(state.reshape(ways, tok, q_width // ways))]
    ppermute x0 -> x3, waiting for transfers between devices: none -> 11.8 us  [body(): lax.ppermute(piece, ('core', 'head'), [(i, i ^ m) for i in range(4)])]
    ppermute x0 -> x3, starting transfers between devices: none -> 2.52 us  [body(): lax.ppermute(piece, ('core', 'head'), [(i, i ^ m) for i in range(4)])]
    reshape x1 -> x0, local copies, waits for them, and re-layouts: 1.31 us -> none  [body(): return out.transpose(1, 0, 2).reshape(tok, q_width)]
    pallas_call x0 -> x1, Pallas kernels: none -> 1.04 us  [collect(): pl.pallas_call(collect_kernel, out_shape=jax.ShapeDtypeStruct((tok, ways...]
  transfers between devices with their start and end apart: 12 -> 15, of which waited for: 4 -> 6; matrix products, arithmetic and copies ran while one was open for 10% -> 11% of each run, Pallas kernels for 23% -> 24%
where the time goes in v8:
time: 92.7 us; the launch traced here: 92.4 us
  Pallas kernels  33 us (36%)
  starting transfers between devices  28.8 us (31%)
  waiting for transfers between devices  19.6 us (21%)
  other arithmetic  7.01 us (8%)
  local copies, waits for them, and re-layouts  3.72 us (4%)
    pallas_call x4, Pallas kernels, attend_step(): pl.pallas_call(functools.partial(step_kernel, parts=tuple((len(part) for...  30 us
    ppermute x3, starting transfers between devices, body(): part = lax.ppermute(part, 'chip', up) if n < final else None  13.6 us
    ppermute x3, waiting for transfers between devices, body(): lax.ppermute(piece, ('core', 'head'), [(i, i ^ m) for i in range(4)])  11.8 us
    all_to_all x1, starting transfers between devices, body(): query = swap(query).reshape(-1, max(tok, BLK), q_width // ways)  3.53 us
    ppermute x3, starting transfers between devices, body(): lax.ppermute(pieces[m], ('core', 'head'), [(i, i ^ m) for i in range(4)])  3.08 us
    reduce_and x1, other arithmetic, masks(): hidden = jnp.all(vertical[:, None, None, :] != position[..., None], axis=3)  2.92 us
    ppermute x1, starting transfers between devices, body(): lax.ppermute(waiting[1][0][:, cut:], 'chip', up)  2.84 us
    ppermute x3, starting transfers between devices, body(): other = (lax.ppermute(part, 'chip', across),)  2.56 us
  transfers between devices with their start and end apart: 15, of which 6 were waited for; matrix products, arithmetic and copies ran while one was open for 11% of the time, Pallas kernels for 24%

profile of v8, /device:TPU:0, one launch (start us, length us, event | category | flops | bytes accessed | tf_op | source)
XLA Modules:
  0.0 92.4 jit_solution(14052277672345842451)
XLA Ops:
  0.0 2.0 %shard_map.55 = (bf16[2,128,256]{2,1,0:T(8,128)(2,1)}, bf16[2,128,256]{2,1,0:T(8,128)(2,1)}, bf16[2,128,256]{2,1,0:T(8,128)(2,1)}, bf16[2,128,256]{2,1,0:T(8,128)(2,1)}) custom-call(s32[1]{0:T(128)} %bitcast.me_ref, bf16[128,1024]{1,0:T(8,128)(2,1)} %k_ref.1, bf16[128,1024]{1,0:T(8,128)(2,1)} %v_ref.1), custom_call_target="tpu_custom_call" | custom-call | tf_op jit(solution)/shard_map/pallas_call | solution.py:32
  2.0 3.0 %collective-permute-start = (bf16[2,128,256]{2,1,0:T(8,128)(2,1)}, bf16[2,128,256]{2,1,0:T(8,128)(2,1)S(1)}, u32[]{:S(2)}, u32[]{:S(2)}) collective-permute-start(bf16[2,128,256]{2,1,0:T(8,128)(2,1)} %get-tuple-element.40), channel_id=1, source_target_pairs={{0,1},{1,0},{2,3},{3,2},{4,5},{5,4},{6,7},{7,6},{8,9},{9,8},{10,11... | collective-permute-start | bytes 393224 | tf_op jit(solution)/shard_map/ppermute | solution.py:239
  4.9 0.1 collective-permute-start.2
  5.1 0.1 add_multiply_fusion
  5.1 0.1 iota_add_fusion.4
  5.2 0.1 add.320
  5.3 0.1 add.326
  5.4 0.1 fusion
  5.5 0.1 broadcast_add_fusion.3
  5.6 0.1 add.323
  5.6 0.1 add.335
  5.7 0.1 add.343
  5.8 0.1 add.351
  5.9 0.1 select_select_fusion
  6.0 0.1 iota_add_fusion.2
  6.1 0.1 iota_add_fusion
  6.1 1.7 %copy.12 = bf16[128,4096]{0,1:T(8,128)(2,1)S(1)} copy(bf16[128,4096]{1,0:T(8,128)(2,1)} %param.5) | data formatting | bytes 2097152 | tf_op args[0]
  7.8 1.3 %copy.13 = bf16[128,4,1024]{2,0,1:T(8,128)(2,1)} copy(bf16[128,4,1024]{0,2,1:T(8,128)(2,1)S(1)} %bitcast.22) | data formatting | bytes 2097152 | tf_op jit(solution)/shard_map/reshape | solution.py:249
  9.1 0.0 collective-permute-done
  9.2 1.8 %collective-permute-done.2 = bf16[2,128,256]{2,1,0:T(8,128)(2,1)S(1)} collective-permute-done((bf16[2,128,256]{2,1,0:T(8,128)(2,1)}, bf16[2,128,256]{2,1,0:T(8,128)(2,1)S(1)}, u32[]{:S(2)}, u32[]{:S(2)}) %collective-permute-start.2) | collective-permute-done | bytes 131104 | tf_op jit(solution)/shard_map/ppermute | solution.py:239
  11.0 0.8 pad_maximum_fusion.rest_0_
  11.9 1.4 %collective-permute-start.5 = (bf16[4,2,128,256]{3,2,1,0:T(8,128)(2,1)}, bf16[4,2,128,256]{3,2,1,0:T(8,128)(2,1)}, u32[]{:S(2)}, u32[]{:S(2)}) collective-permute-start(bf16[4,2,128,256]{3,2,1,0:T(8,128)(2,1)} %pad_maximum_fusion.rest_0_), channel_id=1, source_target_pairs={{0,4},{4,0},{8,12},{12,8},{16,20},{20,16},{24,28},{28,24},{1,5},{5... | collective-permute-start | bytes 1572872 | tf_op jit(solution)/shard_map/ppermute | solution.py:316
  13.3 4.3 %collective-permute-start.3 = (bf16[4,2,128,256]{3,2,1,0:T(8,128)(2,1)}, bf16[4,2,128,256]{3,2,1,0:T(8,128)(2,1)}, u32[]{:S(2)}, u32[]{:S(2)}) collective-permute-start(bf16[4,2,128,256]{3,2,1,0:T(8,128)(2,1)} %pad_maximum_fusion.rest_0_), channel_id=1, source_target_pairs={{0,8},{4,12},{8,16},{12,20},{16,24},{20,28},{1,9},{5,13},{9,17},{1... | collective-permute-start | bytes 1572872 | tf_op jit(solution)/shard_map/ppermute | solution.py:324
  17.6 0.1 copy.10
  17.7 1.2 %compare_reduce_fusion.4 = (pred[2,8,16]{2,1,0:T(8,128)(4,1)S(1)}, pred[2,8,16]{2,1,0:T(8,128)(4,1)S(1)}, pred[2,8,16]{2,1,0:T(8,128)(4,1)S(1)}, pred[2,8,16]{2,1,0:T(8,128)(4,1)S(1)}) fusion(s32[2,8,40]{2,1,0:T(8,128)S(1)} %bitcast.27, s32[16]{0:T(128)S(1)} %add.351, s32[16]{0:T(128)S(1)} %add.335, s32[16]{0:T(128)S(1)} %add.343, s32[16]{0:T(128)S(1)} %add.323), kind=kLoop, calls=%fused_computation.12 | loop fusion | flops 80896 | bytes 3840 | tf_op jit(solution)/shard_map/reduce_or | solution.py:273
  19.0 3.5 %all-to-all-start = ((bf16[4,128,1024]{2,1,0:T(8,128)(2,1)}), bf16[4,128,1024]{2,1,0:T(8,128)(2,1)S(1)}, u32[]{:S(2)}, u32[]{:S(2)}) async-start(bf16[4,128,1024]{2,1,0:T(8,128)(2,1)} %bitcast.14), calls=%async_computation | async-start | bytes 2097152 | tf_op jit(solution)/shard_map/all_to_all | solution.py:304
  22.5 2.9 %compare_reduce_fusion = (pred[2,16,64]{2,1,0:T(8,128)(4,1)S(1)}, pred[2,16,64]{2,1,0:T(8,128)(4,1)S(1)}, pred[2,16,64]{2,1,0:T(8,128)(4,1)S(1)}, pred[2,16,64]{2,1,0:T(8,128)(4,1)S(1)}) fusion(s32[16,64]{1,0:T(8,128)S(1)} %get-tuple-element.103, s32[2,128]{1,0:T(2,128)S(1)} %constant_dynamic-slice_fusion, s32[16,64]{1,0:T(8,128)S(1)} %get-tuple-element.105, ...), kind=kLoop, calls=%fused_computation.1 | loop fusion | flops 2088960 | bytes 25600 | tf_op jit(solution)/shard_map/reduce_and | solution.py:281
  25.5 1.4 %and_convert_fusion = (bf16[2,16,64,128]{3,2,1,0:T(8,128)(2,1)S(1)}, bf16[2,16,64,128]{3,2,1,0:T(8,128)(2,1)S(1)}, bf16[2,16,64,128]{3,2,1,0:T(8,128)(2,1)S(1)}, bf16[2,16,64,128]{3,2,1,0:T(8,128)(2,1)S(1)}) fusion(pred[2,16,64]{2,1,0:T(8,128)(4,1)S(1)} %get-tuple-element.77, pred[128]{0:T(512)(128)(4,1)S(1)} %iota_compare_fusion, ...), kind=kLoop, calls=%fused_computation | loop fusion | flops 2097152 | bytes 2105472 | tf_op jit(solution)/shard_map/convert_element_type | solution.py:283
  26.9 1.8 %collective-permute-done.3.rest_0_ = bf16[4,2,128,256]{3,2,1,0:T(8,128)(2,1)} collective-permute-done((bf16[4,2,128,256]{3,2,1,0:T(8,128)(2,1)}, bf16[4,2,128,256]{3,2,1,0:T(8,128)(2,1)}, u32[]{:S(2)}, u32[]{:S(2)}) %collective-permute-start.3) | collective-permute-done | bytes 524320 | tf_op jit(solution)/shard_map/ppermute | solution.py:324
  28.7 5.2 %collective-permute-start.4 = (bf16[4,2,128,256]{3,2,1,0:T(8,128)(2,1)}, bf16[4,2,128,256]{3,2,1,0:T(8,128)(2,1)}, u32[]{:S(2)}, u32[]{:S(2)}) collective-permute-start(bf16[4,2,128,256]{3,2,1,0:T(8,128)(2,1)} %collective-permute-done.3.rest_0_), channel_id=1, source_target_pairs={{0,8},{4,12},{8,16},{12,20},{16,24},{20,28},{1,9},{5,13},{9,17},{1... | collective-permute-start | bytes 1572872 | tf_op jit(solution)/shard_map/ppermute | solution.py:324
  33.9 0.5 collective-permute-start.7
  34.4 2.6 %all-to-all-done.q_ref = bf16[4,128,1024]{2,1,0:T(8,128)(2,1)S(1)} async-done(((bf16[4,128,1024]{2,1,0:T(8,128)(2,1)}), bf16[4,128,1024]{2,1,0:T(8,128)(2,1)S(1)}, u32[]{:S(2)}, u32[]{:S(2)}) %all-to-all-start) | async-done | bytes 1048608 | tf_op jit(solution)/shard_map/all_to_all | solution.py:304
  37.0 7.4 %shard_map.56 = (f32[16,128,256]{2,1,0:T(8,128)S(1)}, f32[16,16,256]{2,1,0:T(8,128)S(1)}, bf16[16,128]{1,0:T(8,128)(2,1)S(1)}) custom-call(s32[2,8,16]{2,1,0:T(8,128)S(1)} %broadcast_select_fusion.3.code_ref, bf16[4,128,1024]{2,1,0:T(8,128)(2,1)S(1)} %all-to-all-done.q_ref, bf16[2,16,64,128]{3,2,1,0:T(8,128)(2,1)S(1)} %get-tuple-element.52.pick_ref, ...), custom_call_target="tpu_custom_call" | custom-call | flops 2147483648 | bytes 8388608 | tf_op jit(solution)/shard_map/pallas_call | solution.py:190
  44.4 0.6 collective-permute-start.9
  45.0 4.1 %collective-permute-start.6 = (bf16[4,2,128,256]{3,2,1,0:T(8,128)(2,1)}, bf16[4,2,128,256]{3,2,1,0:T(8,128)(2,1)S(1)}, u32[]{:S(2)}, u32[]{:S(2)}) collective-permute-start(bf16[4,2,128,256]{3,2,1,0:T(8,128)(2,1)} %collective-permute-done.4.rest_0_), channel_id=1, source_target_pairs={{0,8},{4,12},{8,16},{12,20},{16,24},{20,28},{1,9},{5,13},{9,17},{1... | collective-permute-start | bytes 1572872 | tf_op jit(solution)/shard_map/ppermute | solution.py:324
  49.1 7.5 %shard_map.57 = (f32[16,128,256]{2,1,0:T(8,128)S(1)}, f32[16,16,256]{2,1,0:T(8,128)S(1)}, bf16[16,128]{1,0:T(8,128)(2,1)S(1)}) custom-call(s32[2,8,16]{2,1,0:T(8,128)S(1)} %broadcast_select_fusion.2.code_ref, bf16[4,128,1024]{2,1,0:T(8,128)(2,1)S(1)} %all-to-all-done.q_ref, bf16[2,16,64,128]{3,2,1,0:T(8,128)(2,1)S(1)} %get-tuple-element.56.pick_ref, ...), custom_call_target="tpu_custom_call" | custom-call | flops 2147483648 | bytes 8388608 | tf_op jit(solution)/shard_map/pallas_call | solution.py:190
  56.7 1.7 %collective-permute-done.9.rest_1_ = bf16[4,2,128,256]{3,2,1,0:T(8,128)(2,1)S(1)} collective-permute-done((bf16[4,2,128,256]{3,2,1,0:T(8,128)(2,1)}, bf16[4,2,128,256]{3,2,1,0:T(8,128)(2,1)S(1)}, u32[]{:S(2)}, u32[]{:S(2)}) %collective-permute-start.9) | collective-permute-done | bytes 524320 | tf_op jit(solution)/shard_map/ppermute | solution.py:316
  58.3 2.8 %collective-permute-start.10 = (bf16[4,1,128,256]{3,2,1,0:T(8,128)(2,1)S(1)}, bf16[4,1,128,256]{3,2,1,0:T(8,128)(2,1)S(1)}, u32[]{:S(2)}, u32[]{:S(2)}) collective-permute-start(bf16[4,1,128,256]{3,2,1,0:T(8,128)(2,1)S(1)} %slice.8), channel_id=1, source_target_pairs={{0,8},{4,12},{8,16},{12,20},{16,24},{20,28},{1,9},{5,13},{9,17},{1... | collective-permute-start | bytes 786440 | tf_op jit(solution)/shard_map/ppermute | solution.py:321
  61.2 0.6 collective-permute-start.8
  61.8 7.4 %shard_map.58 = (f32[16,128,256]{2,1,0:T(8,128)S(1)}, f32[16,16,256]{2,1,0:T(8,128)S(1)}, bf16[16,128]{1,0:T(8,128)(2,1)S(1)}) custom-call(s32[2,8,16]{2,1,0:T(8,128)S(1)} %get-tuple-element.62.code_ref, bf16[4,128,1024]{2,1,0:T(8,128)(2,1)S(1)} %all-to-all-done.q_ref, bf16[2,16,64,128]{3,2,1,0:T(8,128)(2,1)S(1)} %get-tuple-element.63.pick_ref, ...), custom_call_target="tpu_custom_call" | custom-call | flops 2147483648 | bytes 8388608 | tf_op jit(solution)/shard_map/pallas_call | solution.py:190
  69.2 7.7 %shard_map.59.own_ref = bf16[4,128,1024]{2,1,0:T(8,128)(2,1)S(1)} custom-call(s32[2,8,16]{2,1,0:T(8,128)S(1)} %get-tuple-element.47.code_ref, bf16[4,128,1024]{2,1,0:T(8,128)(2,1)S(1)} %all-to-all-done.q_ref, bf16[2,16,64,128]{3,2,1,0:T(8,128)(2,1)S(1)} %get-tuple-element.49.pick_ref, bf16[4,2,128,256]{3,2,1,0:T(8,128)(2,1)S(1)} %collective-permute-done.6.rest_0_, ...), custom_call_target="tpu_custom_call" | custom-call | flops 2147483648 | bytes 8388608 | tf_op jit(solution)/shard_map/pallas_call | solution.py:190
  77.0 0.1 dynamic-slice_bitcast_fusion
  77.0 0.1 collective-permute-start.13
  77.1 2.4 %collective-permute-start.12 = (bf16[128,1024]{1,0:T(8,128)(2,1)S(1)}, bf16[128,1024]{1,0:T(8,128)(2,1)S(1)}, u32[]{:S(2)}, u32[]{:S(2)}) collective-permute-start(bf16[128,1024]{1,0:T(8,128)(2,1)S(1)} %get-tuple-element.84), channel_id=1, source_target_pairs={{0,2},{1,3},{2,0},{3,1},{4,6},{5,7},{6,4},{7,5},{8,10},{9,11},{10,... | collective-permute-start | bytes 786440 | tf_op jit(solution)/shard_map/ppermute | solution.py:352
  79.5 0.0 collective-permute-start.11
  79.5 5.3 %collective-permute-done.13.rest_2_ = bf16[128,1024]{1,0:T(8,128)(2,1)S(1)} collective-permute-done((bf16[128,1024]{1,0:T(8,128)(2,1)S(1)}, bf16[128,1024]{1,0:T(8,128)(2,1)S(1)}, u32[]{:S(2)}, u32[]{:S(2)}) %collective-permute-start.13) | collective-permute-done | bytes 262176 | tf_op jit(solution)/shard_map/ppermute | solution.py:352
  84.9 6.5 %collective-permute-done.11.rest_0_ = bf16[128,1024]{1,0:T(8,128)(2,1)S(1)} collective-permute-done((bf16[128,1024]{1,0:T(8,128)(2,1)S(1)}, bf16[128,1024]{1,0:T(8,128)(2,1)S(1)}, u32[]{:S(2)}, u32[]{:S(2)}) %collective-permute-start.11) | collective-permute-done | bytes 262176 | tf_op jit(solution)/shard_map/ppermute | solution.py:352
  91.3 1.0 %shard_map.60 = bf16[128,4096]{1,0:T(8,128)(2,1)} custom-call(s32[1]{0:T(128)} %bitcast.me_ref, bf16[4,128,1024]{2,1,0:T(8,128)(2,1)S(1)} %shard_map.59.own_ref, bf16[128,1024]{1,0:T(8,128)(2,1)S(1)} %collective-permute-done.11.rest_0_, bf16[128,1024]{1,0:T(8,128)(2,1)S(1)} %collective-permute-done.12.rest_1_, ...), custom_call_target="tpu_custom_call" | custom-call | tf_op jit(solution)/shard_map/pallas_call | solution.py:57
  (31 shorter events, 0.2 us)
Async XLA Ops:
  0.0 17.6 %copy-start = (s32[4,128]{1,0:T(4,128)S(1)}, s32[4,128]{1,0:T(4,128)}, u32[]{:S(2)}) copy-start(s32[4,128]{1,0:T(4,128)} %param.8) | copy-start | bytes 6148
  2.0 7.2 %collective-permute-start = (bf16[2,128,256]{2,1,0:T(8,128)(2,1)}, bf16[2,128,256]{2,1,0:T(8,128)(2,1)S(1)}, u32[]{:S(2)}, u32[]{:S(2)}) collective-permute-start(bf16[2,128,256]{2,1,0:T(8,128)(2,1)} %get-tuple-element.40), channel_id=1, source_target_pairs={{0,1},{1,0},{2,3},{3,2},{4,5},{5,4},{6,7},{7,6},{8,9},{9,8},{10,11... | collective-permute-start | bytes 393224 | tf_op jit(solution)/shard_map/ppermute | solution.py:239
  4.9 4.2 %collective-permute-start.1 = (bf16[2,128,256]{2,1,0:T(8,128)(2,1)}, bf16[2,128,256]{2,1,0:T(8,128)(2,1)S(1)}, u32[]{:S(2)}, u32[]{:S(2)}) collective-permute-start(bf16[2,128,256]{2,1,0:T(8,128)(2,1)} %get-tuple-element.41), channel_id=1, source_target_pairs={{0,2},{1,3},{2,0},{3,1},{4,6},{5,7},{6,4},{7,5},{8,10},{9,11},{10,... | collective-permute-start | bytes 393224 | tf_op jit(solution)/shard_map/ppermute | solution.py:239
  4.9 6.1 %collective-permute-start.2 = (bf16[2,128,256]{2,1,0:T(8,128)(2,1)}, bf16[2,128,256]{2,1,0:T(8,128)(2,1)S(1)}, u32[]{:S(2)}, u32[]{:S(2)}) collective-permute-start(bf16[2,128,256]{2,1,0:T(8,128)(2,1)} %get-tuple-element.42), channel_id=1, source_target_pairs={{0,3},{1,2},{2,1},{3,0},{4,7},{5,6},{6,5},{7,4},{8,11},{9,10},{10,... | collective-permute-start | bytes 393224 | tf_op jit(solution)/shard_map/ppermute | solution.py:239
  6.1 4.9 %copy-start.1 = (bf16[2,128,256]{2,1,0:T(8,128)(2,1)S(1)}, bf16[2,128,256]{2,1,0:T(8,128)(2,1)}, u32[]{:S(2)}) copy-start(bf16[2,128,256]{2,1,0:T(8,128)(2,1)} %get-tuple-element.39) | copy-start | bytes 393220
  7.8 9.8 %copy-start.2 = (s32[4,64,40]{1,2,0:T(8,128)S(1)}, s32[4,64,40]{1,2,0:T(8,128)}, u32[]{:S(2)}) copy-start(s32[4,64,40]{1,2,0:T(8,128)} %param.9) | copy-start | bytes 122884
  11.9 22.5 %collective-permute-start.5 = (bf16[4,2,128,256]{3,2,1,0:T(8,128)(2,1)}, bf16[4,2,128,256]{3,2,1,0:T(8,128)(2,1)}, u32[]{:S(2)}, u32[]{:S(2)}) collective-permute-start(bf16[4,2,128,256]{3,2,1,0:T(8,128)(2,1)} %pad_maximum_fusion.rest_0_), channel_id=1, source_target_pairs={{0,4},{4,0},{8,12},{12,8},{16,20},{20,16},{24,28},{28,24},{1,5},{5... | collective-permute-start | bytes 1572872 | tf_op jit(solution)/shard_map/ppermute | solution.py:316
  13.3 15.4 %collective-permute-start.3 = (bf16[4,2,128,256]{3,2,1,0:T(8,128)(2,1)}, bf16[4,2,128,256]{3,2,1,0:T(8,128)(2,1)}, u32[]{:S(2)}, u32[]{:S(2)}) collective-permute-start(bf16[4,2,128,256]{3,2,1,0:T(8,128)(2,1)} %pad_maximum_fusion.rest_0_), channel_id=1, source_target_pairs={{0,8},{4,12},{8,16},{12,20},{16,24},{20,28},{1,9},{5,13},{9,17},{1... | collective-permute-start | bytes 1572872 | tf_op jit(solution)/shard_map/ppermute | solution.py:324
  19.0 18.0 %all-to-all-start = ((bf16[4,128,1024]{2,1,0:T(8,128)(2,1)}), bf16[4,128,1024]{2,1,0:T(8,128)(2,1)S(1)}, u32[]{:S(2)}, u32[]{:S(2)}) async-start(bf16[4,128,1024]{2,1,0:T(8,128)(2,1)} %bitcast.14), calls=%async_computation | async-start | bytes 2097152 | tf_op jit(solution)/shard_map/all_to_all | solution.py:304
  28.7 15.7 %collective-permute-start.4 = (bf16[4,2,128,256]{3,2,1,0:T(8,128)(2,1)}, bf16[4,2,128,256]{3,2,1,0:T(8,128)(2,1)}, u32[]{:S(2)}, u32[]{:S(2)}) collective-permute-start(bf16[4,2,128,256]{3,2,1,0:T(8,128)(2,1)} %collective-permute-done.3.rest_0_), channel_id=1, source_target_pairs={{0,8},{4,12},{8,16},{12,20},{16,24},{20,28},{1,9},{5,13},{9,17},{1... | collective-permute-start | bytes 1572872 | tf_op jit(solution)/shard_map/ppermute | solution.py:324
  33.9 15.3 %collective-permute-start.7 = (bf16[4,2,128,256]{3,2,1,0:T(8,128)(2,1)}, bf16[4,2,128,256]{3,2,1,0:T(8,128)(2,1)}, u32[]{:S(2)}, u32[]{:S(2)}) collective-permute-start(bf16[4,2,128,256]{3,2,1,0:T(8,128)(2,1)} %collective-permute-done.3.rest_0_), channel_id=1, source_target_pairs={{0,4},{4,0},{8,12},{12,8},{16,20},{20,16},{24,28},{28,24},{1,5},{5... | collective-permute-start | bytes 1572872 | tf_op jit(solution)/shard_map/ppermute | solution.py:316
  44.4 13.9 %collective-permute-start.9 = (bf16[4,2,128,256]{3,2,1,0:T(8,128)(2,1)}, bf16[4,2,128,256]{3,2,1,0:T(8,128)(2,1)S(1)}, u32[]{:S(2)}, u32[]{:S(2)}) collective-permute-start(bf16[4,2,128,256]{3,2,1,0:T(8,128)(2,1)} %collective-permute-done.4.rest_0_), channel_id=1, source_target_pairs={{0,4},{4,0},{8,12},{12,8},{16,20},{20,16},{24,28},{28,24},{1,5},{5... | collective-permute-start | bytes 1572872 | tf_op jit(solution)/shard_map/ppermute | solution.py:316
  45.0 16.2 %collective-permute-start.6 = (bf16[4,2,128,256]{3,2,1,0:T(8,128)(2,1)}, bf16[4,2,128,256]{3,2,1,0:T(8,128)(2,1)S(1)}, u32[]{:S(2)}, u32[]{:S(2)}) collective-permute-start(bf16[4,2,128,256]{3,2,1,0:T(8,128)(2,1)} %collective-permute-done.4.rest_0_), channel_id=1, source_target_pairs={{0,8},{4,12},{8,16},{12,20},{16,24},{20,28},{1,9},{5,13},{9,17},{1... | collective-permute-start | bytes 1572872 | tf_op jit(solution)/shard_map/ppermute | solution.py:324
  58.3 10.9 %collective-permute-start.10 = (bf16[4,1,128,256]{3,2,1,0:T(8,128)(2,1)S(1)}, bf16[4,1,128,256]{3,2,1,0:T(8,128)(2,1)S(1)}, u32[]{:S(2)}, u32[]{:S(2)}) collective-permute-start(bf16[4,1,128,256]{3,2,1,0:T(8,128)(2,1)S(1)} %slice.8), channel_id=1, source_target_pairs={{0,8},{4,12},{8,16},{12,20},{16,24},{20,28},{1,9},{5,13},{9,17},{1... | collective-permute-start | bytes 786440 | tf_op jit(solution)/shard_map/ppermute | solution.py:321
  61.2 8.0 %collective-permute-start.8 = (bf16[4,1,128,256]{3,2,1,0:T(8,128)(2,1)S(1)}, bf16[4,1,128,256]{3,2,1,0:T(8,128)(2,1)S(1)}, u32[]{:S(2)}, u32[]{:S(2)}) collective-permute-start(bf16[4,1,128,256]{3,2,1,0:T(8,128)(2,1)S(1)} %slice.6), channel_id=1, source_target_pairs={{0,4},{4,0},{8,12},{12,8},{16,20},{20,16},{24,28},{28,24},{1,5},{5... | collective-permute-start | bytes 786440 | tf_op jit(solution)/shard_map/ppermute | solution.py:320
  77.0 7.8 %collective-permute-start.13 = (bf16[128,1024]{1,0:T(8,128)(2,1)S(1)}, bf16[128,1024]{1,0:T(8,128)(2,1)S(1)}, u32[]{:S(2)}, u32[]{:S(2)}) collective-permute-start(bf16[128,1024]{1,0:T(8,128)(2,1)S(1)} %get-tuple-element.83), channel_id=1, source_target_pairs={{0,3},{1,2},{2,1},{3,0},{4,7},{5,6},{6,5},{7,4},{8,11},{9,10},{10,... | collective-permute-start | bytes 786440 | tf_op jit(solution)/shard_map/ppermute | solution.py:352
  77.1 7.8 %collective-permute-start.12 = (bf16[128,1024]{1,0:T(8,128)(2,1)S(1)}, bf16[128,1024]{1,0:T(8,128)(2,1)S(1)}, u32[]{:S(2)}, u32[]{:S(2)}) collective-permute-start(bf16[128,1024]{1,0:T(8,128)(2,1)S(1)} %get-tuple-element.84), channel_id=1, source_target_pairs={{0,2},{1,3},{2,0},{3,1},{4,6},{5,7},{6,4},{7,5},{8,10},{9,11},{10,... | collective-permute-start | bytes 786440 | tf_op jit(solution)/shard_map/ppermute | solution.py:352
  79.5 11.8 %collective-permute-start.11 = (bf16[128,1024]{1,0:T(8,128)(2,1)S(1)}, bf16[128,1024]{1,0:T(8,128)(2,1)S(1)}, u32[]{:S(2)}, u32[]{:S(2)}) collective-permute-start(bf16[128,1024]{1,0:T(8,128)(2,1)S(1)} %get-tuple-element.85), channel_id=1, source_target_pairs={{0,1},{1,0},{2,3},{3,2},{4,5},{5,4},{6,7},{7,6},{8,9},{9,8},{10,11... | collective-permute-start | bytes 786440 | tf_op jit(solution)/shard_map/ppermute | solution.py:352

commit v9 on v8

--- a/solution.py
+++ b/solution.py
@@ -48,7 +48,7 @@
     for m in range(4):
         way = way_of(lax.bitwise_xor(me, m))
         columns = pl.ds(pl.multiple_of(way * width, width), width)
-        out_ref[:, columns] = own_ref[way] if m == 0 else pieces[m - 1][...]
+        out_ref[:, columns] = own_ref[0] if m == 0 else pieces[m - 1][...]
 
 
 def collect(me, own, pieces):
@@ -246,7 +246,18 @@
             axis=3,
         )
         pair = swap(pair.transpose(1, 2, 0, 3))
-    query = queries.reshape(tok, ways, q_width // ways).transpose(1, 0, 2)
+    zero = jnp.zeros((), jnp.int32)
+    if relative:
+        wide = q_width // ways
+        outward = [((me ^ m) & 1) * 2 + ((me ^ m) >> 1) for m in range(4)]
+        query = [
+            lax.dynamic_slice(
+                queries, (zero, way * wide), (tok, wide), allow_negative_indices=False
+            )
+            for way in outward
+        ]
+    else:
+        query = queries.reshape(tok, ways, q_width // ways).transpose(1, 0, 2)
 
     pair, vertical, slash = lax.optimization_barrier((pair, vertical, slash))
 
@@ -262,11 +273,16 @@
     slash = lax.dynamic_slice_in_dim(slash, first_head, mine, axis=0)
     vertical = lax.dynamic_slice_in_dim(vertical, first_head, mine, axis=0)
     lists = lax.dynamic_slice_in_dim(slash, chip * per_group, per_group, axis=1)
-    if cores > 1:
+    if relative:
+        four = lists.reshape(mine, 2, 2, along, -1)
+        four = jnp.where(me >> 1 == 1, four[:, ::-1], four)
+        four = jnp.where(me & 1 == 1, four[:, :, ::-1], four)
+        lists = four.reshape(lists.shape)
+    elif cores > 1:
         lists = (
             lists.reshape(mine, cores, heads, along, -1).swapaxes(1, 2).reshape(lists.shape)
         )
-    ids = chip * per_group + local
+    ids = chip * per_group + (local_keys if relative else local)
 
     def masks(source):
         nat = (source[:, None] * per_group + local_keys).reshape(-1)
@@ -301,14 +317,17 @@
             tables.append(masks(jnp.where(row < 0, groups, 2 * row + col)))
         code, query = lax.optimization_barrier((tables[0][0], query))
         tables[0] = (code, tables[0][1])
-        query = swap(query).reshape(-1, max(tok, BLK), q_width // ways)
-        outward = [((me ^ m) & 1) * 2 + ((me ^ m) >> 1) for m in (1, 3, 2)]
+        query = {0: query[0]} | {
+            m: lax.ppermute(query[m], ("core", "head"), [(i, i ^ m) for i in range(4)])
+            for m in (1, 3, 2)
+        }
+        query = jnp.stack([query[m] for m in range(4)])
         part, waiting = pair, None
         for n in range(final + 2):
             fetched = None
             if n <= final:
                 if n == 1:
-                    part, tables, outward = lax.optimization_barrier((part, tables, outward))
+                    part, tables = lax.optimization_barrier((part, tables))
                 if state is not None:
                     part, mark = lax.optimization_barrier((part, state[2]))
                     state = state[:2] + (mark,)
@@ -343,13 +362,10 @@
             state = attend(query, masks(order[g : g + many]), ((part,),), state, g + many == groups)
 
     if relative:
-        pieces = {}
-        zero = jnp.zeros((), jnp.int32)
-        for m, way in zip((1, 3, 2), outward):
-            piece = lax.dynamic_slice(
-                state, (way, zero, zero), (1,) + state.shape[1:], allow_negative_indices=False
-            )[0]
-            pieces[m] = lax.ppermute(piece, ("core", "head"), [(i, i ^ m) for i in range(4)])
+        pieces = {
+            m: lax.ppermute(state[m], ("core", "head"), [(i, i ^ m) for i in range(4)])
+            for m in (1, 3, 2)
+        }
         return collect(me[None], state, [pieces[m] for m in (1, 2, 3)])
     out = swap(state.reshape(ways, tok, q_width // ways))
     return out.transpose(1, 0, 2).reshape(tok, q_width)

time: 92.7 us -> 91.3 us (0.985)
  waiting for transfers between devices: 19.6 us -> 23.8 us
  starting transfers between devices: 28.8 us -> 26.5 us
  local copies, waits for them, and re-layouts: 3.72 us -> 1.89 us
    ppermute x3, waiting for transfers between devices: 1.77 us -> 6.52 us  [body(): part = lax.ppermute(part, 'chip', up) if n < final else None]
    all_to_all x1 -> x0, starting transfers between devices: 3.53 us -> none  [body(): query = swap(query).reshape(-1, max(tok, BLK), q_width // ways)]
    all_to_all x1 -> x0, waiting for transfers between devices: 2.56 us -> none  [body(): query = swap(query).reshape(-1, max(tok, BLK), q_width // ways)]
    ppermute x3 -> x6, starting transfers between devices: 2.52 us -> 4.4 us  [the longest x3 2.21 us: body(): lax.ppermute(query[m], ('core', 'head'), [(i, i ^ m) for i in range(4)])]
    ppermute x3, waiting for transfers between devices: 1.86 us -> 3.64 us  [body(): lax.ppermute(pieces[m], ('core', 'head'), [(i, i ^ m) for i in range(4)])]
    unnamed x7 -> x6, local copies, waits for them, and re-layouts: 1.7 us -> 0.01 us
    reshape x1 -> x0, local copies, waits for them, and re-layouts: 1.31 us -> none  [body(): query = queries.reshape(tok, ways, q_width // ways).transpose(1, 0, 2)]
    ppermute x3, starting transfers between devices: 13.6 us -> 12.3 us  [body(): part = lax.ppermute(part, 'chip', up) if n < final else None]
  transfers between devices with their start and end apart: 15 -> 17, of which waited for: 6 -> 7; matrix products, arithmetic and copies ran while one was open for 11% -> 9% of each run, Pallas kernels for 24% -> 23%
where the time goes in v9:
time: 91.3 us; the launch traced here: 91.1 us
  Pallas kernels  32.2 us (35%)
  starting transfers between devices  26.5 us (29%)
  waiting for transfers between devices  23.8 us (26%)
  other arithmetic  6.38 us (7%)
  local copies, waits for them, and re-layouts  1.89 us (2%)
    pallas_call x4, Pallas kernels, attend_step(): pl.pallas_call(functools.partial(step_kernel, parts=tuple((len(part) for...  29.2 us
    ppermute x3, starting transfers between devices, body(): part = lax.ppermute(part, 'chip', up) if n < final else None  12.3 us
    ppermute x3, waiting for transfers between devices, body(): lax.ppermute(state[m], ('core', 'head'), [(i, i ^ m) for i in range(4)])  12.1 us
    ppermute x3, waiting for transfers between devices, body(): part = lax.ppermute(part, 'chip', up) if n < final else None  6.52 us
    ppermute x3, waiting for transfers between devices, body(): lax.ppermute(pieces[m], ('core', 'head'), [(i, i ^ m) for i in range(4)])  3.64 us
    ppermute x1, starting transfers between devices, body(): lax.ppermute(waiting[1][0][:, cut:], 'chip', up)  3.47 us
    ppermute x3, starting transfers between devices, body(): lax.ppermute(pieces[m], ('core', 'head'), [(i, i ^ m) for i in range(4)])  3.14 us
    reduce_and x1, other arithmetic, masks(): hidden = jnp.all(vertical[:, None, None, :] != position[..., None], axis=3)  2.92 us
  transfers between devices with their start and end apart: 17, of which 7 were waited for; matrix products, arithmetic and copies ran while one was open for 9% of the time, Pallas kernels for 23%

profile of v9, /device:TPU:0, one launch (start us, length us, event | category | flops | bytes accessed | tf_op | source)
XLA Modules:
  0.0 91.1 jit_solution(14737522448279759438)
XLA Ops:
  0.0 2.0 %shard_map.55 = (bf16[2,128,256]{2,1,0:T(8,128)(2,1)}, bf16[2,128,256]{2,1,0:T(8,128)(2,1)}, bf16[2,128,256]{2,1,0:T(8,128)(2,1)}, bf16[2,128,256]{2,1,0:T(8,128)(2,1)}) custom-call(s32[1]{0:T(128)} %bitcast.me_ref, bf16[128,1024]{1,0:T(8,128)(2,1)} %k_ref.1, bf16[128,1024]{1,0:T(8,128)(2,1)} %v_ref.1), custom_call_target="tpu_custom_call" | custom-call | tf_op jit(solution)/shard_map/pallas_call | solution.py:32
  2.0 3.0 %collective-permute-start = (bf16[2,128,256]{2,1,0:T(8,128)(2,1)}, bf16[2,128,256]{2,1,0:T(8,128)(2,1)S(1)}, u32[]{:S(2)}, u32[]{:S(2)}) collective-permute-start(bf16[2,128,256]{2,1,0:T(8,128)(2,1)} %get-tuple-element.40), channel_id=1, source_target_pairs={{0,1},{1,0},{2,3},{3,2},{4,5},{5,4},{6,7},{7,6},{8,9},{9,8},{10,11... | collective-permute-start | bytes 393224 | tf_op jit(solution)/shard_map/ppermute | solution.py:239
  5.0 0.2 collective-permute-start.2
  5.2 0.1 add_multiply_fusion
  5.2 0.1 iota_add_fusion.4
  5.3 0.1 add.309
  5.4 0.1 fusion
  5.5 0.1 broadcast_add_fusion.3
  5.6 0.1 add.312
  5.6 0.1 add.327
  5.7 0.1 add.335
  5.8 0.1 add.343
  5.9 0.1 select_select_fusion
  6.0 0.1 iota_add_fusion.2
  6.1 0.1 iota_add_fusion
  6.1 1.3 %constant_dynamic-slice_fusion.1 = (bf16[128,1024]{1,0:T(8,128)(2,1)S(1)}, bf16[128,1024]{1,0:T(8,128)(2,1)S(1)}, bf16[128,1024]{1,0:T(8,128)(2,1)S(1)}, bf16[128,1024]{1,0:T(8,128)(2,1)S(1)}) fusion(bf16[128,4096]{1,0:T(8,128)(2,1)} %param.5, s32[]{:T(128)S(6)} %mul.128, s32[]{:T(128)S(6)} %mul.124, s32[]{:T(128)S(6)} %mul.122, s32[]{:T(128)S(6)} %mul.126), kind=kLoop, calls=%fused_computation.33 | loop fusion | bytes 2097168 | tf_op jit(solution)/shard_map/dynamic_slice | solution.py:254
  7.4 1.8 %collective-permute-done = bf16[2,128,256]{2,1,0:T(8,128)(2,1)S(1)} collective-permute-done((bf16[2,128,256]{2,1,0:T(8,128)(2,1)}, bf16[2,128,256]{2,1,0:T(8,128)(2,1)S(1)}, u32[]{:S(2)}, u32[]{:S(2)}) %collective-permute-start) | collective-permute-done | bytes 131104 | tf_op jit(solution)/shard_map/ppermute | solution.py:239
  9.2 1.8 %collective-permute-done.2 = bf16[2,128,256]{2,1,0:T(8,128)(2,1)S(1)} collective-permute-done((bf16[2,128,256]{2,1,0:T(8,128)(2,1)}, bf16[2,128,256]{2,1,0:T(8,128)(2,1)S(1)}, u32[]{:S(2)}, u32[]{:S(2)}) %collective-permute-start.2) | collective-permute-done | bytes 131104 | tf_op jit(solution)/shard_map/ppermute | solution.py:239
  11.0 0.1 pad_maximum_fusion.1.rest_0_
  11.1 1.5 %collective-permute-start.8 = (bf16[4,2,128,256]{3,2,1,0:T(8,128)(2,1)S(1)}, bf16[4,2,128,256]{3,2,1,0:T(8,128)(2,1)S(1)}, u32[]{:S(2)}, u32[]{:S(2)}) collective-permute-start(bf16[4,2,128,256]{3,2,1,0:T(8,128)(2,1)S(1)} %pad_maximum_fusion.1.rest_0_), channel_id=1, source_target_pairs={{0,4},{4,0},{8,12},{12,8},{16,20},{20,16},{24,28},{28,24},{1,5},{5... | collective-permute-start | bytes 1572872 | tf_op jit(solution)/shard_map/ppermute | solution.py:335
  12.6 3.5 %collective-permute-start.3 = (bf16[4,2,128,256]{3,2,1,0:T(8,128)(2,1)S(1)}, bf16[4,2,128,256]{3,2,1,0:T(8,128)(2,1)S(1)}, u32[]{:S(2)}, u32[]{:S(2)}) collective-permute-start(bf16[4,2,128,256]{3,2,1,0:T(8,128)(2,1)S(1)} %pad_maximum_fusion.1.rest_0_), channel_id=1, source_target_pairs={{0,8},{4,12},{8,16},{12,20},{16,24},{20,28},{1,9},{5,13},{9,17},{1... | collective-permute-start | bytes 1572872 | tf_op jit(solution)/shard_map/ppermute | solution.py:343
  16.1 0.1 copy.7
  16.3 1.2 %compare_reduce_fusion.4 = (pred[2,8,16]{2,1,0:T(8,128)(4,1)S(1)}, pred[2,8,16]{2,1,0:T(8,128)(4,1)S(1)}, pred[2,8,16]{2,1,0:T(8,128)(4,1)S(1)}, pred[2,8,16]{2,1,0:T(8,128)(4,1)S(1)}) fusion(s32[2,8,40]{2,1,0:T(8,128)S(1)} %bitcast.30, s32[16]{0:T(128)S(1)} %add.343, s32[16]{0:T(128)S(1)} %add.327, s32[16]{0:T(128)S(1)} %add.335, s32[16]{0:T(128)S(1)} %add.312), kind=kLoop, calls=%fused_computation.13 | loop fusion | flops 80896 | bytes 3840 | tf_op jit(solution)/shard_map/reduce_or | solution.py:289
  17.6 1.2 %collective-permute-start.4 = (bf16[128,1024]{1,0:T(8,128)(2,1)S(1)}, bf16[128,1024]{1,0:T(8,128)(2,1)S(1)}, u32[]{:S(2)}, u32[]{:S(2)}) collective-permute-start(bf16[128,1024]{1,0:T(8,128)(2,1)S(1)} %get-tuple-element.49), channel_id=1, source_target_pairs={{0,1},{1,0},{2,3},{3,2},{4,5},{5,4},{6,7},{7,6},{8,9},{9,8},{10,11... | collective-permute-start | bytes 786440 | tf_op jit(solution)/shard_map/ppermute | solution.py:321
  18.7 0.1 collective-permute-start.5
  18.9 0.9 collective-permute-start.6
  19.8 2.9 %compare_reduce_fusion = (pred[2,16,64]{2,1,0:T(8,128)(4,1)S(1)}, pred[2,16,64]{2,1,0:T(8,128)(4,1)S(1)}, pred[2,16,64]{2,1,0:T(8,128)(4,1)S(1)}, pred[2,16,64]{2,1,0:T(8,128)(4,1)S(1)}) fusion(s32[16,64]{1,0:T(8,128)S(1)} %get-tuple-element.107, s32[2,128]{1,0:T(2,128)S(1)} %constant_dynamic-slice_fusion, s32[16,64]{1,0:T(8,128)S(1)} %get-tuple-element.109, ...), kind=kLoop, calls=%fused_computation.2 | loop fusion | flops 2088960 | bytes 25600 | tf_op jit(solution)/shard_map/reduce_and | solution.py:297
  22.7 1.4 %and_convert_fusion = (bf16[2,16,64,128]{3,2,1,0:T(8,128)(2,1)S(1)}, bf16[2,16,64,128]{3,2,1,0:T(8,128)(2,1)S(1)}, bf16[2,16,64,128]{3,2,1,0:T(8,128)(2,1)S(1)}, bf16[2,16,64,128]{3,2,1,0:T(8,128)(2,1)S(1)}) fusion(pred[2,16,64]{2,1,0:T(8,128)(4,1)S(1)} %get-tuple-element.77, pred[128]{0:T(512)(128)(4,1)S(1)} %iota_compare_fusion, ...), kind=kLoop, calls=%fused_computation.1 | loop fusion | flops 2097152 | bytes 2105472 | tf_op jit(solution)/shard_map/convert_element_type | solution.py:299
  24.1 3.6 %collective-permute-done.3.rest_0_ = bf16[4,2,128,256]{3,2,1,0:T(8,128)(2,1)S(1)} collective-permute-done((bf16[4,2,128,256]{3,2,1,0:T(8,128)(2,1)S(1)}, bf16[4,2,128,256]{3,2,1,0:T(8,128)(2,1)S(1)}, u32[]{:S(2)}, u32[]{:S(2)}) %collective-permute-start.3) | collective-permute-done | bytes 524320 | tf_op jit(solution)/shard_map/ppermute | solution.py:343
  27.7 4.4 %collective-permute-start.7 = (bf16[4,2,128,256]{3,2,1,0:T(8,128)(2,1)S(1)}, bf16[4,2,128,256]{3,2,1,0:T(8,128)(2,1)S(1)}, u32[]{:S(2)}, u32[]{:S(2)}) collective-permute-start(bf16[4,2,128,256]{3,2,1,0:T(8,128)(2,1)S(1)} %collective-permute-done.3.rest_0_), channel_id=1, source_target_pairs={{0,8},{4,12},{8,16},{12,20},{16,24},{20,28},{1,9},{5,13},{9,17},{1... | collective-permute-start | bytes 1572872 | tf_op jit(solution)/shard_map/ppermute | solution.py:343
  32.1 0.1 pad_maximum_fusion.q_ref
  32.3 0.6 collective-permute-start.10
  32.9 7.0 %shard_map.56 = (f32[16,128,256]{2,1,0:T(8,128)S(1)}, f32[16,16,256]{2,1,0:T(8,128)S(1)}, bf16[16,128]{1,0:T(8,128)(2,1)S(1)}) custom-call(s32[2,8,16]{2,1,0:T(8,128)S(1)} %broadcast_select_fusion.3.code_ref, bf16[4,128,1024]{2,1,0:T(8,128)(2,1)S(1)} %pad_maximum_fusion.q_ref, bf16[2,16,64,128]{3,2,1,0:T(8,128)(2,1)S(1)} %get-tuple-element.55.pick_ref, ...), custom_call_target="tpu_custom_call" | custom-call | flops 2147483648 | bytes 8388608 | tf_op jit(solution)/shard_map/pallas_call | solution.py:190
  39.9 3.0 %collective-permute-done.7.rest_0_ = bf16[4,2,128,256]{3,2,1,0:T(8,128)(2,1)S(1)} collective-permute-done((bf16[4,2,128,256]{3,2,1,0:T(8,128)(2,1)S(1)}, bf16[4,2,128,256]{3,2,1,0:T(8,128)(2,1)S(1)}, u32[]{:S(2)}, u32[]{:S(2)}) %collective-permute-start.7) | collective-permute-done | bytes 524320 | tf_op jit(solution)/shard_map/ppermute | solution.py:343
  42.9 0.5 collective-permute-start.12
  43.4 4.4 %collective-permute-start.9 = (bf16[4,2,128,256]{3,2,1,0:T(8,128)(2,1)S(1)}, bf16[4,2,128,256]{3,2,1,0:T(8,128)(2,1)S(1)}, u32[]{:S(2)}, u32[]{:S(2)}) collective-permute-start(bf16[4,2,128,256]{3,2,1,0:T(8,128)(2,1)S(1)} %collective-permute-done.7.rest_0_), channel_id=1, source_target_pairs={{0,8},{4,12},{8,16},{12,20},{16,24},{20,28},{1,9},{5,13},{9,17},{1... | collective-permute-start | bytes 1572872 | tf_op jit(solution)/shard_map/ppermute | solution.py:343
  47.8 7.2 %shard_map.57 = (f32[16,128,256]{2,1,0:T(8,128)S(1)}, f32[16,16,256]{2,1,0:T(8,128)S(1)}, bf16[16,128]{1,0:T(8,128)(2,1)S(1)}) custom-call(s32[2,8,16]{2,1,0:T(8,128)S(1)} %broadcast_select_fusion.2.code_ref, bf16[4,128,1024]{2,1,0:T(8,128)(2,1)S(1)} %pad_maximum_fusion.q_ref, bf16[2,16,64,128]{3,2,1,0:T(8,128)(2,1)S(1)} %get-tuple-element.59.pick_ref, ...), custom_call_target="tpu_custom_call" | custom-call | flops 2147483648 | bytes 8388608 | tf_op jit(solution)/shard_map/pallas_call | solution.py:190
  55.0 1.6 %collective-permute-done.12.rest_1_ = bf16[4,2,128,256]{3,2,1,0:T(8,128)(2,1)S(1)} collective-permute-done((bf16[4,2,128,256]{3,2,1,0:T(8,128)(2,1)S(1)}, bf16[4,2,128,256]{3,2,1,0:T(8,128)(2,1)S(1)}, u32[]{:S(2)}, u32[]{:S(2)}) %collective-permute-start.12) | collective-permute-done | bytes 524320 | tf_op jit(solution)/shard_map/ppermute | solution.py:335
  56.6 3.5 %collective-permute-start.13 = (bf16[4,1,128,256]{3,2,1,0:T(8,128)(2,1)S(1)}, bf16[4,1,128,256]{3,2,1,0:T(8,128)(2,1)S(1)}, u32[]{:S(2)}, u32[]{:S(2)}) collective-permute-start(bf16[4,1,128,256]{3,2,1,0:T(8,128)(2,1)S(1)} %slice.20), channel_id=1, source_target_pairs={{0,8},{4,12},{8,16},{12,20},{16,24},{20,28},{1,9},{5,13},{9,17},{1... | collective-permute-start | bytes 786440 | tf_op jit(solution)/shard_map/ppermute | solution.py:340
  60.1 0.6 collective-permute-start.11
  60.7 7.1 %shard_map.58 = (f32[16,128,256]{2,1,0:T(8,128)S(1)}, f32[16,16,256]{2,1,0:T(8,128)S(1)}, bf16[16,128]{1,0:T(8,128)(2,1)S(1)}) custom-call(s32[2,8,16]{2,1,0:T(8,128)S(1)} %get-tuple-element.65.code_ref, bf16[4,128,1024]{2,1,0:T(8,128)(2,1)S(1)} %pad_maximum_fusion.q_ref, bf16[2,16,64,128]{3,2,1,0:T(8,128)(2,1)S(1)} %get-tuple-element.66.pick_ref, ...), custom_call_target="tpu_custom_call" | custom-call | flops 2147483648 | bytes 8388608 | tf_op jit(solution)/shard_map/pallas_call | solution.py:190
  67.8 7.8 %shard_map.59.own_ref = bf16[4,128,1024]{2,1,0:T(8,128)(2,1)S(1)} custom-call(s32[2,8,16]{2,1,0:T(8,128)S(1)} %get-tuple-element.47.code_ref, bf16[4,128,1024]{2,1,0:T(8,128)(2,1)S(1)} %pad_maximum_fusion.q_ref, bf16[2,16,64,128]{3,2,1,0:T(8,128)(2,1)S(1)} %get-tuple-element.52.pick_ref, bf16[4,2,128,256]{3,2,1,0:T(8,128)(2,1)S(1)} %collective-permute-done.9.rest_0_, ...), custom_call_target="tpu_custom_call" | custom-call | flops 2147483648 | bytes 8388608 | tf_op jit(solution)/shard_map/pallas_call | solution.py:190
  75.7 0.1 collective-permute-start.16
  75.8 2.0 %collective-permute-start.15 = (bf16[128,1024]{1,0:T(8,128)(2,1)S(1)}, bf16[128,1024]{1,0:T(8,128)(2,1)S(1)}, u32[]{:S(2)}, u32[]{:S(2)}) collective-permute-start(bf16[128,1024]{1,0:T(8,128)(2,1)S(1)} %get-tuple-element.84), channel_id=1, source_target_pairs={{0,2},{1,3},{2,0},{3,1},{4,6},{5,7},{6,4},{7,5},{8,10},{9,11},{10,... | collective-permute-start | bytes 786440 | tf_op jit(solution)/shard_map/ppermute | solution.py:366
  77.8 0.1 collective-permute-start.14
  78.0 6.1 %collective-permute-done.16.rest_2_ = bf16[128,1024]{1,0:T(8,128)(2,1)S(1)} collective-permute-done((bf16[128,1024]{1,0:T(8,128)(2,1)S(1)}, bf16[128,1024]{1,0:T(8,128)(2,1)S(1)}, u32[]{:S(2)}, u32[]{:S(2)}) %collective-permute-start.16) | collective-permute-done | bytes 262176 | tf_op jit(solution)/shard_map/ppermute | solution.py:366
  84.1 6.0 %collective-permute-done.14.rest_0_ = bf16[128,1024]{1,0:T(8,128)(2,1)S(1)} collective-permute-done((bf16[128,1024]{1,0:T(8,128)(2,1)S(1)}, bf16[128,1024]{1,0:T(8,128)(2,1)S(1)}, u32[]{:S(2)}, u32[]{:S(2)}) %collective-permute-start.14) | collective-permute-done | bytes 262176 | tf_op jit(solution)/shard_map/ppermute | solution.py:366
  90.0 1.0 %shard_map.60 = bf16[128,4096]{1,0:T(8,128)(2,1)} custom-call(s32[1]{0:T(128)} %bitcast.me_ref, bf16[4,128,1024]{2,1,0:T(8,128)(2,1)S(1)} %shard_map.59.own_ref, bf16[128,1024]{1,0:T(8,128)(2,1)S(1)} %collective-permute-done.14.rest_0_, bf16[128,1024]{1,0:T(8,128)(2,1)S(1)} %collective-permute-done.15.rest_1_, ...), custom_call_target="tpu_custom_call" | custom-call | tf_op jit(solution)/shard_map/pallas_call | solution.py:57
  (35 shorter events, 0.2 us)
Async XLA Ops:
  0.0 16.1 %copy-start = (s32[4,128]{1,0:T(4,128)S(1)}, s32[4,128]{1,0:T(4,128)}, u32[]{:S(2)}) copy-start(s32[4,128]{1,0:T(4,128)} %param.8) | copy-start | bytes 6148
  0.0 16.1 %copy-start.2 = (s32[4,64,40]{1,2,0:T(8,128)S(1)}, s32[4,64,40]{1,2,0:T(8,128)}, u32[]{:S(2)}) copy-start(s32[4,64,40]{1,2,0:T(8,128)} %param.9) | copy-start | bytes 122884
  2.0 9.0 %copy-start.1 = (bf16[2,128,256]{2,1,0:T(8,128)(2,1)S(1)}, bf16[2,128,256]{2,1,0:T(8,128)(2,1)}, u32[]{:S(2)}) copy-start(bf16[2,128,256]{2,1,0:T(8,128)(2,1)} %get-tuple-element.39) | copy-start | bytes 393220
  2.0 7.2 %collective-permute-start = (bf16[2,128,256]{2,1,0:T(8,128)(2,1)}, bf16[2,128,256]{2,1,0:T(8,128)(2,1)S(1)}, u32[]{:S(2)}, u32[]{:S(2)}) collective-permute-start(bf16[2,128,256]{2,1,0:T(8,128)(2,1)} %get-tuple-element.40), channel_id=1, source_target_pairs={{0,1},{1,0},{2,3},{3,2},{4,5},{5,4},{6,7},{7,6},{8,9},{9,8},{10,11... | collective-permute-start | bytes 393224 | tf_op jit(solution)/shard_map/ppermute | solution.py:239
  5.0 4.2 %collective-permute-start.1 = (bf16[2,128,256]{2,1,0:T(8,128)(2,1)}, bf16[2,128,256]{2,1,0:T(8,128)(2,1)S(1)}, u32[]{:S(2)}, u32[]{:S(2)}) collective-permute-start(bf16[2,128,256]{2,1,0:T(8,128)(2,1)} %get-tuple-element.41), channel_id=1, source_target_pairs={{0,2},{1,3},{2,0},{3,1},{4,6},{5,7},{6,4},{7,5},{8,10},{9,11},{10,... | collective-permute-start | bytes 393224 | tf_op jit(solution)/shard_map/ppermute | solution.py:239
  5.0 6.1 %collective-permute-start.2 = (bf16[2,128,256]{2,1,0:T(8,128)(2,1)}, bf16[2,128,256]{2,1,0:T(8,128)(2,1)S(1)}, u32[]{:S(2)}, u32[]{:S(2)}) collective-permute-start(bf16[2,128,256]{2,1,0:T(8,128)(2,1)} %get-tuple-element.42), channel_id=1, source_target_pairs={{0,3},{1,2},{2,1},{3,0},{4,7},{5,6},{6,5},{7,4},{8,11},{9,10},{10,... | collective-permute-start | bytes 393224 | tf_op jit(solution)/shard_map/ppermute | solution.py:239
  11.1 21.8 %collective-permute-start.8 = (bf16[4,2,128,256]{3,2,1,0:T(8,128)(2,1)S(1)}, bf16[4,2,128,256]{3,2,1,0:T(8,128)(2,1)S(1)}, u32[]{:S(2)}, u32[]{:S(2)}) collective-permute-start(bf16[4,2,128,256]{3,2,1,0:T(8,128)(2,1)S(1)} %pad_maximum_fusion.1.rest_0_), channel_id=1, source_target_pairs={{0,4},{4,0},{8,12},{12,8},{16,20},{20,16},{24,28},{28,24},{1,5},{5... | collective-permute-start | bytes 1572872 | tf_op jit(solution)/shard_map/ppermute | solution.py:335
  12.6 15.1 %collective-permute-start.3 = (bf16[4,2,128,256]{3,2,1,0:T(8,128)(2,1)S(1)}, bf16[4,2,128,256]{3,2,1,0:T(8,128)(2,1)S(1)}, u32[]{:S(2)}, u32[]{:S(2)}) collective-permute-start(bf16[4,2,128,256]{3,2,1,0:T(8,128)(2,1)S(1)} %pad_maximum_fusion.1.rest_0_), channel_id=1, source_target_pairs={{0,8},{4,12},{8,16},{12,20},{16,24},{20,28},{1,9},{5,13},{9,17},{1... | collective-permute-start | bytes 1572872 | tf_op jit(solution)/shard_map/ppermute | solution.py:343
  17.6 14.5 %collective-permute-start.4 = (bf16[128,1024]{1,0:T(8,128)(2,1)S(1)}, bf16[128,1024]{1,0:T(8,128)(2,1)S(1)}, u32[]{:S(2)}, u32[]{:S(2)}) collective-permute-start(bf16[128,1024]{1,0:T(8,128)(2,1)S(1)} %get-tuple-element.49), channel_id=1, source_target_pairs={{0,1},{1,0},{2,3},{3,2},{4,5},{5,4},{6,7},{7,6},{8,9},{9,8},{10,11... | collective-permute-start | bytes 786440 | tf_op jit(solution)/shard_map/ppermute | solution.py:321
  18.7 13.4 %collective-permute-start.5 = (bf16[128,1024]{1,0:T(8,128)(2,1)S(1)}, bf16[128,1024]{1,0:T(8,128)(2,1)S(1)}, u32[]{:S(2)}, u32[]{:S(2)}) collective-permute-start(bf16[128,1024]{1,0:T(8,128)(2,1)S(1)} %get-tuple-element.50), channel_id=1, source_target_pairs={{0,2},{1,3},{2,0},{3,1},{4,6},{5,7},{6,4},{7,5},{8,10},{9,11},{10,... | collective-permute-start | bytes 786440 | tf_op jit(solution)/shard_map/ppermute | solution.py:321
  18.9 13.2 %collective-permute-start.6 = (bf16[128,1024]{1,0:T(8,128)(2,1)S(1)}, bf16[128,1024]{1,0:T(8,128)(2,1)S(1)}, u32[]{:S(2)}, u32[]{:S(2)}) collective-permute-start(bf16[128,1024]{1,0:T(8,128)(2,1)S(1)} %get-tuple-element.51), channel_id=1, source_target_pairs={{0,3},{1,2},{2,1},{3,0},{4,7},{5,6},{6,5},{7,4},{8,11},{9,10},{10,... | collective-permute-start | bytes 786440 | tf_op jit(solution)/shard_map/ppermute | solution.py:321
  27.7 15.2 %collective-permute-start.7 = (bf16[4,2,128,256]{3,2,1,0:T(8,128)(2,1)S(1)}, bf16[4,2,128,256]{3,2,1,0:T(8,128)(2,1)S(1)}, u32[]{:S(2)}, u32[]{:S(2)}) collective-permute-start(bf16[4,2,128,256]{3,2,1,0:T(8,128)(2,1)S(1)} %collective-permute-done.3.rest_0_), channel_id=1, source_target_pairs={{0,8},{4,12},{8,16},{12,20},{16,24},{20,28},{1,9},{5,13},{9,17},{1... | collective-permute-start | bytes 1572872 | tf_op jit(solution)/shard_map/ppermute | solution.py:343
  32.3 15.5 %collective-permute-start.10 = (bf16[4,2,128,256]{3,2,1,0:T(8,128)(2,1)S(1)}, bf16[4,2,128,256]{3,2,1,0:T(8,128)(2,1)S(1)}, u32[]{:S(2)}, u32[]{:S(2)}) collective-permute-start(bf16[4,2,128,256]{3,2,1,0:T(8,128)(2,1)S(1)} %collective-permute-done.3.rest_0_), channel_id=1, source_target_pairs={{0,4},{4,0},{8,12},{12,8},{16,20},{20,16},{24,28},{28,24},{1,5},{5... | collective-permute-start | bytes 1572872 | tf_op jit(solution)/shard_map/ppermute | solution.py:335
  42.9 13.7 %collective-permute-start.12 = (bf16[4,2,128,256]{3,2,1,0:T(8,128)(2,1)S(1)}, bf16[4,2,128,256]{3,2,1,0:T(8,128)(2,1)S(1)}, u32[]{:S(2)}, u32[]{:S(2)}) collective-permute-start(bf16[4,2,128,256]{3,2,1,0:T(8,128)(2,1)S(1)} %collective-permute-done.7.rest_0_), channel_id=1, source_target_pairs={{0,4},{4,0},{8,12},{12,8},{16,20},{20,16},{24,28},{28,24},{1,5},{5... | collective-permute-start | bytes 1572872 | tf_op jit(solution)/shard_map/ppermute | solution.py:335
  43.4 16.7 %collective-permute-start.9 = (bf16[4,2,128,256]{3,2,1,0:T(8,128)(2,1)S(1)}, bf16[4,2,128,256]{3,2,1,0:T(8,128)(2,1)S(1)}, u32[]{:S(2)}, u32[]{:S(2)}) collective-permute-start(bf16[4,2,128,256]{3,2,1,0:T(8,128)(2,1)S(1)} %collective-permute-done.7.rest_0_), channel_id=1, source_target_pairs={{0,8},{4,12},{8,16},{12,20},{16,24},{20,28},{1,9},{5,13},{9,17},{1... | collective-permute-start | bytes 1572872 | tf_op jit(solution)/shard_map/ppermute | solution.py:343
  56.6 11.2 %collective-permute-start.13 = (bf16[4,1,128,256]{3,2,1,0:T(8,128)(2,1)S(1)}, bf16[4,1,128,256]{3,2,1,0:T(8,128)(2,1)S(1)}, u32[]{:S(2)}, u32[]{:S(2)}) collective-permute-start(bf16[4,1,128,256]{3,2,1,0:T(8,128)(2,1)S(1)} %slice.20), channel_id=1, source_target_pairs={{0,8},{4,12},{8,16},{12,20},{16,24},{20,28},{1,9},{5,13},{9,17},{1... | collective-permute-start | bytes 786440 | tf_op jit(solution)/shard_map/ppermute | solution.py:340
  60.1 7.7 %collective-permute-start.11 = (bf16[4,1,128,256]{3,2,1,0:T(8,128)(2,1)S(1)}, bf16[4,1,128,256]{3,2,1,0:T(8,128)(2,1)S(1)}, u32[]{:S(2)}, u32[]{:S(2)}) collective-permute-start(bf16[4,1,128,256]{3,2,1,0:T(8,128)(2,1)S(1)} %slice.15), channel_id=1, source_target_pairs={{0,4},{4,0},{8,12},{12,8},{16,20},{20,16},{24,28},{28,24},{1,5},{5... | collective-permute-start | bytes 786440 | tf_op jit(solution)/shard_map/ppermute | solution.py:339
  75.7 8.3 %collective-permute-start.16 = (bf16[128,1024]{1,0:T(8,128)(2,1)S(1)}, bf16[128,1024]{1,0:T(8,128)(2,1)S(1)}, u32[]{:S(2)}, u32[]{:S(2)}) collective-permute-start(bf16[128,1024]{1,0:T(8,128)(2,1)S(1)} %get-tuple-element.83), channel_id=1, source_target_pairs={{0,3},{1,2},{2,1},{3,0},{4,7},{5,6},{6,5},{7,4},{8,11},{9,10},{10,... | collective-permute-start | bytes 786440 | tf_op jit(solution)/shard_map/ppermute | solution.py:366
  75.8 8.2 %collective-permute-start.15 = (bf16[128,1024]{1,0:T(8,128)(2,1)S(1)}, bf16[128,1024]{1,0:T(8,128)(2,1)S(1)}, u32[]{:S(2)}, u32[]{:S(2)}) collective-permute-start(bf16[128,1024]{1,0:T(8,128)(2,1)S(1)} %get-tuple-element.84), channel_id=1, source_target_pairs={{0,2},{1,3},{2,0},{3,1},{4,6},{5,7},{6,4},{7,5},{8,10},{9,11},{10,... | collective-permute-start | bytes 786440 | tf_op jit(solution)/shard_map/ppermute | solution.py:366
  77.8 12.2 %collective-permute-start.14 = (bf16[128,1024]{1,0:T(8,128)(2,1)S(1)}, bf16[128,1024]{1,0:T(8,128)(2,1)S(1)}, u32[]{:S(2)}, u32[]{:S(2)}) collective-permute-start(bf16[128,1024]{1,0:T(8,128)(2,1)S(1)} %get-tuple-element.85), channel_id=1, source_target_pairs={{0,1},{1,0},{2,3},{3,2},{4,5},{5,4},{6,7},{7,6},{8,9},{9,8},{10,11... | collective-permute-start | bytes 786440 | tf_op jit(solution)/shard_map/ppermute | solution.py:366

commit v10 on v9

--- a/solution.py
+++ b/solution.py
@@ -91,9 +91,14 @@
     qext[...] = jnp.where(masked, -BIG, 0.0).astype(BF16)
     key_iota = lax.broadcasted_iota(jnp.int32, (BLK, head_dim), 0)
     lane = lax.broadcasted_iota(jnp.int32, (BLK, head_dim), 1)
-    etile[LIVE] = jnp.zeros((BLK, head_dim), BF16)
-    etile[DEAD] = jnp.where(lane == BLK, 1.0, 0.0).astype(BF16)
-    etile[OWN] = jnp.where(lane == key_iota, 1.0, 0.0).astype(BF16)
+    each = PICKED + slots
+    for head in range(*span):
+        base = head * each
+        etile[base + LIVE] = jnp.zeros((BLK, head_dim), BF16)
+        etile[base + DEAD] = jnp.where(lane == BLK, 1.0, 0.0).astype(BF16)
+        etile[base + OWN] = jnp.where(lane == key_iota, 1.0, 0.0).astype(BF16)
+        for slot in range(slots):
+            etile[base + PICKED + slot] = pick_ref[head, slot]
 
     def held(p, head, c):
         for ref in part_refs[p]:
@@ -105,11 +110,12 @@
         start = pl.multiple_of(lax.rem(here, per_q) * BLK, BLK)
         return lax.div(here, per_q), pl.ds(start, BLK), pl.ds(g * head_dim, head_dim)
 
-    def stage(head, ahead, ahead_buffer, here, buffer, top):
-        query = jnp.concatenate(
-            [q_ref[place(ahead, head * group + g)] for g in range(group)], axis=0
-        )
-        query = jnp.concatenate([query, qext[...]], axis=1)
+    def stage(next_head, ahead, ahead_buffer, head, here, buffer, top):
+        if ahead is not None:
+            query = jnp.concatenate(
+                [q_ref[place(ahead, next_head * group + g)] for g in range(group)], axis=0
+            )
+            query = jnp.concatenate([query, qext[...]], axis=1)
         at = head * blocks_here + here if here is not None else None
         if here is not None and not first:
             before = stat_in[at, :8]
@@ -118,20 +124,22 @@
         ahead_top = jnp.full((8, rows), -jnp.inf, F32)
         shares, values = [], []
         for p in range(len(parts)):
-            left = [held(p, head, c)[:, pl.ds(0, head_dim)] for c in range(chunks)]
-            right = [
-                etile[code_ref[head, ahead, p * per_part + i]] for i in range(per_part)
-            ]
-            key = jnp.concatenate(
-                [jnp.concatenate(left, axis=0), jnp.concatenate(right, axis=0)], axis=1
-            )
-            tile = lax.dot_general(
-                key, query, (((1,), (1,)), ((), ())), preferred_element_type=F32
-            )
-            ahead_buffer[pl.ds(p * size, size), :] = tile
-            ahead_top = jnp.maximum(
-                ahead_top, jnp.max(tile.reshape(size // 8, 8, rows), axis=0)
-            )
+            if ahead is not None:
+                left = [held(p, next_head, c)[:, pl.ds(0, head_dim)] for c in range(chunks)]
+                right = [
+                    etile[next_head * each + code_ref[next_head, ahead, p * per_part + i]]
+                    for i in range(per_part)
+                ]
+                key = jnp.concatenate(
+                    [jnp.concatenate(left, axis=0), jnp.concatenate(right, axis=0)], axis=1
+                )
+                tile = lax.dot_general(
+                    key, query, (((1,), (1,)), ((), ())), preferred_element_type=F32
+                )
+                ahead_buffer[pl.ds(p * size, size), :] = tile
+                ahead_top = jnp.maximum(
+                    ahead_top, jnp.max(tile.reshape(size // 8, 8, rows), axis=0)
+                )
             if here is not None:
                 tile = buffer[pl.ds(p * size, size), :].reshape(size // 8, 8, rows)
                 expo = jnp.exp2((tile - top[None]) * scale)
@@ -157,17 +165,18 @@
             out_ref[place(here, (head - span[0]) * group + g)] = result[g * BLK : (g + 1) * BLK]
         return ahead_top
 
+    top = stage(span[0], 0, score_a, None, None, None, None)
+    final = blocks_here - 1
     for head in range(*span):
-        for slot in range(slots):
-            etile[PICKED + slot] = pick_ref[head, slot]
 
         def two(step, top):
-            top = stage(head, 2 * step + 1, score_b, 2 * step, score_a, top)
-            ahead = jnp.minimum(2 * step + 2, blocks_here - 1)
-            return stage(head, ahead, score_a, 2 * step + 1, score_b, top)
-
-        top = stage(head, 0, score_a, None, None, None)
-        lax.fori_loop(0, blocks_here // 2, two, top)
+            top = stage(head, 2 * step + 1, score_b, head, 2 * step, score_a, top)
+            return stage(head, 2 * step + 2, score_a, head, 2 * step + 1, score_b, top)
+
+        top = lax.fori_loop(0, blocks_here // 2 - 1, two, top)
+        top = stage(head, final, score_b, head, final - 1, score_a, top)
+        following = 0 if head + 1 < span[1] else None
+        top = stage(head + 1, following, score_a, head, final, score_b, top)
 
 
 def attend_step(code, query, pick, parts, state, span, last, head_dim, group):
@@ -202,7 +211,7 @@
         out_specs=vmem if last else (vmem,) * 3,
         scratch_shapes=[
             pltpu.VMEM((rows, head_dim), BF16),
-            pltpu.VMEM((PICKED + slots, BLK, head_dim), BF16),
+            pltpu.VMEM((heads * (PICKED + slots), BLK, head_dim), BF16),
             pltpu.VMEM((slots * BLK, rows), F32),
             pltpu.VMEM((slots * BLK, rows), F32),
         ],

time: 91.3 us -> 90.8 us (level)
  Pallas kernels: 32.2 us -> 30.7 us
    pallas_call x4, Pallas kernels: 29.2 us -> 27.7 us  [attend_step(): pl.pallas_call(functools.partial(step_kernel, parts=tuple((len(part) for...]
  transfers between devices with their start and end apart: 17 -> 17, of which waited for: 7 -> 7; matrix products, arithmetic and copies ran while one was open for 9% -> 9% of each run, Pallas kernels for 23% -> 22%
where the time goes in v10:
time: 90.8 us; the launch traced here: 90.5 us
  Pallas kernels  30.7 us (34%)
  starting transfers between devices  26.7 us (29%)
  waiting for transfers between devices  24.5 us (27%)
  other arithmetic  6.38 us (7%)
  local copies, waits for them, and re-layouts  1.89 us (2%)
    pallas_call x4, Pallas kernels, attend_step(): pl.pallas_call(functools.partial(step_kernel, parts=tuple((len(part) for...  27.7 us
    ppermute x3, starting transfers between devices, body(): part = lax.ppermute(part, 'chip', up) if n < final else None  12.3 us
    ppermute x3, waiting for transfers between devices, body(): lax.ppermute(state[m], ('core', 'head'), [(i, i ^ m) for i in range(4)])  12.1 us
    ppermute x3, waiting for transfers between devices, body(): part = lax.ppermute(part, 'chip', up) if n < final else None  6.92 us
    ppermute x1, starting transfers between devices, body(): lax.ppermute(waiting[1][0][:, cut:], 'chip', up)  3.65 us
    ppermute x3, waiting for transfers between devices, body(): lax.ppermute(pieces[m], ('core', 'head'), [(i, i ^ m) for i in range(4)])  3.64 us
    ppermute x3, starting transfers between devices, body(): lax.ppermute(pieces[m], ('core', 'head'), [(i, i ^ m) for i in range(4)])  3.14 us
    reduce_and x1, other arithmetic, masks(): hidden = jnp.all(vertical[:, None, None, :] != position[..., None], axis=3)  2.92 us
  transfers between devices with their start and end apart: 17, of which 7 were waited for; matrix products, arithmetic and copies ran while one was open for 9% of the time, Pallas kernels for 22%

profile of v10, /device:TPU:0, one launch (start us, length us, event | category | flops | bytes accessed | tf_op | source)
XLA Modules:
  0.0 90.5 jit_solution(16343663218597688118)
XLA Ops:
  0.0 2.0 %shard_map.55 = (bf16[2,128,256]{2,1,0:T(8,128)(2,1)}, bf16[2,128,256]{2,1,0:T(8,128)(2,1)}, bf16[2,128,256]{2,1,0:T(8,128)(2,1)}, bf16[2,128,256]{2,1,0:T(8,128)(2,1)}) custom-call(s32[1]{0:T(128)} %bitcast.me_ref, bf16[128,1024]{1,0:T(8,128)(2,1)} %k_ref.1, bf16[128,1024]{1,0:T(8,128)(2,1)} %v_ref.1), custom_call_target="tpu_custom_call" | custom-call | tf_op jit(solution)/shard_map/pallas_call | solution.py:32
  2.0 3.0 %collective-permute-start = (bf16[2,128,256]{2,1,0:T(8,128)(2,1)}, bf16[2,128,256]{2,1,0:T(8,128)(2,1)S(1)}, u32[]{:S(2)}, u32[]{:S(2)}) collective-permute-start(bf16[2,128,256]{2,1,0:T(8,128)(2,1)} %get-tuple-element.40), channel_id=1, source_target_pairs={{0,1},{1,0},{2,3},{3,2},{4,5},{5,4},{6,7},{7,6},{8,9},{9,8},{10,11... | collective-permute-start | bytes 393224 | tf_op jit(solution)/shard_map/ppermute | solution.py:248
  5.0 0.2 collective-permute-start.2
  5.2 0.1 add_multiply_fusion
  5.2 0.1 iota_add_fusion.4
  5.3 0.1 add.309
  5.4 0.1 fusion
  5.5 0.1 broadcast_add_fusion.3
  5.6 0.1 add.312
  5.6 0.1 add.327
  5.7 0.1 add.335
  5.8 0.1 add.343
  5.9 0.1 select_select_fusion
  6.0 0.1 iota_add_fusion.2
  6.1 0.1 iota_add_fusion
  6.1 1.3 %constant_dynamic-slice_fusion.1 = (bf16[128,1024]{1,0:T(8,128)(2,1)S(1)}, bf16[128,1024]{1,0:T(8,128)(2,1)S(1)}, bf16[128,1024]{1,0:T(8,128)(2,1)S(1)}, bf16[128,1024]{1,0:T(8,128)(2,1)S(1)}) fusion(bf16[128,4096]{1,0:T(8,128)(2,1)} %param.5, s32[]{:T(128)S(6)} %mul.128, s32[]{:T(128)S(6)} %mul.124, s32[]{:T(128)S(6)} %mul.122, s32[]{:T(128)S(6)} %mul.126), kind=kLoop, calls=%fused_computation.33 | loop fusion | bytes 2097168 | tf_op jit(solution)/shard_map/dynamic_slice | solution.py:263
  7.4 1.8 %collective-permute-done = bf16[2,128,256]{2,1,0:T(8,128)(2,1)S(1)} collective-permute-done((bf16[2,128,256]{2,1,0:T(8,128)(2,1)}, bf16[2,128,256]{2,1,0:T(8,128)(2,1)S(1)}, u32[]{:S(2)}, u32[]{:S(2)}) %collective-permute-start) | collective-permute-done | bytes 131104 | tf_op jit(solution)/shard_map/ppermute | solution.py:248
  9.2 1.8 %collective-permute-done.2 = bf16[2,128,256]{2,1,0:T(8,128)(2,1)S(1)} collective-permute-done((bf16[2,128,256]{2,1,0:T(8,128)(2,1)}, bf16[2,128,256]{2,1,0:T(8,128)(2,1)S(1)}, u32[]{:S(2)}, u32[]{:S(2)}) %collective-permute-start.2) | collective-permute-done | bytes 131104 | tf_op jit(solution)/shard_map/ppermute | solution.py:248
  11.0 0.1 pad_maximum_fusion.1.rest_0_
  11.1 1.5 %collective-permute-start.8 = (bf16[4,2,128,256]{3,2,1,0:T(8,128)(2,1)S(1)}, bf16[4,2,128,256]{3,2,1,0:T(8,128)(2,1)S(1)}, u32[]{:S(2)}, u32[]{:S(2)}) collective-permute-start(bf16[4,2,128,256]{3,2,1,0:T(8,128)(2,1)S(1)} %pad_maximum_fusion.1.rest_0_), channel_id=1, source_target_pairs={{0,4},{4,0},{8,12},{12,8},{16,20},{20,16},{24,28},{28,24},{1,5},{5... | collective-permute-start | bytes 1572872 | tf_op jit(solution)/shard_map/ppermute | solution.py:344
  12.6 3.5 %collective-permute-start.3 = (bf16[4,2,128,256]{3,2,1,0:T(8,128)(2,1)S(1)}, bf16[4,2,128,256]{3,2,1,0:T(8,128)(2,1)S(1)}, u32[]{:S(2)}, u32[]{:S(2)}) collective-permute-start(bf16[4,2,128,256]{3,2,1,0:T(8,128)(2,1)S(1)} %pad_maximum_fusion.1.rest_0_), channel_id=1, source_target_pairs={{0,8},{4,12},{8,16},{12,20},{16,24},{20,28},{1,9},{5,13},{9,17},{1... | collective-permute-start | bytes 1572872 | tf_op jit(solution)/shard_map/ppermute | solution.py:352
  16.1 0.1 copy.7
  16.3 1.2 %compare_reduce_fusion.4 = (pred[2,8,16]{2,1,0:T(8,128)(4,1)S(1)}, pred[2,8,16]{2,1,0:T(8,128)(4,1)S(1)}, pred[2,8,16]{2,1,0:T(8,128)(4,1)S(1)}, pred[2,8,16]{2,1,0:T(8,128)(4,1)S(1)}) fusion(s32[2,8,40]{2,1,0:T(8,128)S(1)} %bitcast.30, s32[16]{0:T(128)S(1)} %add.343, s32[16]{0:T(128)S(1)} %add.327, s32[16]{0:T(128)S(1)} %add.335, s32[16]{0:T(128)S(1)} %add.312), kind=kLoop, calls=%fused_computation.13 | loop fusion | flops 80896 | bytes 3840 | tf_op jit(solution)/shard_map/reduce_or | solution.py:298
  17.6 1.2 %collective-permute-start.4 = (bf16[128,1024]{1,0:T(8,128)(2,1)S(1)}, bf16[128,1024]{1,0:T(8,128)(2,1)S(1)}, u32[]{:S(2)}, u32[]{:S(2)}) collective-permute-start(bf16[128,1024]{1,0:T(8,128)(2,1)S(1)} %get-tuple-element.49), channel_id=1, source_target_pairs={{0,1},{1,0},{2,3},{3,2},{4,5},{5,4},{6,7},{7,6},{8,9},{9,8},{10,11... | collective-permute-start | bytes 786440 | tf_op jit(solution)/shard_map/ppermute | solution.py:330
  18.7 0.1 collective-permute-start.5
  18.9 0.9 collective-permute-start.6
  19.8 2.9 %compare_reduce_fusion = (pred[2,16,64]{2,1,0:T(8,128)(4,1)S(1)}, pred[2,16,64]{2,1,0:T(8,128)(4,1)S(1)}, pred[2,16,64]{2,1,0:T(8,128)(4,1)S(1)}, pred[2,16,64]{2,1,0:T(8,128)(4,1)S(1)}) fusion(s32[16,64]{1,0:T(8,128)S(1)} %get-tuple-element.107, s32[2,128]{1,0:T(2,128)S(1)} %constant_dynamic-slice_fusion, s32[16,64]{1,0:T(8,128)S(1)} %get-tuple-element.109, ...), kind=kLoop, calls=%fused_computation.2 | loop fusion | flops 2088960 | bytes 25600 | tf_op jit(solution)/shard_map/reduce_and | solution.py:306
  22.7 1.4 %and_convert_fusion = (bf16[2,16,64,128]{3,2,1,0:T(8,128)(2,1)S(1)}, bf16[2,16,64,128]{3,2,1,0:T(8,128)(2,1)S(1)}, bf16[2,16,64,128]{3,2,1,0:T(8,128)(2,1)S(1)}, bf16[2,16,64,128]{3,2,1,0:T(8,128)(2,1)S(1)}) fusion(pred[2,16,64]{2,1,0:T(8,128)(4,1)S(1)} %get-tuple-element.77, pred[128]{0:T(512)(128)(4,1)S(1)} %iota_compare_fusion, ...), kind=kLoop, calls=%fused_computation.1 | loop fusion | flops 2097152 | bytes 2105472 | tf_op jit(solution)/shard_map/convert_element_type | solution.py:308
  24.1 3.6 %collective-permute-done.3.rest_0_ = bf16[4,2,128,256]{3,2,1,0:T(8,128)(2,1)S(1)} collective-permute-done((bf16[4,2,128,256]{3,2,1,0:T(8,128)(2,1)S(1)}, bf16[4,2,128,256]{3,2,1,0:T(8,128)(2,1)S(1)}, u32[]{:S(2)}, u32[]{:S(2)}) %collective-permute-start.3) | collective-permute-done | bytes 524320 | tf_op jit(solution)/shard_map/ppermute | solution.py:352
  27.7 4.4 %collective-permute-start.7 = (bf16[4,2,128,256]{3,2,1,0:T(8,128)(2,1)S(1)}, bf16[4,2,128,256]{3,2,1,0:T(8,128)(2,1)S(1)}, u32[]{:S(2)}, u32[]{:S(2)}) collective-permute-start(bf16[4,2,128,256]{3,2,1,0:T(8,128)(2,1)S(1)} %collective-permute-done.3.rest_0_), channel_id=1, source_target_pairs={{0,8},{4,12},{8,16},{12,20},{16,24},{20,28},{1,9},{5,13},{9,17},{1... | collective-permute-start | bytes 1572872 | tf_op jit(solution)/shard_map/ppermute | solution.py:352
  32.1 0.1 pad_maximum_fusion.q_ref
  32.3 0.6 collective-permute-start.10
  32.9 6.6 %shard_map.56 = (f32[16,128,256]{2,1,0:T(8,128)S(1)}, f32[16,16,256]{2,1,0:T(8,128)S(1)}, bf16[16,128]{1,0:T(8,128)(2,1)S(1)}) custom-call(s32[2,8,16]{2,1,0:T(8,128)S(1)} %broadcast_select_fusion.3.code_ref, bf16[4,128,1024]{2,1,0:T(8,128)(2,1)S(1)} %pad_maximum_fusion.q_ref, bf16[2,16,64,128]{3,2,1,0:T(8,128)(2,1)S(1)} %get-tuple-element.55.pick_ref, ...), custom_call_target="tpu_custom_call" | custom-call | flops 2147483648 | bytes 8388608 | tf_op jit(solution)/shard_map/pallas_call | solution.py:199
  39.5 3.4 %collective-permute-done.7.rest_0_ = bf16[4,2,128,256]{3,2,1,0:T(8,128)(2,1)S(1)} collective-permute-done((bf16[4,2,128,256]{3,2,1,0:T(8,128)(2,1)S(1)}, bf16[4,2,128,256]{3,2,1,0:T(8,128)(2,1)S(1)}, u32[]{:S(2)}, u32[]{:S(2)}) %collective-permute-start.7) | collective-permute-done | bytes 524320 | tf_op jit(solution)/shard_map/ppermute | solution.py:352
  42.9 0.5 collective-permute-start.12
  43.4 4.4 %collective-permute-start.9 = (bf16[4,2,128,256]{3,2,1,0:T(8,128)(2,1)S(1)}, bf16[4,2,128,256]{3,2,1,0:T(8,128)(2,1)S(1)}, u32[]{:S(2)}, u32[]{:S(2)}) collective-permute-start(bf16[4,2,128,256]{3,2,1,0:T(8,128)(2,1)S(1)} %collective-permute-done.7.rest_0_), channel_id=1, source_target_pairs={{0,8},{4,12},{8,16},{12,20},{16,24},{20,28},{1,9},{5,13},{9,17},{1... | collective-permute-start | bytes 1572872 | tf_op jit(solution)/shard_map/ppermute | solution.py:352
  47.8 6.9 %shard_map.57 = (f32[16,128,256]{2,1,0:T(8,128)S(1)}, f32[16,16,256]{2,1,0:T(8,128)S(1)}, bf16[16,128]{1,0:T(8,128)(2,1)S(1)}) custom-call(s32[2,8,16]{2,1,0:T(8,128)S(1)} %broadcast_select_fusion.2.code_ref, bf16[4,128,1024]{2,1,0:T(8,128)(2,1)S(1)} %pad_maximum_fusion.q_ref, bf16[2,16,64,128]{3,2,1,0:T(8,128)(2,1)S(1)} %get-tuple-element.59.pick_ref, ...), custom_call_target="tpu_custom_call" | custom-call | flops 2147483648 | bytes 8388608 | tf_op jit(solution)/shard_map/pallas_call | solution.py:199
  54.7 1.9 %collective-permute-done.12.rest_1_ = bf16[4,2,128,256]{3,2,1,0:T(8,128)(2,1)S(1)} collective-permute-done((bf16[4,2,128,256]{3,2,1,0:T(8,128)(2,1)S(1)}, bf16[4,2,128,256]{3,2,1,0:T(8,128)(2,1)S(1)}, u32[]{:S(2)}, u32[]{:S(2)}) %collective-permute-start.12) | collective-permute-done | bytes 524320 | tf_op jit(solution)/shard_map/ppermute | solution.py:344
  56.6 3.6 %collective-permute-start.13 = (bf16[4,1,128,256]{3,2,1,0:T(8,128)(2,1)S(1)}, bf16[4,1,128,256]{3,2,1,0:T(8,128)(2,1)S(1)}, u32[]{:S(2)}, u32[]{:S(2)}) collective-permute-start(bf16[4,1,128,256]{3,2,1,0:T(8,128)(2,1)S(1)} %slice.20), channel_id=1, source_target_pairs={{0,8},{4,12},{8,16},{12,20},{16,24},{20,28},{1,9},{5,13},{9,17},{1... | collective-permute-start | bytes 786440 | tf_op jit(solution)/shard_map/ppermute | solution.py:349
  60.3 0.6 collective-permute-start.11
  60.9 6.7 %shard_map.58 = (f32[16,128,256]{2,1,0:T(8,128)S(1)}, f32[16,16,256]{2,1,0:T(8,128)S(1)}, bf16[16,128]{1,0:T(8,128)(2,1)S(1)}) custom-call(s32[2,8,16]{2,1,0:T(8,128)S(1)} %get-tuple-element.65.code_ref, bf16[4,128,1024]{2,1,0:T(8,128)(2,1)S(1)} %pad_maximum_fusion.q_ref, bf16[2,16,64,128]{3,2,1,0:T(8,128)(2,1)S(1)} %get-tuple-element.66.pick_ref, ...), custom_call_target="tpu_custom_call" | custom-call | flops 2147483648 | bytes 8388608 | tf_op jit(solution)/shard_map/pallas_call | solution.py:199
  67.7 7.5 %shard_map.59.own_ref = bf16[4,128,1024]{2,1,0:T(8,128)(2,1)S(1)} custom-call(s32[2,8,16]{2,1,0:T(8,128)S(1)} %get-tuple-element.47.code_ref, bf16[4,128,1024]{2,1,0:T(8,128)(2,1)S(1)} %pad_maximum_fusion.q_ref, bf16[2,16,64,128]{3,2,1,0:T(8,128)(2,1)S(1)} %get-tuple-element.52.pick_ref, bf16[4,2,128,256]{3,2,1,0:T(8,128)(2,1)S(1)} %collective-permute-done.9.rest_0_, ...), custom_call_target="tpu_custom_call" | custom-call | flops 2147483648 | bytes 8388608 | tf_op jit(solution)/shard_map/pallas_call | solution.py:199
  75.2 0.1 collective-permute-start.16
  75.3 2.0 %collective-permute-start.15 = (bf16[128,1024]{1,0:T(8,128)(2,1)S(1)}, bf16[128,1024]{1,0:T(8,128)(2,1)S(1)}, u32[]{:S(2)}, u32[]{:S(2)}) collective-permute-start(bf16[128,1024]{1,0:T(8,128)(2,1)S(1)} %get-tuple-element.84), channel_id=1, source_target_pairs={{0,2},{1,3},{2,0},{3,1},{4,6},{5,7},{6,4},{7,5},{8,10},{9,11},{10,... | collective-permute-start | bytes 786440 | tf_op jit(solution)/shard_map/ppermute | solution.py:375
  77.3 0.1 collective-permute-start.14
  77.4 6.1 %collective-permute-done.16.rest_2_ = bf16[128,1024]{1,0:T(8,128)(2,1)S(1)} collective-permute-done((bf16[128,1024]{1,0:T(8,128)(2,1)S(1)}, bf16[128,1024]{1,0:T(8,128)(2,1)S(1)}, u32[]{:S(2)}, u32[]{:S(2)}) %collective-permute-start.16) | collective-permute-done | bytes 262176 | tf_op jit(solution)/shard_map/ppermute | solution.py:375
  83.5 6.0 %collective-permute-done.14.rest_0_ = bf16[128,1024]{1,0:T(8,128)(2,1)S(1)} collective-permute-done((bf16[128,1024]{1,0:T(8,128)(2,1)S(1)}, bf16[128,1024]{1,0:T(8,128)(2,1)S(1)}, u32[]{:S(2)}, u32[]{:S(2)}) %collective-permute-start.14) | collective-permute-done | bytes 262176 | tf_op jit(solution)/shard_map/ppermute | solution.py:375
  89.5 1.0 %shard_map.60 = bf16[128,4096]{1,0:T(8,128)(2,1)} custom-call(s32[1]{0:T(128)} %bitcast.me_ref, bf16[4,128,1024]{2,1,0:T(8,128)(2,1)S(1)} %shard_map.59.own_ref, bf16[128,1024]{1,0:T(8,128)(2,1)S(1)} %collective-permute-done.14.rest_0_, bf16[128,1024]{1,0:T(8,128)(2,1)S(1)} %collective-permute-done.15.rest_1_, ...), custom_call_target="tpu_custom_call" | custom-call | tf_op jit(solution)/shard_map/pallas_call | solution.py:57
  (35 shorter events, 0.2 us)
Async XLA Ops:
  0.0 16.1 %copy-start = (s32[4,128]{1,0:T(4,128)S(1)}, s32[4,128]{1,0:T(4,128)}, u32[]{:S(2)}) copy-start(s32[4,128]{1,0:T(4,128)} %param.8) | copy-start | bytes 6148
  0.0 16.1 %copy-start.2 = (s32[4,64,40]{1,2,0:T(8,128)S(1)}, s32[4,64,40]{1,2,0:T(8,128)}, u32[]{:S(2)}) copy-start(s32[4,64,40]{1,2,0:T(8,128)} %param.9) | copy-start | bytes 122884
  2.0 9.0 %copy-start.1 = (bf16[2,128,256]{2,1,0:T(8,128)(2,1)S(1)}, bf16[2,128,256]{2,1,0:T(8,128)(2,1)}, u32[]{:S(2)}) copy-start(bf16[2,128,256]{2,1,0:T(8,128)(2,1)} %get-tuple-element.39) | copy-start | bytes 393220
  2.0 7.2 %collective-permute-start = (bf16[2,128,256]{2,1,0:T(8,128)(2,1)}, bf16[2,128,256]{2,1,0:T(8,128)(2,1)S(1)}, u32[]{:S(2)}, u32[]{:S(2)}) collective-permute-start(bf16[2,128,256]{2,1,0:T(8,128)(2,1)} %get-tuple-element.40), channel_id=1, source_target_pairs={{0,1},{1,0},{2,3},{3,2},{4,5},{5,4},{6,7},{7,6},{8,9},{9,8},{10,11... | collective-permute-start | bytes 393224 | tf_op jit(solution)/shard_map/ppermute | solution.py:248
  5.0 4.2 %collective-permute-start.1 = (bf16[2,128,256]{2,1,0:T(8,128)(2,1)}, bf16[2,128,256]{2,1,0:T(8,128)(2,1)S(1)}, u32[]{:S(2)}, u32[]{:S(2)}) collective-permute-start(bf16[2,128,256]{2,1,0:T(8,128)(2,1)} %get-tuple-element.41), channel_id=1, source_target_pairs={{0,2},{1,3},{2,0},{3,1},{4,6},{5,7},{6,4},{7,5},{8,10},{9,11},{10,... | collective-permute-start | bytes 393224 | tf_op jit(solution)/shard_map/ppermute | solution.py:248
  5.0 6.1 %collective-permute-start.2 = (bf16[2,128,256]{2,1,0:T(8,128)(2,1)}, bf16[2,128,256]{2,1,0:T(8,128)(2,1)S(1)}, u32[]{:S(2)}, u32[]{:S(2)}) collective-permute-start(bf16[2,128,256]{2,1,0:T(8,128)(2,1)} %get-tuple-element.42), channel_id=1, source_target_pairs={{0,3},{1,2},{2,1},{3,0},{4,7},{5,6},{6,5},{7,4},{8,11},{9,10},{10,... | collective-permute-start | bytes 393224 | tf_op jit(solution)/shard_map/ppermute | solution.py:248
  11.1 21.8 %collective-permute-start.8 = (bf16[4,2,128,256]{3,2,1,0:T(8,128)(2,1)S(1)}, bf16[4,2,128,256]{3,2,1,0:T(8,128)(2,1)S(1)}, u32[]{:S(2)}, u32[]{:S(2)}) collective-permute-start(bf16[4,2,128,256]{3,2,1,0:T(8,128)(2,1)S(1)} %pad_maximum_fusion.1.rest_0_), channel_id=1, source_target_pairs={{0,4},{4,0},{8,12},{12,8},{16,20},{20,16},{24,28},{28,24},{1,5},{5... | collective-permute-start | bytes 1572872 | tf_op jit(solution)/shard_map/ppermute | solution.py:344
  12.6 15.1 %collective-permute-start.3 = (bf16[4,2,128,256]{3,2,1,0:T(8,128)(2,1)S(1)}, bf16[4,2,128,256]{3,2,1,0:T(8,128)(2,1)S(1)}, u32[]{:S(2)}, u32[]{:S(2)}) collective-permute-start(bf16[4,2,128,256]{3,2,1,0:T(8,128)(2,1)S(1)} %pad_maximum_fusion.1.rest_0_), channel_id=1, source_target_pairs={{0,8},{4,12},{8,16},{12,20},{16,24},{20,28},{1,9},{5,13},{9,17},{1... | collective-permute-start | bytes 1572872 | tf_op jit(solution)/shard_map/ppermute | solution.py:352
  17.6 14.5 %collective-permute-start.4 = (bf16[128,1024]{1,0:T(8,128)(2,1)S(1)}, bf16[128,1024]{1,0:T(8,128)(2,1)S(1)}, u32[]{:S(2)}, u32[]{:S(2)}) collective-permute-start(bf16[128,1024]{1,0:T(8,128)(2,1)S(1)} %get-tuple-element.49), channel_id=1, source_target_pairs={{0,1},{1,0},{2,3},{3,2},{4,5},{5,4},{6,7},{7,6},{8,9},{9,8},{10,11... | collective-permute-start | bytes 786440 | tf_op jit(solution)/shard_map/ppermute | solution.py:330
  18.7 13.4 %collective-permute-start.5 = (bf16[128,1024]{1,0:T(8,128)(2,1)S(1)}, bf16[128,1024]{1,0:T(8,128)(2,1)S(1)}, u32[]{:S(2)}, u32[]{:S(2)}) collective-permute-start(bf16[128,1024]{1,0:T(8,128)(2,1)S(1)} %get-tuple-element.50), channel_id=1, source_target_pairs={{0,2},{1,3},{2,0},{3,1},{4,6},{5,7},{6,4},{7,5},{8,10},{9,11},{10,... | collective-permute-start | bytes 786440 | tf_op jit(solution)/shard_map/ppermute | solution.py:330
  18.9 13.2 %collective-permute-start.6 = (bf16[128,1024]{1,0:T(8,128)(2,1)S(1)}, bf16[128,1024]{1,0:T(8,128)(2,1)S(1)}, u32[]{:S(2)}, u32[]{:S(2)}) collective-permute-start(bf16[128,1024]{1,0:T(8,128)(2,1)S(1)} %get-tuple-element.51), channel_id=1, source_target_pairs={{0,3},{1,2},{2,1},{3,0},{4,7},{5,6},{6,5},{7,4},{8,11},{9,10},{10,... | collective-permute-start | bytes 786440 | tf_op jit(solution)/shard_map/ppermute | solution.py:330
  27.7 15.2 %collective-permute-start.7 = (bf16[4,2,128,256]{3,2,1,0:T(8,128)(2,1)S(1)}, bf16[4,2,128,256]{3,2,1,0:T(8,128)(2,1)S(1)}, u32[]{:S(2)}, u32[]{:S(2)}) collective-permute-start(bf16[4,2,128,256]{3,2,1,0:T(8,128)(2,1)S(1)} %collective-permute-done.3.rest_0_), channel_id=1, source_target_pairs={{0,8},{4,12},{8,16},{12,20},{16,24},{20,28},{1,9},{5,13},{9,17},{1... | collective-permute-start | bytes 1572872 | tf_op jit(solution)/shard_map/ppermute | solution.py:352
  32.3 15.5 %collective-permute-start.10 = (bf16[4,2,128,256]{3,2,1,0:T(8,128)(2,1)S(1)}, bf16[4,2,128,256]{3,2,1,0:T(8,128)(2,1)S(1)}, u32[]{:S(2)}, u32[]{:S(2)}) collective-permute-start(bf16[4,2,128,256]{3,2,1,0:T(8,128)(2,1)S(1)} %collective-permute-done.3.rest_0_), channel_id=1, source_target_pairs={{0,4},{4,0},{8,12},{12,8},{16,20},{20,16},{24,28},{28,24},{1,5},{5... | collective-permute-start | bytes 1572872 | tf_op jit(solution)/shard_map/ppermute | solution.py:344
  42.9 13.7 %collective-permute-start.12 = (bf16[4,2,128,256]{3,2,1,0:T(8,128)(2,1)S(1)}, bf16[4,2,128,256]{3,2,1,0:T(8,128)(2,1)S(1)}, u32[]{:S(2)}, u32[]{:S(2)}) collective-permute-start(bf16[4,2,128,256]{3,2,1,0:T(8,128)(2,1)S(1)} %collective-permute-done.7.rest_0_), channel_id=1, source_target_pairs={{0,4},{4,0},{8,12},{12,8},{16,20},{20,16},{24,28},{28,24},{1,5},{5... | collective-permute-start | bytes 1572872 | tf_op jit(solution)/shard_map/ppermute | solution.py:344
  43.4 16.9 %collective-permute-start.9 = (bf16[4,2,128,256]{3,2,1,0:T(8,128)(2,1)S(1)}, bf16[4,2,128,256]{3,2,1,0:T(8,128)(2,1)S(1)}, u32[]{:S(2)}, u32[]{:S(2)}) collective-permute-start(bf16[4,2,128,256]{3,2,1,0:T(8,128)(2,1)S(1)} %collective-permute-done.7.rest_0_), channel_id=1, source_target_pairs={{0,8},{4,12},{8,16},{12,20},{16,24},{20,28},{1,9},{5,13},{9,17},{1... | collective-permute-start | bytes 1572872 | tf_op jit(solution)/shard_map/ppermute | solution.py:352
  56.6 11.0 %collective-permute-start.13 = (bf16[4,1,128,256]{3,2,1,0:T(8,128)(2,1)S(1)}, bf16[4,1,128,256]{3,2,1,0:T(8,128)(2,1)S(1)}, u32[]{:S(2)}, u32[]{:S(2)}) collective-permute-start(bf16[4,1,128,256]{3,2,1,0:T(8,128)(2,1)S(1)} %slice.20), channel_id=1, source_target_pairs={{0,8},{4,12},{8,16},{12,20},{16,24},{20,28},{1,9},{5,13},{9,17},{1... | collective-permute-start | bytes 786440 | tf_op jit(solution)/shard_map/ppermute | solution.py:349
  60.3 7.4 %collective-permute-start.11 = (bf16[4,1,128,256]{3,2,1,0:T(8,128)(2,1)S(1)}, bf16[4,1,128,256]{3,2,1,0:T(8,128)(2,1)S(1)}, u32[]{:S(2)}, u32[]{:S(2)}) collective-permute-start(bf16[4,1,128,256]{3,2,1,0:T(8,128)(2,1)S(1)} %slice.15), channel_id=1, source_target_pairs={{0,4},{4,0},{8,12},{12,8},{16,20},{20,16},{24,28},{28,24},{1,5},{5... | collective-permute-start | bytes 786440 | tf_op jit(solution)/shard_map/ppermute | solution.py:348
  75.2 8.3 %collective-permute-start.16 = (bf16[128,1024]{1,0:T(8,128)(2,1)S(1)}, bf16[128,1024]{1,0:T(8,128)(2,1)S(1)}, u32[]{:S(2)}, u32[]{:S(2)}) collective-permute-start(bf16[128,1024]{1,0:T(8,128)(2,1)S(1)} %get-tuple-element.83), channel_id=1, source_target_pairs={{0,3},{1,2},{2,1},{3,0},{4,7},{5,6},{6,5},{7,4},{8,11},{9,10},{10,... | collective-permute-start | bytes 786440 | tf_op jit(solution)/shard_map/ppermute | solution.py:375
  75.3 8.2 %collective-permute-start.15 = (bf16[128,1024]{1,0:T(8,128)(2,1)S(1)}, bf16[128,1024]{1,0:T(8,128)(2,1)S(1)}, u32[]{:S(2)}, u32[]{:S(2)}) collective-permute-start(bf16[128,1024]{1,0:T(8,128)(2,1)S(1)} %get-tuple-element.84), channel_id=1, source_target_pairs={{0,2},{1,3},{2,0},{3,1},{4,6},{5,7},{6,4},{7,5},{8,10},{9,11},{10,... | collective-permute-start | bytes 786440 | tf_op jit(solution)/shard_map/ppermute | solution.py:375
  77.3 12.2 %collective-permute-start.14 = (bf16[128,1024]{1,0:T(8,128)(2,1)S(1)}, bf16[128,1024]{1,0:T(8,128)(2,1)S(1)}, u32[]{:S(2)}, u32[]{:S(2)}) collective-permute-start(bf16[128,1024]{1,0:T(8,128)(2,1)S(1)} %get-tuple-element.85), channel_id=1, source_target_pairs={{0,1},{1,0},{2,3},{3,2},{4,5},{5,4},{6,7},{7,6},{8,9},{9,8},{10,11... | collective-permute-start | bytes 786440 | tf_op jit(solution)/shard_map/ppermute | solution.py:375
